TPU v7x, 32 devices: a whole 2x2x4 slice. The times are simulated.
32 devices in a mesh: seq: 4 (over z), dp: 8 (over y, x, core).
Axes of the slice: x: 2, y: 2, z: 4, core: 2. Of those that a mesh axis runs over, the one named last changes fastest.
Arguments:
- layer_input: bfloat16 [8, 2048, 768], P('dp', 'seq'), may hold values from -6 to 6
- triple_weight: bfloat16 [768, 2304], P('dp'), may hold values from -0.21875 to 0.21875
- query_bias: bfloat16 [768], P('dp'), may hold values from -3 to 3
- value_bias: bfloat16 [768], P('dp'), may hold values from -3 to 3
- mixer_weight: bfloat16 [768, 768], P('dp'), may hold values from -4 to 4
- mixer_bias: bfloat16 [768], P('dp'), may hold values from -1.75 to 1.75
- first_gain: bfloat16 [768], P('dp'), may hold values from 0.5 to 1.5
- first_shift: bfloat16 [768], P('dp'), may hold values from -1.75 to 1.75
- expand_weight: bfloat16 [768, 3072], P('dp'), may hold values from -0.21875 to 0.21875
- expand_bias: bfloat16 [3072], P('dp'), may hold values from -1.75 to 1.75
- shrink_weight: bfloat16 [3072, 768], P('dp'), may hold values from -0.109375 to 0.109375
- shrink_bias: bfloat16 [768], P('dp'), may hold values from -1.75 to 1.75
- second_gain: bfloat16 [768], P('dp'), may hold values from 0.5 to 1.5
- second_shift: bfloat16 [768], P('dp'), may hold values from -1.75 to 1.75
- project_weight: bfloat16 [768, 128], P('dp'), may hold values from -0.21875 to 0.21875
- kept_tokens: int32 [8, 2048], P('dp', 'seq'), may hold values 0 or 1
- upstream: float32 [8, 2048, 128], P('dp', 'seq'), may hold values from -96 to 96
Outputs:
- embeddings: float32 [8, 2048, 128], P('dp', 'seq')
- input_grad: float32 [8, 2048, 768], P('dp', 'seq')
- grad_triple: float32 [768, 2304], P('dp')
- grad_queries: float32 [768], P('dp')
- grad_values: float32 [768], P('dp')
- grad_mixer: float32 [768, 768], P('dp')
- grad_offset: float32 [768], P('dp')
- grad_gamma: float32 [768], P('dp')
- grad_beta: float32 [768], P('dp')
- grad_expand: float32 [768, 3072], P('dp')
- grad_lift: float32 [3072], P('dp')
- grad_shrink: float32 [3072, 768], P('dp')
- grad_settle: float32 [768], P('dp')
- grad_gain: float32 [768], P('dp')
- grad_shift: float32 [768], P('dp')
- grad_project: float32 [768, 128], P('dp')
All inputs are finite; a program needn't handle non-finite values. No bound on the sum of `kept_tokens` on one device may be relied on, other than what follows from the above.
Results may differ from a plain program's by a relative error of at most 0.018.
Values may be sent and summed in bfloat16 or wider, within the bound.
No kernel may reach another device: no remote copies, remote signals or barrier semaphores. Data moves between devices by JAX's collectives and lax.ppermute only.
A program may use at most 128 MiB of HBM per device.

v0:
```python
import functools

import jax
import jax.numpy as jnp
from jax import lax
from jax.experimental import pallas as pl
from jax.experimental.pallas import tpu as pltpu
from jax.sharding import PartitionSpec as P

HD = 64
LOG2E = 1.4426950408889634
f32 = jnp.float32
bf16 = jnp.bfloat16
SHORT = pl.CostEstimate(flops=0, transcendentals=0, bytes_accessed=0)
NT = (((1,), (1,)), ((), ()))
NN = (((1,), (0,)), ((), ()))
TN = (((0,), (0,)), ((), ()))


def dot(a, b, dims):
    return lax.dot_general(a, b, dims, preferred_element_type=f32)


def attend_forward_kernel(parts, block, heads, *refs):
    joined = refs[:parts]
    mixed_ref, stats_ref = refs[parts:]
    count = joined[0].shape[0]
    for h in range(heads):
        base = 3 * HD * h
        query = joined[block][:, base : base + HD] * jnp.asarray(HD**-0.5, bf16)
        scores = [
            dot(query, j[:, base + HD : base + 2 * HD], NT) * LOG2E for j in joined
        ]
        top = jnp.max(scores[0], axis=1, keepdims=True)
        for s in scores[1:]:
            top = jnp.maximum(top, jnp.max(s, axis=1, keepdims=True))
        total = None
        for s, j in zip(scores, joined):
            probs = jnp.exp2(s - top).astype(bf16)
            wide = jnp.concatenate(
                [j[:, base + 2 * HD : base + 3 * HD], jnp.ones((count, HD), bf16)], axis=1
            )
            part = dot(probs, wide, NN)
            total = part if total is None else total + part
        mass = total[:, HD : HD + 1]
        mixed_ref[:, HD * h : HD * (h + 1)] = (total[:, :HD] / mass).astype(bf16)
        stats_ref[:, h : h + 1] = top + jnp.log2(mass)


def attend_forward(joined, block, heads):
    parts = len(joined)
    count = joined[0].shape[0]
    return pl.pallas_call(
        functools.partial(attend_forward_kernel, parts, block, heads),
        out_shape=[
            jax.ShapeDtypeStruct((count, heads * HD), bf16),
            jax.ShapeDtypeStruct((count, 8), f32),
        ],
        in_specs=[pl.BlockSpec(memory_space=pltpu.VMEM)] * parts,
        out_specs=[pl.BlockSpec(memory_space=pltpu.VMEM)] * 2,
        compiler_params=pltpu.CompilerParams(vmem_limit_bytes=40 << 20),
        cost_estimate=SHORT,
        name="attend_forward",
    )(*joined)


def attend_backward_kernel(parts, h, *refs):
    joined = refs[:parts]
    grads = refs[parts : 2 * parts]
    mixed = refs[2 * parts : 3 * parts]
    stats = refs[3 * parts : 4 * parts]
    outs = refs[4 * parts : 5 * parts]
    keys_sum, values_sum = refs[5 * parts :]
    base = 3 * HD * h
    count = joined[0].shape[0]
    for b in range(parts):
        query = joined[b][:, base : base + HD] * jnp.asarray(HD**-0.5, bf16)
        grad = grads[b][:, HD * h : HD * (h + 1)]
        inner = jnp.sum(
            grad.astype(f32) * mixed[b][:, HD * h : HD * (h + 1)].astype(f32), axis=1, keepdims=True
        )
        level = stats[b][:, h : h + 1]
        query_t = query.T
        grad_t = grad.T
        total = None
        for c in range(parts):
            keys = joined[c][:, base + HD : base + 2 * HD]
            values = joined[c][:, base + 2 * HD : base + 3 * HD]
            probs = jnp.exp2(dot(query, keys, NT) * LOG2E - level)
            grad_probs = dot(grad, values, NT)
            grad_scores = (probs * (grad_probs - inner)).astype(bf16)
            part = dot(grad_scores, keys, NN)
            total = part if total is None else total + part
            span = slice(c * count, (c + 1) * count)
            grad_values = dot(grad_t, probs.astype(bf16), NN)
            grad_keys = dot(query_t, grad_scores, NN)
            if b == 0:
                values_sum[:, span] = grad_values
                keys_sum[:, span] = grad_keys
            else:
                values_sum[:, span] += grad_values
                keys_sum[:, span] += grad_keys
        outs[b][:, :HD] = (total * HD**-0.5).astype(bf16)
    for c in range(parts):
        span = slice(c * count, (c + 1) * count)
        outs[c][:, HD : 2 * HD] = keys_sum[:, span].T.astype(bf16)
        outs[c][:, 2 * HD :] = values_sum[:, span].T.astype(bf16)


def attend_backward(joined, grads, mixed, stats, h):
    parts = len(joined)
    count = joined[0].shape[0]
    return pl.pallas_call(
        functools.partial(attend_backward_kernel, parts, h),
        out_shape=[jax.ShapeDtypeStruct((count, 3 * HD), bf16)] * parts,
        grid=(1,),
        scratch_shapes=[pltpu.VMEM((HD, parts * count), f32)] * 2,
        compiler_params=pltpu.CompilerParams(vmem_limit_bytes=60 << 20),
        cost_estimate=SHORT,
        name="attend_backward",
    )(*joined, *grads, *mixed, *stats)


def normal_cdf_and_density(x):
    a = jnp.abs(x) * (0.5**0.5)
    t = 1.0 / (1.0 + 0.5 * a)
    series = -0.82215223 + t * 0.17087277
    for c in (1.48851587, -1.13520398, 0.27886807, -0.18628806, 0.09678418, 0.37409196, 1.00002368):
        series = c + t * series
    tail = 0.5 * t * jnp.exp(-a * a - 1.26551223 + t * series)
    cdf = jnp.where(x >= 0, 1.0 - tail, tail)
    return cdf, jnp.exp(-0.5 * x * x) * 0.3989422804014327


def standardize(rows):
    mean = jnp.mean(rows, axis=-1, keepdims=True)
    centred = rows - mean
    spread = jnp.mean(centred * centred, axis=-1, keepdims=True)
    scale = lax.rsqrt(spread + 1e-12)
    return centred * scale, scale


def norm_back(grad, gain, normed, scale):
    g = grad * gain
    return (
        g
        - jnp.mean(g, axis=-1, keepdims=True)
        - normed * jnp.mean(g * normed, axis=-1, keepdims=True)
    ) * scale


def ffn_kernel(parts, step, wide_from, shrink_from, place_ref, turn_ref, *refs):
    rows_ref, arrived, refs = refs[0], refs[1 : 1 + parts], refs[1 + parts :]
    vec_ref, lift_bias_ref, keep_ref, ct_ref = refs[:4]
    groups = len(wide_from)
    wide_hbm, shrink_hbm = refs[4 : 4 + groups], refs[4 + groups : 4 + 2 * groups]
    outs = refs[4 + 2 * groups :]
    (embedded_ref, resid_ref, first_ref, active_ref, second_ref, plow_ref, two_ref, lifted_ref, one_ref, sums_ref) = outs[:10]
    mixed_grads = outs[10 : 10 + parts]
    mixer_ref, expand_ref, shrink_ref, slope_ref, total_ref, sems = outs[10 + parts :]
    width = rows_ref.shape[1]
    hidden = lift_bias_ref.shape[1]
    local = width // parts
    chunks = hidden // step
    place = place_ref[0]

    pieces = sum(len(f) for f in wide_from)

    def load(sources, origin, columns, target, first):
        count = target.shape[0] // pieces
        copies = []
        for source, ks in zip(sources, origin):
            for i, k in enumerate(ks):
                at = pl.multiple_of(lax.bitwise_xor(turn_ref[0], k) * count, count) if pieces > 1 else 0
                copies.append(
                    pltpu.make_async_copy(
                        source.at[i, :, columns],
                        target.at[pl.ds(at, count), :],
                        sems.at[first + len(copies)],
                    )
                )
                copies[-1].start()
        return copies

    side = width + ct_ref.shape[1]
    load_mixer = load(wide_hbm, wide_from, slice(hidden, hidden + side), mixer_ref, 0)
    load_expand = load(wide_hbm, wide_from, slice(0, hidden), expand_ref, pieces)
    load_shrink = load(shrink_hbm, shrink_from, slice(0, width), shrink_ref, 2 * pieces)

    def vec(i):
        return vec_ref[i : i + 1, :]

    def mixer_rows(r):
        at = lax.rem(place + r, parts) * local
        return mixer_ref[pl.ds(pl.multiple_of(at, local), local), :width]

    for copy in load_mixer:
        copy.wait()
    branch = vec(2)
    for r in range(parts):
        branch = branch + dot(arrived[r][...], mixer_rows(r), NN)
    normed_one, scale_one = standardize(rows_ref[...].astype(f32) + branch)
    first = normed_one * vec(3) + vec(4)
    first_low = first.astype(bf16)
    first_ref[...] = first_low
    total_ref[...] = first + vec(5)

    for copy in load_expand + load_shrink:
        copy.wait()

    def forward(c, carry):
        at = pl.multiple_of(c * step, step)
        lifted = dot(first_ref[...], expand_ref[:, pl.ds(at, step)], NN) + lift_bias_ref[:, pl.ds(at, step)]
        cdf, density = normal_cdf_and_density(lifted)
        active = (lifted * cdf).astype(bf16)
        active_ref[:, pl.ds(at, step)] = active
        slope_ref[:, pl.ds(at, step)] = cdf + lifted * density
        total_ref[...] += dot(active, shrink_ref[pl.ds(at, step), :], NN)
        return carry

    lax.fori_loop(0, chunks, forward, 0)

    normed_two, scale_two = standardize(total_ref[...])
    second_low = (normed_two * vec(6) + vec(7)).astype(bf16)
    second_ref[...] = second_low
    w_project = mixer_ref[:, width:]
    projected = dot(second_low, w_project, NN)
    keep = keep_ref[...]
    inverse = lax.rsqrt(jnp.sum(projected * projected, axis=-1, keepdims=True) + 1e-06)
    unit = projected * inverse
    embedded_ref[...] = unit * keep
    ct = ct_ref[...]
    plow = (keep * (ct - unit * jnp.sum(unit * ct, axis=-1, keepdims=True)) * inverse).astype(bf16)
    plow_ref[...] = plow
    grad_second = dot(plow, w_project, NT)
    sums_ref[4:5, :] = jnp.sum(grad_second * normed_two, axis=0, keepdims=True)
    sums_ref[5:6, :] = jnp.sum(grad_second, axis=0, keepdims=True)
    grad_two = norm_back(grad_second, vec(6), normed_two, scale_two)
    two_low = grad_two.astype(bf16)
    two_ref[...] = two_low
    sums_ref[3:4, :] = jnp.sum(two_low.astype(f32), axis=0, keepdims=True)
    total_ref[...] = grad_two

    def backward(c, carry):
        at = pl.multiple_of(c * step, step)
        grad_active = dot(two_ref[...], shrink_ref[pl.ds(at, step), :], NT)
        low = (grad_active * slope_ref[:, pl.ds(at, step)]).astype(bf16)
        lifted_ref[:, pl.ds(at, step)] = low
        total_ref[...] += dot(low, expand_ref[:, pl.ds(at, step)], NT)
        return carry

    lax.fori_loop(0, chunks, backward, 0)
    for c in range(hidden // width):
        sums_ref[6 + c : 7 + c, :] = jnp.sum(
            lifted_ref[:, c * width : (c + 1) * width].astype(f32), axis=0, keepdims=True
        )

    grad_first = total_ref[...]
    sums_ref[1:2, :] = jnp.sum(grad_first * normed_one, axis=0, keepdims=True)
    sums_ref[2:3, :] = jnp.sum(grad_first, axis=0, keepdims=True)
    grad_one = norm_back(grad_first, vec(3), normed_one, scale_one)
    resid_ref[...] = grad_one
    one_low = grad_one.astype(bf16)
    one_ref[...] = one_low
    sums_ref[0:1, :] = jnp.sum(one_low.astype(f32), axis=0, keepdims=True)
    for r in range(parts):
        mixed_grads[r][...] = dot(one_low, mixer_rows(r), NT).astype(bf16)
    used = 6 + hidden // width
    sums_ref[used:, :] = jnp.zeros((sums_ref.shape[0] - used, width), f32)


def feed_forward(place, turn, rows, arrived, vec, lift_bias, keep, ct, wide, wide_from, shrink, shrink_from):
    parts = len(arrived)
    groups = len(wide)
    pieces = sum(len(f) for f in wide_from)
    tokens, width = rows.shape
    hidden = lift_bias.shape[1]
    emb = ct.shape[1]
    local = width // parts
    V = pl.BlockSpec(memory_space=pltpu.VMEM)
    A = pl.BlockSpec(memory_space=pl.ANY)
    M = pl.BlockSpec(memory_space=pltpu.SMEM)
    S = jax.ShapeDtypeStruct
    return pl.pallas_call(
        functools.partial(ffn_kernel, parts, hidden // 2, wide_from, shrink_from),
        out_shape=[
            S((tokens, emb), f32),
            S((tokens, width), f32),
            S((tokens, width), bf16),
            S((tokens, hidden), bf16),
            S((tokens, width), bf16),
            S((tokens, emb), bf16),
            S((tokens, width), bf16),
            S((tokens, hidden), bf16),
            S((tokens, width), bf16),
            S((16, width), f32),
        ]
        + [S((tokens, local), bf16)] * parts,
        in_specs=[M, M, V] + [V] * parts + [V] * 4 + [A] * (2 * groups),
        out_specs=[V] * (10 + parts),
        scratch_shapes=[
            pltpu.VMEM((width, width + emb), bf16),
            pltpu.VMEM((width, hidden), bf16),
            pltpu.VMEM((hidden, width), bf16),
            pltpu.VMEM((tokens, hidden), f32),
            pltpu.VMEM((tokens, width), f32),
            pltpu.SemaphoreType.DMA((3 * pieces,)),
        ],
        compiler_params=pltpu.CompilerParams(vmem_limit_bytes=56 << 20),
        cost_estimate=SHORT,
        name="feed_forward",
    )(place, turn, rows, *arrived, vec, lift_bias, keep, ct, *wide, *shrink)


def prepare_kernel(parts, heads, place_ref, triple_ref, *refs):
    vectors, (own_ref, rest_ref) = refs[:-2], refs[-2:]
    lines = triple_ref.shape[0]
    local = heads * HD
    width = parts * local
    shift = lax.rem(parts - place_ref[0], parts) * local
    kinds = [
        pltpu.roll(triple_ref[:, i * width : (i + 1) * width].astype(f32), shift, 1).astype(bf16)
        for i in range(3)
    ]
    for h in range(heads):
        for r in range(parts):
            piece = jnp.concatenate(
                [k[:, r * local + h * HD : r * local + (h + 1) * HD] for k in kinds], axis=1
            )
            if r == 0:
                own_ref[:lines, h * 3 * HD : (h + 1) * 3 * HD] = piece
            else:
                at = (h * (parts - 1) + r - 1) * 3 * HD
                rest_ref[:, at : at + 3 * HD] = piece
    lane = own_ref.shape[1]
    lined = [jnp.zeros((16 - len(vectors), lane), f32)]
    for v in vectors[::-1]:
        line = v[...].astype(f32).reshape(1, -1)
        lined.insert(0, jnp.pad(line, ((0, 0), (0, lane - line.shape[1]))))
    own_ref[lines:, :] = jnp.concatenate(lined).astype(bf16)


def prepare(place, triple, vectors, parts):
    lines, columns = triple.shape
    own = columns // parts
    V = pl.BlockSpec(memory_space=pltpu.VMEM)
    return pl.pallas_call(
        functools.partial(prepare_kernel, parts, own // (3 * HD)),
        out_shape=[
            jax.ShapeDtypeStruct((lines + 16, own), bf16),
            jax.ShapeDtypeStruct((lines, columns - own), bf16),
        ],
        in_specs=[pl.BlockSpec(memory_space=pltpu.SMEM), V] + [V] * len(vectors),
        out_specs=[V] * 2,
        cost_estimate=SHORT,
        name="prepare",
    )(place, triple, *vectors)


def assemble_kernel(parts, origin, place_ref, turn_ref, *refs):
    stacks, (w_ref, bias_ref, vec_ref, lift_ref, all_ref) = refs[:-5], refs[-5:]
    dp = all_ref.shape[0]
    lines = w_ref.shape[0] // dp
    hlines = lift_ref.shape[1] // dp
    width = vec_ref.shape[1]
    local = width // parts
    for stack, ks in zip(stacks, origin):
        for i, k in enumerate(ks):
            s = lax.bitwise_xor(turn_ref[0], k)
            w_ref[pl.ds(pl.multiple_of(s * lines, lines), lines), :] = stack[i, :lines, :]
            all_ref[s] = stack[i, lines:, :].astype(f32)
    vec_ref[...] = jnp.concatenate([all_ref[s][:8, :lines] for s in range(dp)], axis=1)
    lift_ref[...] = jnp.concatenate([all_ref[s][8:9, :hlines] for s in range(dp)], axis=1)
    shift = lax.rem(parts - place_ref[0], parts) * local
    turned = pltpu.roll(vec_ref[...], shift, 1)
    pieces = []
    for at in range(0, local, HD):
        pieces += [turned[0:1, at : at + HD], jnp.zeros((1, HD), f32), turned[1:2, at : at + HD]]
    bias_ref[...] = jnp.concatenate(pieces, axis=1)


def assemble(place, turn, stacks, origin, parts, dp, hidden):
    count, own = stacks[0].shape[1:]
    width = (count - 16) * dp
    V = pl.BlockSpec(memory_space=pltpu.VMEM)
    M = pl.BlockSpec(memory_space=pltpu.SMEM)
    return pl.pallas_call(
        functools.partial(assemble_kernel, parts, origin),
        out_shape=[
            jax.ShapeDtypeStruct((width, own), bf16),
            jax.ShapeDtypeStruct((1, own), f32),
            jax.ShapeDtypeStruct((8, width), f32),
            jax.ShapeDtypeStruct((1, hidden), f32),
        ],
        in_specs=[M, M] + [V] * len(stacks),
        out_specs=[V] * 4,
        scratch_shapes=[pltpu.VMEM((dp, 16, own), f32)],
        cost_estimate=SHORT,
        name="assemble",
    )(place, turn, *stacks)


def input_grad_kernel(origin, parts, heads, turn_ref, resid_ref, own_ref, *refs):
    landed, refs = refs[: heads * parts], refs[heads * parts :]
    stacks, (out_ref, rest_ref) = refs[: len(origin)], refs[len(origin) :]
    pieces = sum(len(ks) for ks in origin)
    count = rest_ref.shape[0] // pieces
    for source, ks in zip(stacks, origin):
        for i, k in enumerate(ks):
            at = pl.multiple_of(lax.bitwise_xor(turn_ref[0], k) * count, count) if pieces > 1 else 0
            rest_ref[pl.ds(at, count), :] = source[i]
    near = jnp.concatenate([landed[h * parts][...] for h in range(heads)], axis=1)
    far = jnp.concatenate(
        [landed[h * parts + r][...] for h in range(heads) for r in range(1, parts)], axis=1
    )
    out_ref[...] = resid_ref[...] + dot(near, own_ref[...], NT) + dot(far, rest_ref[...], NT)


def input_gradient(turn, resid, w_own, landed, stacks, origin):
    heads, parts = len(landed), len(landed[0])
    W = pl.BlockSpec()
    return pl.pallas_call(
        functools.partial(input_grad_kernel, origin, parts, heads),
        grid=(1,),
        out_shape=jax.ShapeDtypeStruct(resid.shape, f32),
        in_specs=[pl.BlockSpec(memory_space=pltpu.SMEM)] + [W] * (2 + heads * parts + len(stacks)),
        out_specs=W,
        scratch_shapes=[pltpu.VMEM((resid.shape[1], stacks[0].shape[2]), bf16)],
        compiler_params=pltpu.CompilerParams(vmem_limit_bytes=60 << 20),
        cost_estimate=SHORT,
        name="input_gradient",
    )(turn, resid, w_own, *[v for h in landed for v in h], *stacks)


def put(keep_ref, give_ref, k, rows, columns, value):
    place = 2 * lax.bitwise_and(lax.shift_right_logical(k, 1), 1) + lax.shift_right_logical(k, 2)

    @pl.when(lax.bitwise_and(k, 1) == 0)
    def _():
        keep_ref[place, rows, columns] = value

    @pl.when(lax.bitwise_and(k, 1) == 1)
    def _():
        give_ref[place, rows, columns] = value


def weight_grads_kernel(parts, dp, turn_ref, place_ref, *refs):
    arrived = refs[:parts]
    first_ref, active_ref, second_ref, plow_ref, two_ref, lifted_ref, one_ref, sums_ref = refs[parts : parts + 8]
    keep_ref, give_ref, out_ref, sems = refs[parts + 8 :]
    width = first_ref.shape[1]
    hidden = active_ref.shape[1]
    emb = plow_ref.shape[1]
    lines, hlines, local = width // dp, hidden // dp, width // parts
    turn = turn_ref[0]
    place = place_ref[0]
    slabs = hidden // width
    base_mixer = hlines + lines * slabs
    base_project = base_mixer + lines
    piece = lines * emb // width
    base_vec = base_project + piece

    def leave(stage, at, count):
        for s in range(dp):
            k = lax.bitwise_xor(turn, s)
            slot = 2 * lax.bitwise_and(lax.shift_right_logical(k, 1), 1) + lax.shift_right_logical(k, 2)
            source = out_ref.at[s, pl.ds(at, count)]
            sem = sems.at[stage, s]

            @pl.when(lax.bitwise_and(k, 1) == 0)
            def _():
                pltpu.make_async_copy(source, keep_ref.at[slot, pl.ds(at, count)], sem).start()

            @pl.when(lax.bitwise_and(k, 1) == 1)
            def _():
                pltpu.make_async_copy(source, give_ref.at[slot, pl.ds(at, count)], sem).start()

    two = two_ref[...]
    per = width // hlines
    for c in range(slabs):
        part = dot(active_ref[:, c * width : (c + 1) * width], two, TN).astype(bf16)
        for i in range(per):
            out_ref[c * per + i, :hlines, :] = part[i * hlines : (i + 1) * hlines]
    leave(0, 0, hlines)
    first = first_ref[...]
    for c in range(slabs):
        part = dot(first, lifted_ref[:, c * width : (c + 1) * width], TN).astype(bf16)
        at = hlines + c * lines
        for s in range(dp):
            out_ref[s, at : at + lines, :] = part[s * lines : (s + 1) * lines]
    leave(1, hlines, base_mixer - hlines)
    vectors = sums_ref[...].astype(bf16)
    part = dot(second_ref[...], plow_ref[...], TN).astype(bf16)
    for s in range(dp):
        for a in range(width // emb):
            at = s * lines + a * piece
            out_ref[s, base_project : base_project + piece, a * emb : (a + 1) * emb] = part[at : at + piece]
        out_ref[s, base_vec : base_vec + 16, :] = vectors
    one = one_ref[...]
    per = local // lines
    for r in range(parts):
        part = dot(arrived[r][...], one, TN).astype(bf16)
        j = lax.rem(place + r, parts)
        for i in range(per):
            out_ref[j * per + i, base_mixer : base_mixer + lines, :] = part[i * lines : (i + 1) * lines]
    rest = base_vec + 16 - base_mixer
    leave(2, base_mixer, rest)
    for stage, (at, count) in enumerate(
        ((0, hlines), (hlines, base_mixer - hlines), (base_mixer, rest))
    ):
        for s in range(dp):
            pltpu.make_async_copy(
                out_ref.at[s, pl.ds(at, count)], keep_ref.at[0, pl.ds(at, count)], sems.at[stage, s]
            ).wait()


def weight_grads(turn, place, arrived, first, active, second, plow, two, lifted, one, sums, dp):
    parts = len(arrived)
    tokens, width = first.shape
    hidden = active.shape[1]
    emb = plow.shape[1]
    lines, hlines = width // dp, hidden // dp
    total = hlines + lines * (hidden // width) + lines + lines * emb // width + 16
    V = pl.BlockSpec(memory_space=pltpu.VMEM)
    M = pl.BlockSpec(memory_space=pltpu.SMEM)
    return pl.pallas_call(
        functools.partial(weight_grads_kernel, parts, dp),
        out_shape=[jax.ShapeDtypeStruct((dp // 2, total, width), bf16)] * 2,
        in_specs=[M, M] + [V] * (parts + 8),
        out_specs=[pl.BlockSpec(memory_space=pl.ANY)] * 2,
        scratch_shapes=[pltpu.VMEM((dp, total, width), bf16), pltpu.SemaphoreType.DMA((3, dp))],
        compiler_params=pltpu.CompilerParams(vmem_limit_bytes=56 << 20),
        cost_estimate=SHORT,
        name="weight_grads",
    )(turn, place, *arrived, first, active, second, plow, two, lifted, one, sums)


def triple_grads_kernel(parts, heads, dp, turn_ref, *refs):
    blocks = refs[:parts]
    backs = refs[parts : parts + heads * parts]
    keep_ref, give_ref = refs[parts + heads * parts :]
    width = blocks[0].shape[1]
    lines = width // dp
    turn = turn_ref[0]
    ones = jnp.ones((16, blocks[0].shape[0]), bf16)
    total = sums = None
    for r in range(parts):
        grad = jnp.concatenate([backs[h * parts + r][...] for h in range(heads)], axis=1)
        part, line = dot(blocks[r][...], grad, TN), dot(ones, grad, NN)
        total = part if r == 0 else total + part
        sums = line if r == 0 else sums + line
    total, sums = total.astype(bf16), sums.astype(bf16)
    columns = slice(0, total.shape[1])
    for s in range(dp):
        k = lax.bitwise_xor(turn, s)
        put(keep_ref, give_ref, k, slice(0, lines), columns, total[s * lines : (s + 1) * lines])
        put(keep_ref, give_ref, k, slice(lines, lines + 16), columns, sums)


def triple_grads(turn, blocks, backs, dp):
    parts, heads = len(blocks), len(backs)
    count, width = blocks[0].shape
    V = pl.BlockSpec(memory_space=pltpu.VMEM)
    return pl.pallas_call(
        functools.partial(triple_grads_kernel, parts, heads, dp),
        out_shape=[jax.ShapeDtypeStruct((dp // 2, width // dp + 16, 3 * HD * heads), bf16)] * 2,
        in_specs=[pl.BlockSpec(memory_space=pltpu.SMEM)] + [V] * (parts + heads * parts),
        out_specs=[V] * 2,
        compiler_params=pltpu.CompilerParams(vmem_limit_bytes=56 << 20),
        cost_estimate=SHORT,
        name="triple_grads",
    )(turn, *blocks, *[b for back in backs for b in back])


FOUR = (0, 2, 1, 3)


def unpack_kernel(slabs, place_ref, turn_ref, near_ref, far_ref, *refs):
    outs, all_ref = refs[:-1], refs[-1]
    shrink_ref, expand_ref, mixer_ref, project_ref = outs[:4]
    count, width = near_ref.shape[1:]
    for i, k in enumerate(FOUR):
        j = lax.bitwise_xor(place_ref[0], k)
        piece = (near_ref, far_ref)[i // 2][i % 2]
        all_ref[pl.ds(pl.multiple_of(j * count, count), count), :] = piece.astype(f32)
    lines, emb = project_ref.shape
    at = shrink_ref.shape[0]
    shrink_ref[...] = all_ref[:at, :]
    for c in range(slabs):
        expand_ref[:, c * width : (c + 1) * width] = all_ref[at : at + lines, :]
        at += lines
    mixer_ref[...] = all_ref[at : at + lines, :]
    at += lines
    piece = lines * emb // width
    for a in range(width // emb):
        project_ref[a * piece : (a + 1) * piece, :] = all_ref[at : at + piece, a * emb : (a + 1) * emb]
    at += piece
    mine = turn_ref[0]
    turned = pltpu.roll(all_ref[at : at + 8, :], width - mine * lines, 1)
    for i in range(6):
        outs[4 + i][...] = turned[i, :lines]
    hlines = outs[10].shape[0]
    per = width // hlines
    line = all_ref[pl.ds(at + 6 + lax.div(mine, per), 1), :]
    line = jnp.broadcast_to(line, (8, width))
    outs[10][...] = pltpu.roll(line, width - lax.rem(mine, per) * hlines, 1)[0, :hlines]


def unpack(place, turn, pairs, dp, hidden, emb):
    count, width = pairs[0].shape[1:]
    lines, hlines = width // dp, hidden // dp
    S = jax.ShapeDtypeStruct
    V = pl.BlockSpec(memory_space=pltpu.VMEM)
    M = pl.BlockSpec(memory_space=pltpu.SMEM)
    return pl.pallas_call(
        functools.partial(unpack_kernel, hidden // width),
        out_shape=[
            S((hlines, width), f32),
            S((lines, hidden), f32),
            S((lines, width), f32),
            S((lines, emb), f32),
        ]
        + [S((lines,), f32)] * 6
        + [S((hlines,), f32)],
        in_specs=[M, M, V, V],
        out_specs=[V] * 11,
        scratch_shapes=[pltpu.VMEM((4 * count, width), f32)],
        cost_estimate=SHORT,
        name="unpack",
    )(place, turn, *pairs)


def unpack_triple_kernel(heads, place_ref, turn_ref, *refs):
    four, (triple_ref, queries_ref, values_ref, all_ref) = refs[:-4], refs[-4:]
    parts = len(four)
    lines = triple_ref.shape[0]
    local = heads * HD
    width = parts * local
    for piece, k in zip(four, FOUR):
        all_ref[lax.bitwise_xor(place_ref[0], k)] = piece[...].astype(f32)
    for kind in range(3):
        part = jnp.concatenate(
            [
                all_ref[j][: lines + 8, (3 * h + kind) * HD : (3 * h + kind + 1) * HD]
                for j in range(parts)
                for h in range(heads)
            ],
            axis=1,
        )
        triple_ref[:, kind * width : (kind + 1) * width] = part[:lines]
        if kind != 1:
            sums = pltpu.roll(part[lines:], width - turn_ref[0] * lines, 1)
            (queries_ref, None, values_ref)[kind][...] = sums[0, :lines]


def unpack_triple(place, turn, four, heads):
    parts = len(four)
    count, columns = four[0].shape
    lines = count - 16
    S = jax.ShapeDtypeStruct
    V = pl.BlockSpec(memory_space=pltpu.VMEM)
    M = pl.BlockSpec(memory_space=pltpu.SMEM)
    return pl.pallas_call(
        functools.partial(unpack_triple_kernel, heads),
        out_shape=[S((lines, parts * columns), f32), S((lines,), f32), S((lines,), f32)],
        in_specs=[M, M] + [V] * parts,
        out_specs=[V] * 3,
        scratch_shapes=[pltpu.VMEM((parts, count, columns), f32)],
        cost_estimate=SHORT,
        name="unpack_triple",
    )(place, turn, *four)


def gather(v):
    return lax.all_gather(v, "dp", axis=0, tiled=False)


def send(v, shift):
    if shift == 0:
        return v
    parts = lax.axis_size("seq")
    return lax.ppermute(v, "seq", [(i, (i + shift) % parts) for i in range(parts)])


def hop(v, step):
    parts = lax.axis_size("seq")
    return lax.ppermute(v, "seq", [(i, i + step) for i in range(parts) if 0 <= i + step < parts])


def swap(v, bits):
    return lax.ppermute(v, "dp", [(i, i ^ bits) for i in range(lax.axis_size("dp"))])


def double(v, bits):
    return jnp.concatenate([v, swap(v, bits)])


def together(*values):
    return lax.optimization_barrier(values)


def add(a, b):
    return (a.astype(f32) + b.astype(f32)).astype(bf16)


def sum_dp_core(keep, other):
    half = keep.shape[1] // 32 * 16
    a, b = slice(0, half), slice(half, None)
    pick = lambda rows, *slots: jnp.concatenate(
        [add(keep[i : i + 1, rows], other[i : i + 1, rows]) for i in slots]
    )
    return (pick(a, 0, 1), pick(a, 2, 3), pick(b, 0, 2), pick(b, 1, 3))


def sum_dp_first(sums):
    a_keep, a_give, b_keep, b_give = sums
    return (a_keep, swap(a_give, 2), b_keep, swap(b_give, 4))


def sum_dp_second(sums):
    a_keep, a_came, b_keep, b_came = sums
    a, b = add(a_keep, a_came), add(b_keep, b_came)
    return (a[0], a[1], b[0], b[1])


def sum_dp_last(sums):
    a_keep, a_give, b_keep, b_give = sums
    return (a_keep, swap(a_give, 4), b_keep, swap(b_give, 2))


def swap_seq(v, bits):
    return lax.ppermute(v, "seq", [(i, i ^ bits) for i in range(lax.axis_size("seq"))])


def turned_seq(items):
    place = lax.axis_index("seq")
    came = jnp.stack(items)
    return [
        lax.dynamic_index_in_dim(came, lax.bitwise_xor(place, k), keepdims=False)
        for k in range(len(items))
    ]


def sum_seq_first(v):
    v = v.reshape(4, -1, v.shape[1])
    v = turned_seq([v[i] for i in range(4)])
    came = swap_seq(jnp.stack([v[1], v[3]]), 1)
    return add(v[0], came[0]), add(v[2], came[1])


def sum_seq_second(v):
    return add(v[0], swap_seq(v[1], 2))


def rows_of(pieces, dp, width):
    flat = jnp.concatenate(pieces, axis=1)
    pad = -flat.shape[1] % width
    return jnp.pad(flat, ((0, 0), (0, pad))).reshape(dp, -1, width)


def shards(
    layer_input,
    triple_weight,
    query_bias,
    value_bias,
    mixer_weight,
    mixer_bias,
    first_gain,
    first_shift,
    expand_weight,
    expand_bias,
    shrink_weight,
    shrink_bias,
    second_gain,
    second_shift,
    project_weight,
    kept_tokens,
    upstream,
):
    parts = lax.axis_size("seq")
    dp = lax.axis_size("dp")
    place = lax.axis_index("seq")
    mine = lax.axis_index("dp")
    rows = layer_input[0]
    tokens, width = rows.shape
    local = width // parts
    heads = local // HD
    lines = width // dp
    hidden = expand_weight.shape[1]
    hlines = hidden // dp
    emb = project_weight.shape[1]

    fast = dp == 8 and parts == 4 and heads == 3 and lines % 16 == 0
    if not fast:
        blocks = [send(rows, r) for r in range(parts)]

    where = jnp.reshape(place, (1,))
    turn = jnp.reshape(mine, (1,))
    vectors = [
        query_bias,
        value_bias,
        mixer_bias,
        first_gain,
        first_shift,
        shrink_bias,
        second_gain,
        second_shift,
        expand_bias,
    ]
    both = jnp.concatenate([mixer_weight, project_weight], axis=1)
    if fast:
        wide, shrink = jnp.concatenate([expand_weight, both], axis=1)[None], shrink_weight[None]
        own, rest = prepare(where, triple_weight, vectors, parts)
        x_first, y_first = [(0, 2), (4, 6), (1, 3), (5, 7)], [(0, 4), (2, 6), (1, 5), (3, 7)]
        below, above = [rows, hop(rows, 1)], [rows, hop(rows, -1)]
        own = [own] + [swap(own, k) for k in (2, 4, 6)]
        own, below[1], above[1], wide, shrink = lax.optimization_barrier(
            (own, below[1], above[1], wide, shrink)
        )
        below.append(hop(below[1], 1))
        above.append(hop(above[1], -1))
        own = jnp.stack(own)
        own = [own, swap(own, 1)]
        wide, shrink = double(wide, 2), double(shrink, 4)
        below[2], above[2], wide, shrink, own = lax.optimization_barrier(
            (below[2], above[2], wide, shrink, own)
        )
        below.append(hop(below[2], 1))
        above.append(hop(above[2], -1))
        w_wide = [wide, swap(wide, 4)]
        w_shrink = [shrink, swap(shrink, 2)]
        w_own, bias, vec, b_expand = assemble(
            where, turn, own, [(0, 2, 4, 6), (1, 3, 5, 7)], parts, dp, hidden
        )
        blocks = [rows] + [
            jnp.where(place >= r, below[r], above[parts - r]) for r in range(1, parts)
        ]
    else:
        turned = jnp.roll(
            triple_weight.reshape(lines, 3, parts, heads, HD), -place, axis=2
        ).transpose(0, 2, 3, 1, 4)
        w_own = gather(turned[:, 0].reshape(lines, 3 * local)).reshape(width, 3 * local)
        w_rest = [gather(turned[:, 1:].swapaxes(1, 2).reshape(lines, -1)).reshape(1, width, -1)]
        small = gather(jnp.concatenate(vectors)).astype(f32)
        vec = jnp.stack([small[:, i * lines : (i + 1) * lines].reshape(width) for i in range(8)])
        b_expand = small[:, 8 * lines :].reshape(1, hidden)
        b_query, b_value = [
            lax.dynamic_slice(vec[i], (place * local,), (local,)).reshape(heads, HD) for i in (0, 1)
        ]
        bias = jnp.stack([b_query, jnp.zeros((heads, HD), f32), b_value], axis=1).reshape(1, -1)
        w_wide = [gather(jnp.concatenate([expand_weight, both], axis=1)).reshape(1, width, -1)]
        w_shrink = [gather(shrink_weight).reshape(1, hidden, width)]
        x_first = y_first = [(0,)]

    joined = [(dot(b, w_own, NN) + bias).astype(bf16) for b in blocks]
    order = list(range(2, parts)) + [1, 0]
    mixed_own = [None] * parts
    stats = [None] * parts
    arrived = [None] * parts
    for i, r in enumerate(order):
        if i > 0:
            joined, mixed_own[order[i - 1]] = together(joined, mixed_own[order[i - 1]])
        if fast and i == 0:
            early = [swap(w_wide[0], 1), swap(w_shrink[0], 1)]
            joined, early = together(joined, early)
        mixed_own[r], stats[r] = attend_forward(joined, r, heads)
        arrived[r] = send(mixed_own[r], -r)
    if fast:
        w_wide[1], w_shrink[1], mixed_own[0], arrived[2], arrived[3] = lax.optimization_barrier(
            (w_wide[1], w_shrink[1], mixed_own[0], arrived[2], arrived[3])
        )
        w_wide += [early[0], swap(w_wide[1], 1)]
        w_shrink += [early[1], swap(w_shrink[1], 1)]
        rest, arrived, w_wide[3], w_shrink[3] = together(rest[None], arrived, w_wide[3], w_shrink[3])
        rest = double(rest, 2)
    results = feed_forward(
        where,
        turn,
        rows,
        arrived,
        vec,
        b_expand,
        kept_tokens[0].astype(f32)[:, None],
        upstream[0],
        w_wide,
        x_first,
        w_shrink,
        y_first,
    )
    embedded, grad_resid_one, first, active, second, plow, two, lifted, one, sums = results[:10]
    grads = [send(g, r) for r, g in enumerate(results[10:])]

    slabs = hidden // width
    backs = []
    landed = []
    inputs = (joined, grads, mixed_own, stats)

    def backward(h, inputs):
        back = attend_backward(*inputs, h)
        backs.append(back)
        landed.append([send(back[r], -r) for r in range(parts)])

    if fast:
        first, rest = together(first, rest)
        w_rest = [rest, swap(rest, 4)]
        keep, give = weight_grads(
            turn, where, arrived, first, active, second, plow, two, lifted, one, sums, dp
        )
        grads, give, w_rest = together(grads, give, w_rest)
        other = swap(give, 1)
        w_rest += [swap(w, 1) for w in w_rest]
        inputs, keep = together((joined, grads, mixed_own, stats), keep)
        backward(0, inputs)
        keep, other, backs[0] = together(keep, other, backs[0])
        batch = sum_dp_core(keep, other)
        inputs, batch, w_rest = together(inputs, batch, w_rest)
        batch = sum_dp_first(batch)
        backward(1, inputs)
        batch, landed[0], backs[1] = together(batch, landed[0], backs[1])
        batch = sum_dp_second(batch)
        inputs, batch = together(inputs, batch)
        batch = sum_dp_last(batch)
        backward(2, inputs)
        batch = jnp.concatenate([add(batch[0], batch[1]), add(batch[2], batch[3])])
        backs, landed[1], batch = together(backs, landed[1], batch)
        batch = sum_seq_first(batch)
        keep, give = triple_grads(turn, blocks, backs, dp)
        give, batch, landed[2] = together(give, batch, landed[2])
        last = add(keep, swap(give, 1))
        last = add(last[:2], swap(last[2:], 2))
        last = add(last[0], swap(last[1], 4))
        batch = sum_seq_second(batch)
        input_grad = input_gradient(turn, grad_resid_one, w_own, landed, w_rest, x_first)
        batch, last, input_grad = together(batch, last, input_grad)
        last = [last, swap_seq(last, 2)]
        both = jnp.stack([batch, swap_seq(batch, 2)])
        both, last = together(both, last)
        last += [swap_seq(v, 1) for v in last]
        r_triple, r_queries, r_values = unpack_triple(where, turn, last, heads)
        outs = unpack(where, turn, [both, swap_seq(both, 1)], dp, hidden, emb)
        r_shrink, r_expand, r_mixer, r_project = outs[:4]
        r_offset, r_gamma, r_beta, r_settle, r_gain, r_shift, r_lift = outs[4:]
    else:
        g_expand = dot(first, lifted, TN).astype(bf16)
        mixed = jnp.concatenate(arrived, axis=1)
        g_mixer = jnp.roll(dot(mixed, one, TN).reshape(parts, local, width), place, axis=0)
        g_project = dot(second, plow, TN).astype(bf16)
        batch = jnp.concatenate(
            [
                dot(active, two, TN).astype(bf16).reshape(dp, hlines, width),
                *[
                    g_expand[:, c * width : (c + 1) * width].reshape(dp, lines, width)
                    for c in range(slabs)
                ],
                g_mixer.astype(bf16).reshape(dp, lines, width),
                jnp.stack([rows_of([g[None].reshape(1, -1)], 1, width)[0] for g in g_project.reshape(dp, lines, emb)]),
                jnp.broadcast_to(sums.astype(bf16), (dp,) + sums.shape),
            ],
            axis=1,
        )
        batch = lax.psum_scatter(batch, "dp", scatter_dimension=0, tiled=False)
        batch = lax.psum(batch, "seq")
        for h in range(heads):
            backward(h, inputs)
        g_own = jnp.concatenate([jnp.concatenate(back, axis=0) for back in backs], axis=1)
        g_triple = dot(jnp.concatenate(blocks, axis=0), g_own, TN)
        columns = jnp.sum(g_own.astype(f32), axis=0).astype(bf16)
        last = jnp.concatenate(
            [
                g_triple.astype(bf16).reshape(dp, lines, 3 * local),
                jnp.broadcast_to(columns, (dp, 1, 3 * local)),
            ],
            axis=1,
        )
        last = lax.psum_scatter(last, "dp", scatter_dimension=0, tiled=False)
        last = lax.all_gather(last, "seq", axis=0, tiled=False)
        batch = batch.astype(f32)
        r_shrink = batch[:hlines]
        at = hlines
        r_expand = jnp.concatenate(
            [batch[at + c * lines : at + (c + 1) * lines] for c in range(slabs)], axis=1
        )
        at += lines * slabs
        r_mixer = batch[at : at + lines]
        at += lines
        piece = lines * emb // width
        r_project = batch[at : at + piece].reshape(lines, emb)
        tail = batch[at + piece :]
        r_offset, r_gamma, r_beta, r_settle, r_gain, r_shift = [
            lax.dynamic_slice(tail[i], (mine * lines,), (lines,)) for i in range(6)
        ]
        r_lift = lax.dynamic_slice(
            tail[6 : 6 + slabs].reshape(hidden), (mine * hlines,), (hlines,)
        )

        last = last.astype(f32)
        last = last.reshape(parts, lines + 1, heads, 3, HD).transpose(1, 3, 0, 2, 4)
        r_triple = last[:lines].reshape(lines, 3 * width)
        sums = last[lines].reshape(3, width)
        r_queries = lax.dynamic_slice(sums[0], (mine * lines,), (lines,))
        r_values = lax.dynamic_slice(sums[2], (mine * lines,), (lines,))
        input_grad = input_gradient(turn, grad_resid_one, w_own, landed, w_rest, x_first)
    return (
        embedded[None],
        input_grad[None],
        r_triple,
        r_queries,
        r_values,
        r_mixer,
        r_offset,
        r_gamma,
        r_beta,
        r_expand,
        r_lift,
        r_shrink,
        r_settle,
        r_gain,
        r_shift,
        r_project,
    )


def solution(mesh):
    whole = P("dp", "seq", None)
    rows = P("dp", None)
    flat = P("dp")
    in_specs = (
        whole,
        rows,
        flat,
        flat,
        rows,
        flat,
        flat,
        flat,
        rows,
        flat,
        rows,
        flat,
        flat,
        flat,
        rows,
        P("dp", "seq"),
        whole,
    )
    out_specs = (
        whole,
        whole,
        rows,
        flat,
        flat,
        rows,
        flat,
        flat,
        flat,
        rows,
        flat,
        rows,
        flat,
        flat,
        flat,
        rows,
    )
    return jax.shard_map(shards, mesh=mesh, in_specs=in_specs, out_specs=out_specs, check_vma=False)
```

profile of v0, /device:TPU:0, one launch (start us, length us, event | category | flops | bytes accessed | tf_op | source)
XLA Modules:
  0.0 368.9 jit_solution(17265661523934199955)
XLA Ops:
  0.7 6.0 %collective-permute-start.3 = (bf16[512,768]{1,0:T(8,128)(2,1)}, bf16[512,768]{1,0:T(8,128)(2,1)}, u32[]{:S(2)}, u32[]{:S(2)}) collective-permute-start(bf16[512,768]{1,0:T(8,128)(2,1)} %bitcast.56), channel_id=1, source_target_pairs={{0,8},{8,16},{16,24},{1,9},{9,17},{17,25},{2,10},{10,18},{18,26},{... | collective-permute-start | bytes 2359304 | tf_op jit(solution)/shard_map/ppermute | solution.py:687
  8.0 2.5 prepare.1
  10.5 1.5 collective-permute-start
  12.0 1.5 collective-permute-start.1
  14.0 2.1 maximum_bitcast_fusion
  16.6 3.8 %collective-permute-done.1 = bf16[112,576]{1,0:T(8,128)(2,1)S(1)} collective-permute-done((bf16[112,576]{1,0:T(8,128)(2,1)}, bf16[112,576]{1,0:T(8,128)(2,1)S(1)}, u32[]{:S(2)}, u32[]{:S(2)}) %collective-permute-start.1) | collective-permute-done | bytes 129056 | tf_op jit(solution)/shard_map/ppermute | solution.py:691
  20.4 2.4 collective-permute-done.3
  22.8 5.0 %collective-permute-done.4 = bf16[512,768]{1,0:T(8,128)(2,1)} collective-permute-done((bf16[512,768]{1,0:T(8,128)(2,1)}, bf16[512,768]{1,0:T(8,128)(2,1)}, u32[]{:S(2)}, u32[]{:S(2)}) %collective-permute-start.4) | collective-permute-done | bytes 786464 | tf_op jit(solution)/shard_map/ppermute | solution.py:687
  27.9 1.5 collective-permute-start.7
  29.4 1.5 collective-permute-start.8
  30.9 3.5 collective-permute-start.5
  35.9 7.0 %collective-permute-done.8 = bf16[1,384,768]{2,1,0:T(8,128)(2,1)S(1)} collective-permute-done((bf16[1,384,768]{2,1,0:T(8,128)(2,1)S(1)}, bf16[1,384,768]{2,1,0:T(8,128)(2,1)S(1)}, u32[]{:S(2)}, u32[]{:S(2)}) %collective-permute-start.8) | collective-permute-done | bytes 589856 | tf_op jit(solution)/shard_map/ppermute | solution.py:691
  43.1 2.7 collective-permute-done.7
  45.7 2.6 pad_maximum_fusion.refs_9_
  48.8 5.1 %collective-permute-done.6 = bf16[512,768]{1,0:T(8,128)(2,1)} collective-permute-done((bf16[512,768]{1,0:T(8,128)(2,1)}, bf16[512,768]{1,0:T(8,128)(2,1)}, u32[]{:S(2)}, u32[]{:S(2)}) %collective-permute-start.6) | collective-permute-done | bytes 786464 | tf_op jit(solution)/shard_map/ppermute | solution.py:687
  55.6 5.6 %collective-permute-start.11 = (bf16[512,768]{1,0:T(8,128)(2,1)}, bf16[512,768]{1,0:T(8,128)(2,1)}, u32[]{:S(2)}, u32[]{:S(2)}) collective-permute-start(bf16[512,768]{1,0:T(8,128)(2,1)} %collective-permute-done.5), channel_id=1, source_target_pairs={{0,8},{8,16},{16,24},{1,9},{9,17},{17,25},{2,10},{10,18},{18,26},{... | collective-permute-start | bytes 2359304 | tf_op jit(solution)/shard_map/ppermute | solution.py:687
  61.3 2.3 assemble.1
  64.4 2.0 fusion.4.refs_0_
  66.4 1.5 broadcast_select_fusion.1.refs_2_
  69.0 7.3 %collective-permute-done.10 = bf16[512,768]{1,0:T(8,128)(2,1)} collective-permute-done((bf16[512,768]{1,0:T(8,128)(2,1)}, bf16[512,768]{1,0:T(8,128)(2,1)}, u32[]{:S(2)}, u32[]{:S(2)}) %collective-permute-start.10) | collective-permute-done | bytes 786464 | tf_op jit(solution)/shard_map/ppermute | solution.py:687
  78.0 1.5 broadcast_select_fusion.refs_3_
  81.2 5.0 %attend_forward.4 = (bf16[512,192]{1,0:T(8,128)(2,1)S(1)}, f32[512,8]{1,0:T(8,128)S(1)}) custom-call(bf16[512,576]{1,0:T(8,128)(2,1)S(1)} %fusion.4.refs_0_, bf16[512,576]{1,0:T(8,128)(2,1)S(1)} %fusion.refs_1_, bf16[512,576]{1,0:T(8,128)(2,1)S(1)} %fusion.1.refs_2_, bf16[512,576]{1,0:T(8,128)(2,1)S(1)} %fusion.2.refs_3_), custom_call_target="tpu_custom_call" | custom-call | tf_op jit(solution)/shard_map/attend_forward/pallas_call | solution.py:53
  86.3 1.8 collective-permute-start.17
  88.0 5.4 %attend_forward.5 = (bf16[512,192]{1,0:T(8,128)(2,1)S(1)}, f32[512,8]{1,0:T(8,128)S(1)}) custom-call(bf16[512,576]{1,0:T(8,128)(2,1)S(1)} %fusion.4.refs_0_, bf16[512,576]{1,0:T(8,128)(2,1)S(1)} %fusion.refs_1_, bf16[512,576]{1,0:T(8,128)(2,1)S(1)} %fusion.1.refs_2_, bf16[512,576]{1,0:T(8,128)(2,1)S(1)} %fusion.2.refs_3_), custom_call_target="tpu_custom_call" | custom-call | tf_op jit(solution)/shard_map/attend_forward/pallas_call | solution.py:53
  94.7 5.0 %attend_forward.6 = (bf16[512,192]{1,0:T(8,128)(2,1)S(1)}, f32[512,8]{1,0:T(8,128)S(1)}) custom-call(bf16[512,576]{1,0:T(8,128)(2,1)S(1)} %fusion.4.refs_0_, bf16[512,576]{1,0:T(8,128)(2,1)S(1)} %fusion.refs_1_, bf16[512,576]{1,0:T(8,128)(2,1)S(1)} %fusion.1.refs_2_, bf16[512,576]{1,0:T(8,128)(2,1)S(1)} %fusion.2.refs_3_), custom_call_target="tpu_custom_call" | custom-call | tf_op jit(solution)/shard_map/attend_forward/pallas_call | solution.py:53
  99.8 5.0 %attend_forward.7 = (bf16[512,192]{1,0:T(8,128)(2,1)S(1)}, f32[512,8]{1,0:T(8,128)S(1)}) custom-call(bf16[512,576]{1,0:T(8,128)(2,1)S(1)} %fusion.4.refs_0_, bf16[512,576]{1,0:T(8,128)(2,1)S(1)} %fusion.refs_1_, bf16[512,576]{1,0:T(8,128)(2,1)S(1)} %fusion.1.refs_2_, bf16[512,576]{1,0:T(8,128)(2,1)S(1)} %fusion.2.refs_3_), custom_call_target="tpu_custom_call" | custom-call | tf_op jit(solution)/shard_map/attend_forward/pallas_call | solution.py:53
  106.8 2.7 collective-permute-start.14
  109.5 5.8 %collective-permute-done.14.refs_2_.refs_1_ = bf16[512,192]{1,0:T(8,128)(2,1)S(1)} collective-permute-done((bf16[512,192]{1,0:T(8,128)(2,1)S(1)}, bf16[512,192]{1,0:T(8,128)(2,1)S(1)}, u32[]{:S(2)}, u32[]{:S(2)}) %collective-permute-start.14) | collective-permute-done | bytes 196640 | tf_op jit(solution)/shard_map/ppermute | solution.py:682
  117.8 29.4 %feed_forward.1 = (f32[512,128]{1,0:T(8,128)}, f32[512,768]{1,0:T(8,128)}, bf16[512,768]{1,0:T(8,128)(2,1)}, bf16[512,3072]{1,0:T(8,128)(2,1)}, bf16[512,768]{1,...) custom-call(s32[1]{0:T(128)} %bitcast.place_ref, ...), custom_call_target="tpu_custom_call" | custom-call | tf_op jit(solution)/shard_map/feed_forward/pallas_call | solution.py:284
  148.4 1.6 collective-permute-start.25
  151.1 3.4 collective-permute-start.22
  154.9 12.0 %weight_grads.1 = (bf16[4,896,768]{2,1,0:T(8,128)(2,1)}, bf16[4,896,768]{2,1,0:T(8,128)(2,1)}) custom-call(s32[1]{0:T(128)} %bitcast.1.turn_ref, s32[1]{0:T(128)} %bitcast.place_ref, bf16[512,192]{1,0:T(8,128)(2,1)} %copy-done.4, bf16[512,192]{1,0:T(8,128)(2,1)} %copy-done.28, bf16[512,192]{1,0:T(8,128)(2,1)} %copy-done.26, bf16[512,192]{1,0:T(8,128)(2,1)} %copy-done.27, ...), custom_call_target="tpu_custom_call" | custom-call | tf_op jit(solution)/shard_map/weight_grads/pallas_call | solution.py:526
  166.9 3.5 collective-permute-done.22.refs_6_
  171.2 13.7 %attend_backward.3 = (bf16[512,192]{1,0:T(8,128)(2,1)}, bf16[512,192]{1,0:T(8,128)(2,1)}, bf16[512,192]{1,0:T(8,128)(2,1)}, bf16[512,192]{1,0:T(8,128)(2,1)}) custom-call(bf16[512,576]{1,0:T(8,128)(2,1)} %copy-done, bf16[512,576]{1,0:T(8,128)(2,1)} %copy-done.2, bf16[512,576]{1,0:T(8,128)(2,1)} %copy-done.1, bf16[512,576]{1,0:T(8,128)(2,1)} %copy-done.3, ...), custom_call_target="tpu_custom_call" | custom-call | tf_op jit(solution)/shard_map/attend_backward/pallas_call | solution.py:113
  185.0 4.8 %add_convert_fusion.5 = (bf16[1,448,768]{2,1,0:T(8,128)(2,1)S(1)}, bf16[1,448,768]{2,1,0:T(8,128)(2,1)S(1)}, bf16[1,448,768]{2,1,0:T(8,128)(2,1)S(1)}, bf16[1,44...) fusion(bf16[4,896,768]{2,1,0:T(8,128)(2,1)} %collective-permute, ...), kind=kLoop, calls=%fused_computation.16 | loop fusion | flops 11010048 | bytes 16515072 | tf_op jit(solution)/shard_map/convert_element_type | solution.py:703
  192.5 1.5 collective-permute-start.29
  194.5 5.4 %collective-permute-start.31 = (bf16[512,192]{1,0:T(8,128)(2,1)}, bf16[512,192]{1,0:T(8,128)(2,1)}, u32[]{:S(2)}, u32[]{:S(2)}) collective-permute-start(bf16[512,192]{1,0:T(8,128)(2,1)} %get-tuple-element.408.refs_5_), channel_id=1, source_target_pairs={{0,24},{8,0},{16,8},{24,16},{1,25},{9,1},{17,9},{25,17},{2,26},{10... | collective-permute-start | bytes 589832 | tf_op jit(solution)/shard_map/ppermute | solution.py:682
  199.9 2.0 collective-permute-start.32
  201.9 13.9 %attend_backward.4 = (bf16[512,192]{1,0:T(8,128)(2,1)}, bf16[512,192]{1,0:T(8,128)(2,1)}, bf16[512,192]{1,0:T(8,128)(2,1)}, bf16[512,192]{1,0:T(8,128)(2,1)}) custom-call(bf16[512,576]{1,0:T(8,128)(2,1)} %copy-done, bf16[512,576]{1,0:T(8,128)(2,1)} %copy-done.2, bf16[512,576]{1,0:T(8,128)(2,1)} %copy-done.1, bf16[512,576]{1,0:T(8,128)(2,1)} %copy-done.3, ...), custom_call_target="tpu_custom_call" | custom-call | tf_op jit(solution)/shard_map/attend_backward/pallas_call | solution.py:113
  215.8 9.2 %collective-permute-done.32.refs_2_ = bf16[512,192]{1,0:T(8,128)(2,1)} collective-permute-done((bf16[512,192]{1,0:T(8,128)(2,1)}, bf16[512,192]{1,0:T(8,128)(2,1)}, u32[]{:S(2)}, u32[]{:S(2)}) %collective-permute-start.32) | collective-permute-done | bytes 196640 | tf_op jit(solution)/shard_map/ppermute | solution.py:682
  226.3 1.7 add_convert_fusion.1
  230.4 5.4 %collective-permute-start.34 = (bf16[512,192]{1,0:T(8,128)(2,1)}, bf16[512,192]{1,0:T(8,128)(2,1)S(1)}, u32[]{:S(2)}, u32[]{:S(2)}) collective-permute-start(bf16[512,192]{1,0:T(8,128)(2,1)} %get-tuple-element.412.refs_9_), channel_id=1, source_target_pairs={{0,24},{8,0},{16,8},{24,16},{1,25},{9,1},{17,9},{25,17},{2,26},{10... | collective-permute-start | bytes 589832 | tf_op jit(solution)/shard_map/ppermute | solution.py:682
  235.8 2.1 collective-permute-start.35
  238.1 13.5 %attend_backward.5 = (bf16[512,192]{1,0:T(8,128)(2,1)}, bf16[512,192]{1,0:T(8,128)(2,1)}, bf16[512,192]{1,0:T(8,128)(2,1)}, bf16[512,192]{1,0:T(8,128)(2,1)}) custom-call(bf16[512,576]{1,0:T(8,128)(2,1)} %copy-done, bf16[512,576]{1,0:T(8,128)(2,1)} %copy-done.2, bf16[512,576]{1,0:T(8,128)(2,1)} %copy-done.1, bf16[512,576]{1,0:T(8,128)(2,1)} %copy-done.3, ...), custom_call_target="tpu_custom_call" | custom-call | tf_op jit(solution)/shard_map/attend_backward/pallas_call | solution.py:113
  252.1 7.9 %collective-permute-done.35.refs_6_ = bf16[512,192]{1,0:T(8,128)(2,1)S(1)} collective-permute-done((bf16[512,192]{1,0:T(8,128)(2,1)}, bf16[512,192]{1,0:T(8,128)(2,1)S(1)}, u32[]{:S(2)}, u32[]{:S(2)}) %collective-permute-start.35) | collective-permute-done | bytes 196640 | tf_op jit(solution)/shard_map/ppermute | solution.py:682
  261.1 1.7 collective-permute-start.40
  262.8 1.7 collective-permute-start.41
  264.8 7.0 %triple_grads.1 = (bf16[4,112,576]{2,1,0:T(8,128)(2,1)}, bf16[4,112,576]{2,1,0:T(8,128)(2,1)}) custom-call(s32[1]{0:T(128)} %bitcast.1.turn_ref, bf16[512,768]{1,0:T(8,128)(2,1)} %bitcast.59, bf16[512,768]{1,0:T(8,128)(2,1)} %copy-done.15, bf16[512,768]{1,0:T(8,128)(2,1)} %copy-done.14, bf16[512,768]{1,0:T(8,128)(2,1)} %copy-done.16, ...), custom_call_target="tpu_custom_call" | custom-call | tf_op jit(solution)/shard_map/triple_grads/pallas_call | solution.py:564
  271.8 12.9 %collective-permute-done.39 = bf16[2,224,768]{2,1,0:T(8,128)(2,1)S(1)} collective-permute-done((bf16[2,224,768]{2,1,0:T(8,128)(2,1)S(1)}, bf16[2,224,768]{2,1,0:T(8,128)(2,1)S(1)}, u32[]{:S(2)}, u32[]{:S(2)}) %collective-permute-start.39) | collective-permute-done | bytes 688160 | tf_op jit(solution)/shard_map/ppermute | solution.py:732
  284.9 2.6 collective-permute-done.40.refs_9_
  288.3 6.6 %collective-permute-done.42.refs_11_ = bf16[512,192]{1,0:T(8,128)(2,1)S(1)} collective-permute-done((bf16[512,192]{1,0:T(8,128)(2,1)S(1)}, bf16[512,192]{1,0:T(8,128)(2,1)S(1)}, u32[]{:S(2)}, u32[]{:S(2)}) %collective-permute-start.42) | collective-permute-done | bytes 196640 | tf_op jit(solution)/shard_map/ppermute | solution.py:682
  294.9 2.0 collective-permute-done.44
  297.1 1.4 collective-permute-start.45
  298.5 6.9 %input_gradient.1 = f32[512,768]{1,0:T(8,128)} custom-call(s32[1]{0:T(128)} %bitcast.1.turn_ref, f32[512,768]{1,0:T(8,128)} %get-tuple-element.425.resid_ref, bf16[768,576]{1,0:T(8,128)(2,1)} %get-tuple-element.251.own_ref, bf16[512,192]{1,0:T(8,128)(2,1)} %get-tuple-element.426.refs_4_.refs_0_, bf16[512,192]{1,0:T(8,128)(2,1)} %collective-permute-done.31.refs_1_, ...), custom_call_target="tpu_custom_call" | custom-call | tf_op jit(solution)/shard_map/input_gradient/pallas_call | solution.py:422
  306.1 1.6 collective-permute-start.46
  307.8 6.9 %collective-permute-done.43 = bf16[224,768]{1,0:T(8,128)(2,1)S(1)} collective-permute-done((bf16[224,768]{1,0:T(8,128)(2,1)S(1)}, bf16[224,768]{1,0:T(8,128)(2,1)S(1)}, u32[]{:S(2)}, u32[]{:S(2)}) %collective-permute-start.43) | collective-permute-done | bytes 344096 | tf_op jit(solution)/shard_map/ppermute | solution.py:732
  314.9 2.9 collective-permute-start.48
  317.8 17.1 %collective-permute-done.47 = bf16[224,768]{1,0:T(8,128)(2,1)S(1)} collective-permute-done((bf16[224,768]{1,0:T(8,128)(2,1)S(1)}, bf16[224,768]{1,0:T(8,128)(2,1)S(1)}, u32[]{:S(2)}, u32[]{:S(2)}) %collective-permute-start.47) | collective-permute-done | bytes 344096 | tf_op jit(solution)/shard_map/ppermute | solution.py:732
  335.0 2.9 collective-permute-done.48.refs_1_
  337.9 2.0 collective-permute-start.49
  340.0 19.3 %collective-permute-done.49.refs_2_ = bf16[112,576]{1,0:T(8,128)(2,1)S(1)} collective-permute-done((bf16[112,576]{1,0:T(8,128)(2,1)S(1)}, bf16[112,576]{1,0:T(8,128)(2,1)S(1)}, u32[]{:S(2)}, u32[]{:S(2)}) %collective-permute-start.49) | collective-permute-done | bytes 129056 | tf_op jit(solution)/shard_map/ppermute | solution.py:732
  359.3 2.1 collective-permute-done.50.refs_3_
  362.1 2.5 unpack_triple.1
  365.5 3.1 unpack.1
  (192 shorter events, 33.0 us)
Async XLA Ops:
  0.6 28.7 %copy-start.31 = (bf16[384,768]{1,0:T(8,128)(2,1)S(1)}, bf16[384,768]{1,0:T(8,128)(2,1)}, u32[]{:S(2)}) copy-start(bf16[384,768]{1,0:T(8,128)(2,1)} %param.27) | copy-start | bytes 1769476
  0.7 22.2 %collective-permute-start.3 = (bf16[512,768]{1,0:T(8,128)(2,1)}, bf16[512,768]{1,0:T(8,128)(2,1)}, u32[]{:S(2)}, u32[]{:S(2)}) collective-permute-start(bf16[512,768]{1,0:T(8,128)(2,1)} %bitcast.56), channel_id=1, source_target_pairs={{0,8},{8,16},{16,24},{1,9},{9,17},{17,25},{2,10},{10,18},{18,26},{... | collective-permute-start | bytes 2359304 | tf_op jit(solution)/shard_map/ppermute | solution.py:687
  6.7 21.2 %collective-permute-start.4 = (bf16[512,768]{1,0:T(8,128)(2,1)}, bf16[512,768]{1,0:T(8,128)(2,1)}, u32[]{:S(2)}, u32[]{:S(2)}) collective-permute-start(bf16[512,768]{1,0:T(8,128)(2,1)} %bitcast.57), channel_id=1, source_target_pairs={{8,0},{16,8},{24,16},{9,1},{17,9},{25,17},{10,2},{18,10},{26,18},{... | collective-permute-start | bytes 2359304 | tf_op jit(solution)/shard_map/ppermute | solution.py:687
  10.5 25.2 %copy-start.41 = (bf16[112,576]{1,0:T(8,128)(2,1)S(1)}, bf16[112,576]{1,0:T(8,128)(2,1)}, u32[]{:S(2)}) copy-start(bf16[112,576]{1,0:T(8,128)(2,1)} %get-tuple-element.245) | copy-start | bytes 387076
  10.5 6.1 %collective-permute-start = (bf16[112,576]{1,0:T(8,128)(2,1)}, bf16[112,576]{1,0:T(8,128)(2,1)S(1)}, u32[]{:S(2)}, u32[]{:S(2)}) collective-permute-start(bf16[112,576]{1,0:T(8,128)(2,1)} %get-tuple-element.245), channel_id=1, source_target_pairs={{0,2},{1,3},{2,0},{3,1},{4,6},{5,7},{6,4},{7,5},{8,10},{9,11},{10,... | collective-permute-start | bytes 387080 | tf_op jit(solution)/shard_map/ppermute | solution.py:691
  12.0 8.4 %collective-permute-start.1 = (bf16[112,576]{1,0:T(8,128)(2,1)}, bf16[112,576]{1,0:T(8,128)(2,1)S(1)}, u32[]{:S(2)}, u32[]{:S(2)}) collective-permute-start(bf16[112,576]{1,0:T(8,128)(2,1)} %get-tuple-element.245), channel_id=1, source_target_pairs={{0,4},{1,5},{2,6},{3,7},{4,0},{5,1},{6,2},{7,3},{8,12},{9,13},{10,... | collective-permute-start | bytes 387080 | tf_op jit(solution)/shard_map/ppermute | solution.py:691
  13.5 6.9 %collective-permute-start.2 = (bf16[112,576]{1,0:T(8,128)(2,1)}, bf16[112,576]{1,0:T(8,128)(2,1)S(1)}, u32[]{:S(2)}, u32[]{:S(2)}) collective-permute-start(bf16[112,576]{1,0:T(8,128)(2,1)} %get-tuple-element.245), channel_id=1, source_target_pairs={{0,6},{1,7},{2,4},{3,5},{4,2},{5,3},{6,0},{7,1},{8,14},{9,15},{10,... | collective-permute-start | bytes 387080 | tf_op jit(solution)/shard_map/ppermute | solution.py:691
  27.9 17.9 %collective-permute-start.7 = (bf16[1,96,3968]{2,1,0:T(8,128)(2,1)}, bf16[1,96,3968]{2,1,0:T(8,128)(2,1)}, u32[]{:S(2)}, u32[]{:S(2)}) collective-permute-start(bf16[1,96,3968]{2,1,0:T(8,128)(2,1)} %maximum_bitcast_fusion), channel_id=1, source_target_pairs={{0,2},{1,3},{2,0},{3,1},{4,6},{5,7},{6,4},{7,5},{8,10},{9,11},{10,... | collective-permute-start | bytes 2285576 | tf_op jit(solution)/shard_map/ppermute | solution.py:691
  29.4 13.6 %collective-permute-start.8 = (bf16[1,384,768]{2,1,0:T(8,128)(2,1)S(1)}, bf16[1,384,768]{2,1,0:T(8,128)(2,1)S(1)}, u32[]{:S(2)}, u32[]{:S(2)}) collective-permute-start(bf16[1,384,768]{2,1,0:T(8,128)(2,1)S(1)} %bitcast.62), channel_id=1, source_target_pairs={{0,4},{1,5},{2,6},{3,7},{4,0},{5,1},{6,2},{7,3},{8,12},{9,13},{10,... | collective-permute-start | bytes 1769480 | tf_op jit(solution)/shard_map/ppermute | solution.py:691
  30.9 17.9 %collective-permute-start.5 = (bf16[512,768]{1,0:T(8,128)(2,1)}, bf16[512,768]{1,0:T(8,128)(2,1)}, u32[]{:S(2)}, u32[]{:S(2)}) collective-permute-start(bf16[512,768]{1,0:T(8,128)(2,1)} %collective-permute-done.3), channel_id=1, source_target_pairs={{0,8},{8,16},{16,24},{1,9},{9,17},{17,25},{2,10},{10,18},{18,26},{... | collective-permute-start | bytes 2359304 | tf_op jit(solution)/shard_map/ppermute | solution.py:687
  34.4 19.4 %collective-permute-start.6 = (bf16[512,768]{1,0:T(8,128)(2,1)}, bf16[512,768]{1,0:T(8,128)(2,1)}, u32[]{:S(2)}, u32[]{:S(2)}) collective-permute-start(bf16[512,768]{1,0:T(8,128)(2,1)} %collective-permute-done.4), channel_id=1, source_target_pairs={{8,0},{16,8},{24,16},{9,1},{17,9},{25,17},{10,2},{18,10},{26,18},{... | collective-permute-start | bytes 2359304 | tf_op jit(solution)/shard_map/ppermute | solution.py:687
  35.8 12.6 %collective-permute-start.9 = (bf16[4,112,576]{2,1,0:T(8,128)(2,1)S(1)}, bf16[4,112,576]{2,1,0:T(8,128)(2,1)S(1)}, u32[]{:S(2)}, u32[]{:S(2)}) collective-permute-start(bf16[4,112,576]{2,1,0:T(8,128)(2,1)S(1)} %pad_maximum_fusion.11.refs_0_), channel_id=1, source_target_pairs={{0,1},{1,0},{2,3},{3,2},{4,5},{5,4},{6,7},{7,6},{8,9},{9,8},{10,11... | collective-permute-start | bytes 1548296 | tf_op jit(solution)/shard_map/ppermute | solution.py:691
  43.1 33.2 %copy-start.12 = (bf16[2,384,768]{2,1,0:T(8,128)(2,1)}, bf16[2,384,768]{2,1,0:T(8,128)(2,1)S(1)}, u32[]{:S(2)}) copy-start(bf16[2,384,768]{2,1,0:T(8,128)(2,1)S(1)} %pad_maximum_fusion.7.refs_13_) | copy-start | bytes 3538948
  43.1 21.3 %copy-start.13 = (bf16[1,512,768]{2,1,0:T(8,128)(2,1)S(1)}, bf16[1,512,768]{2,1,0:T(8,128)(2,1)}, u32[]{:S(2)}) copy-start(bf16[1,512,768]{2,1,0:T(8,128)(2,1)} %param.17) | copy-start | bytes 2359300
  53.8 27.4 %collective-permute-start.12 = (bf16[2,96,3968]{2,1,0:T(8,128)(2,1)}, bf16[2,96,3968]{2,1,0:T(8,128)(2,1)}, u32[]{:S(2)}, u32[]{:S(2)}) collective-permute-start(bf16[2,96,3968]{2,1,0:T(8,128)(2,1)} %pad_maximum_fusion.refs_9_), channel_id=1, source_target_pairs={{0,1},{1,0},{2,3},{3,2},{4,5},{5,4},{6,7},{7,6},{8,9},{9,8},{10,11... | collective-permute-start | bytes 4571144 | tf_op jit(solution)/shard_map/ppermute | solution.py:691
  53.8 52.3 %collective-permute-start.15 = (bf16[2,96,3968]{2,1,0:T(8,128)(2,1)}, bf16[2,96,3968]{2,1,0:T(8,128)(2,1)}, u32[]{:S(2)}, u32[]{:S(2)}) collective-permute-start(bf16[2,96,3968]{2,1,0:T(8,128)(2,1)} %pad_maximum_fusion.refs_9_), channel_id=1, source_target_pairs={{0,4},{1,5},{2,6},{3,7},{4,0},{5,1},{6,2},{7,3},{8,12},{9,13},{10,... | collective-permute-start | bytes 4571144 | tf_op jit(solution)/shard_map/ppermute | solution.py:691
  54.4 21.9 %collective-permute-start.10 = (bf16[512,768]{1,0:T(8,128)(2,1)}, bf16[512,768]{1,0:T(8,128)(2,1)}, u32[]{:S(2)}, u32[]{:S(2)}) collective-permute-start(bf16[512,768]{1,0:T(8,128)(2,1)} %collective-permute-done.6), channel_id=1, source_target_pairs={{8,0},{16,8},{24,16},{9,1},{17,9},{25,17},{10,2},{18,10},{26,18},{... | collective-permute-start | bytes 2359304 | tf_op jit(solution)/shard_map/ppermute | solution.py:687
  55.6 22.3 %collective-permute-start.11 = (bf16[512,768]{1,0:T(8,128)(2,1)}, bf16[512,768]{1,0:T(8,128)(2,1)}, u32[]{:S(2)}, u32[]{:S(2)}) collective-permute-start(bf16[512,768]{1,0:T(8,128)(2,1)} %collective-permute-done.5), channel_id=1, source_target_pairs={{0,8},{8,16},{16,24},{1,9},{9,17},{17,25},{2,10},{10,18},{18,26},{... | collective-permute-start | bytes 2359304 | tf_op jit(solution)/shard_map/ppermute | solution.py:687
  61.3 19.9 %collective-permute-start.13 = (bf16[2,384,768]{2,1,0:T(8,128)(2,1)S(1)}, bf16[2,384,768]{2,1,0:T(8,128)(2,1)}, u32[]{:S(2)}, u32[]{:S(2)}) collective-permute-start(bf16[2,384,768]{2,1,0:T(8,128)(2,1)S(1)} %pad_maximum_fusion.7.refs_13_), channel_id=1, source_target_pairs={{0,1},{1,0},{2,3},{3,2},{4,5},{5,4},{6,7},{7,6},{8,9},{9,8},{10,11... | collective-permute-start | bytes 3538952 | tf_op jit(solution)/shard_map/ppermute | solution.py:691
  66.4 33.3 %copy-start = (bf16[512,576]{1,0:T(8,128)(2,1)}, bf16[512,576]{1,0:T(8,128)(2,1)S(1)}, u32[]{:S(2)}) copy-start(bf16[512,576]{1,0:T(8,128)(2,1)S(1)} %fusion.4.refs_0_) | copy-start | bytes 1769476
  69.0 30.8 %copy-start.1 = (bf16[512,576]{1,0:T(8,128)(2,1)}, bf16[512,576]{1,0:T(8,128)(2,1)S(1)}, u32[]{:S(2)}) copy-start(bf16[512,576]{1,0:T(8,128)(2,1)S(1)} %fusion.1.refs_2_) | copy-start | bytes 1769476
  76.2 30.0 %collective-permute-start.16 = (bf16[2,384,768]{2,1,0:T(8,128)(2,1)S(1)}, bf16[2,384,768]{2,1,0:T(8,128)(2,1)S(1)}, u32[]{:S(2)}, u32[]{:S(2)}) collective-permute-start(bf16[2,384,768]{2,1,0:T(8,128)(2,1)S(1)} %pad_maximum_fusion.7.refs_13_), channel_id=1, source_target_pairs={{0,2},{1,3},{2,0},{3,1},{4,6},{5,7},{6,4},{7,5},{8,10},{9,11},{10,... | collective-permute-start | bytes 3538952 | tf_op jit(solution)/shard_map/ppermute | solution.py:691
  86.3 19.9 %collective-permute-start.17 = (bf16[512,192]{1,0:T(8,128)(2,1)S(1)}, bf16[512,192]{1,0:T(8,128)(2,1)S(1)}, u32[]{:S(2)}, u32[]{:S(2)}) collective-permute-start(bf16[512,192]{1,0:T(8,128)(2,1)S(1)} %get-tuple-element.393.refs_10_), channel_id=1, source_target_pairs={{0,16},{8,24},{16,0},{24,8},{1,17},{9,25},{17,1},{25,9},{2,18},{10... | collective-permute-start | bytes 589832 | tf_op jit(solution)/shard_map/ppermute | solution.py:682
  93.5 12.8 %collective-permute-start.18 = (bf16[512,192]{1,0:T(8,128)(2,1)S(1)}, bf16[512,192]{1,0:T(8,128)(2,1)S(1)}, u32[]{:S(2)}, u32[]{:S(2)}) collective-permute-start(bf16[512,192]{1,0:T(8,128)(2,1)S(1)} %get-tuple-element.394.refs_11_), channel_id=1, source_target_pairs={{0,8},{8,16},{16,24},{24,0},{1,9},{9,17},{17,25},{25,1},{2,10},{10... | collective-permute-start | bytes 589832 | tf_op jit(solution)/shard_map/ppermute | solution.py:682
  106.2 9.1 %collective-permute-start.19 = (bf16[2,96,3968]{2,1,0:T(8,128)(2,1)}, bf16[2,96,3968]{2,1,0:T(8,128)(2,1)S(1)}, u32[]{:S(2)}, u32[]{:S(2)}) collective-permute-start(bf16[2,96,3968]{2,1,0:T(8,128)(2,1)} %collective-permute-done.15.refs_10_), channel_id=1, source_target_pairs={{0,1},{1,0},{2,3},{3,2},{4,5},{5,4},{6,7},{7,6},{8,9},{9,8},{10,11... | collective-permute-start | bytes 4571144 | tf_op jit(solution)/shard_map/ppermute | solution.py:691
  106.3 9.0 %collective-permute-start.20 = (bf16[2,384,768]{2,1,0:T(8,128)(2,1)S(1)}, bf16[2,384,768]{2,1,0:T(8,128)(2,1)S(1)}, u32[]{:S(2)}, u32[]{:S(2)}) collective-permute-start(bf16[2,384,768]{2,1,0:T(8,128)(2,1)S(1)} %collective-permute-done.16.refs_14_), channel_id=1, source_target_pairs={{0,1},{1,0},{2,3},{3,2},{4,5},{5,4},{6,7},{7,6},{8,9},{9,8},{10,11... | collective-permute-start | bytes 3538952 | tf_op jit(solution)/shard_map/ppermute | solution.py:691
  106.8 8.5 %collective-permute-start.14 = (bf16[512,192]{1,0:T(8,128)(2,1)S(1)}, bf16[512,192]{1,0:T(8,128)(2,1)S(1)}, u32[]{:S(2)}, u32[]{:S(2)}) collective-permute-start(bf16[512,192]{1,0:T(8,128)(2,1)S(1)} %get-tuple-element.392.refs_9_), channel_id=1, source_target_pairs={{0,24},{8,0},{16,8},{24,16},{1,25},{9,1},{17,9},{25,17},{2,26},{10... | collective-permute-start | bytes 589832 | tf_op jit(solution)/shard_map/ppermute | solution.py:682
  116.0 31.2 %collective-permute-start.24 = (bf16[1,96,1728]{2,1,0:T(8,128)(2,1)}, bf16[1,96,1728]{2,1,0:T(8,128)(2,1)}, u32[]{:S(2)}, u32[]{:S(2)}) collective-permute-start(bf16[1,96,1728]{2,1,0:T(8,128)(2,1)} %bitcast.3), channel_id=1, source_target_pairs={{0,2},{1,3},{2,0},{3,1},{4,6},{5,7},{6,4},{7,5},{8,10},{9,11},{10,... | collective-permute-start | bytes 995336 | tf_op jit(solution)/shard_map/ppermute | solution.py:691
  148.4 22.1 %copy-start.18 = (bf16[2,96,1728]{2,1,0:T(8,128)(2,1)}, bf16[2,96,1728]{2,1,0:T(8,128)(2,1)S(1)}, u32[]{:S(2)}) copy-start(bf16[2,96,1728]{2,1,0:T(8,128)(2,1)S(1)} %pad_maximum_fusion.8.refs_12_) | copy-start | bytes 1990660
  148.4 22.0 %collective-permute-start.25 = (bf16[2,96,1728]{2,1,0:T(8,128)(2,1)S(1)}, bf16[2,96,1728]{2,1,0:T(8,128)(2,1)}, u32[]{:S(2)}, u32[]{:S(2)}) collective-permute-start(bf16[2,96,1728]{2,1,0:T(8,128)(2,1)S(1)} %pad_maximum_fusion.8.refs_12_), channel_id=1, source_target_pairs={{0,4},{1,5},{2,6},{3,7},{4,0},{5,1},{6,2},{7,3},{8,12},{9,13},{10,... | collective-permute-start | bytes 1990664 | tf_op jit(solution)/shard_map/ppermute | solution.py:691
  150.0 16.9 %collective-permute-start.21 = (bf16[512,192]{1,0:T(8,128)(2,1)S(1)}, bf16[512,192]{1,0:T(8,128)(2,1)S(1)}, u32[]{:S(2)}, u32[]{:S(2)}) collective-permute-start(bf16[512,192]{1,0:T(8,128)(2,1)S(1)} %copy-done.49), channel_id=1, source_target_pairs={{0,8},{8,16},{16,24},{24,0},{1,9},{9,17},{17,25},{25,1},{2,10},{10... | collective-permute-start | bytes 589832 | tf_op jit(solution)/shard_map/ppermute | solution.py:682
  151.1 19.3 %collective-permute-start.22 = (bf16[512,192]{1,0:T(8,128)(2,1)S(1)}, bf16[512,192]{1,0:T(8,128)(2,1)S(1)}, u32[]{:S(2)}, u32[]{:S(2)}) collective-permute-start(bf16[512,192]{1,0:T(8,128)(2,1)S(1)} %copy-done.48), channel_id=1, source_target_pairs={{0,16},{8,24},{16,0},{24,8},{1,17},{9,25},{17,1},{25,9},{2,18},{10... | collective-permute-start | bytes 589832 | tf_op jit(solution)/shard_map/ppermute | solution.py:682
  154.5 15.9 %collective-permute-start.23 = (bf16[512,192]{1,0:T(8,128)(2,1)S(1)}, bf16[512,192]{1,0:T(8,128)(2,1)S(1)}, u32[]{:S(2)}, u32[]{:S(2)}) collective-permute-start(bf16[512,192]{1,0:T(8,128)(2,1)S(1)} %copy-done.47), channel_id=1, source_target_pairs={{0,24},{8,0},{16,8},{24,16},{1,25},{9,1},{17,9},{25,17},{2,26},{10... | collective-permute-start | bytes 589832 | tf_op jit(solution)/shard_map/ppermute | solution.py:682
  170.4 14.5 %collective-permute-start.26 = (bf16[4,896,768]{2,1,0:T(8,128)(2,1)}, bf16[4,896,768]{2,1,0:T(8,128)(2,1)}, u32[]{:S(2)}, u32[]{:S(2)}) collective-permute-start(bf16[4,896,768]{2,1,0:T(8,128)(2,1)} %get-tuple-element.322), channel_id=1, source_target_pairs={{0,1},{1,0},{2,3},{3,2},{4,5},{5,4},{6,7},{7,6},{8,9},{9,8},{10,11... | collective-permute-start | bytes 16515080 | tf_op jit(solution)/shard_map/ppermute | solution.py:691
  170.5 21.9 %collective-permute-start.27 = (bf16[2,96,1728]{2,1,0:T(8,128)(2,1)S(1)}, bf16[2,96,1728]{2,1,0:T(8,128)(2,1)}, u32[]{:S(2)}, u32[]{:S(2)}) collective-permute-start(bf16[2,96,1728]{2,1,0:T(8,128)(2,1)S(1)} %pad_maximum_fusion.8.refs_12_), channel_id=1, source_target_pairs={{0,1},{1,0},{2,3},{3,2},{4,5},{5,4},{6,7},{7,6},{8,9},{9,8},{10,11... | collective-permute-start | bytes 1990664 | tf_op jit(solution)/shard_map/ppermute | solution.py:691
  171.0 21.5 %collective-permute-start.28 = (bf16[2,96,1728]{2,1,0:T(8,128)(2,1)}, bf16[2,96,1728]{2,1,0:T(8,128)(2,1)}, u32[]{:S(2)}, u32[]{:S(2)}) collective-permute-start(bf16[2,96,1728]{2,1,0:T(8,128)(2,1)} %collective-permute-done.25.refs_13_), channel_id=1, source_target_pairs={{0,1},{1,0},{2,3},{3,2},{4,5},{5,4},{6,7},{7,6},{8,9},{9,8},{10,11... | collective-permute-start | bytes 1990664 | tf_op jit(solution)/shard_map/ppermute | solution.py:691
  192.5 32.7 %collective-permute-start.29 = (bf16[2,448,768]{2,1,0:T(8,128)(2,1)}, bf16[2,448,768]{2,1,0:T(8,128)(2,1)}, u32[]{:S(2)}, u32[]{:S(2)}) collective-permute-start(bf16[2,448,768]{2,1,0:T(8,128)(2,1)} %get-tuple-element.352), channel_id=1, source_target_pairs={{0,2},{1,3},{2,0},{3,1},{4,6},{5,7},{6,4},{7,5},{8,10},{9,11},{10,... | collective-permute-start | bytes 4128776 | tf_op jit(solution)/shard_map/ppermute | solution.py:691
  194.0 32.3 %collective-permute-start.30 = (bf16[2,448,768]{2,1,0:T(8,128)(2,1)}, bf16[2,448,768]{2,1,0:T(8,128)(2,1)S(1)}, u32[]{:S(2)}, u32[]{:S(2)}) collective-permute-start(bf16[2,448,768]{2,1,0:T(8,128)(2,1)} %get-tuple-element.354), channel_id=1, source_target_pairs={{0,4},{1,5},{2,6},{3,7},{4,0},{5,1},{6,2},{7,3},{8,12},{9,13},{10,... | collective-permute-start | bytes 4128776 | tf_op jit(solution)/shard_map/ppermute | solution.py:691
  194.5 21.4 %collective-permute-start.31 = (bf16[512,192]{1,0:T(8,128)(2,1)}, bf16[512,192]{1,0:T(8,128)(2,1)}, u32[]{:S(2)}, u32[]{:S(2)}) collective-permute-start(bf16[512,192]{1,0:T(8,128)(2,1)} %get-tuple-element.408.refs_5_), channel_id=1, source_target_pairs={{0,24},{8,0},{16,8},{24,16},{1,25},{9,1},{17,9},{25,17},{2,26},{10... | collective-permute-start | bytes 589832 | tf_op jit(solution)/shard_map/ppermute | solution.py:682
  199.9 25.2 %collective-permute-start.32 = (bf16[512,192]{1,0:T(8,128)(2,1)}, bf16[512,192]{1,0:T(8,128)(2,1)}, u32[]{:S(2)}, u32[]{:S(2)}) collective-permute-start(bf16[512,192]{1,0:T(8,128)(2,1)} %get-tuple-element.409.refs_6_), channel_id=1, source_target_pairs={{0,16},{8,24},{16,0},{24,8},{1,17},{9,25},{17,1},{25,9},{2,18},{10... | collective-permute-start | bytes 589832 | tf_op jit(solution)/shard_map/ppermute | solution.py:682
  201.9 23.1 %collective-permute-start.33 = (bf16[512,192]{1,0:T(8,128)(2,1)}, bf16[512,192]{1,0:T(8,128)(2,1)}, u32[]{:S(2)}, u32[]{:S(2)}) collective-permute-start(bf16[512,192]{1,0:T(8,128)(2,1)} %get-tuple-element.410.refs_7_), channel_id=1, source_target_pairs={{0,8},{8,16},{16,24},{24,0},{1,9},{9,17},{17,25},{25,1},{2,10},{10... | collective-permute-start | bytes 589832 | tf_op jit(solution)/shard_map/ppermute | solution.py:682
  229.3 22.3 %collective-permute-start.38 = (bf16[448,768]{1,0:T(8,128)(2,1)S(1)}, bf16[448,768]{1,0:T(8,128)(2,1)S(1)}, u32[]{:S(2)}, u32[]{:S(2)}) collective-permute-start(bf16[448,768]{1,0:T(8,128)(2,1)S(1)} %get-tuple-element.406), channel_id=1, source_target_pairs={{0,2},{1,3},{2,0},{3,1},{4,6},{5,7},{6,4},{7,5},{8,10},{9,11},{10,... | collective-permute-start | bytes 2064392 | tf_op jit(solution)/shard_map/ppermute | solution.py:691
  229.9 21.9 %collective-permute-start.37 = (bf16[448,768]{1,0:T(8,128)(2,1)}, bf16[448,768]{1,0:T(8,128)(2,1)S(1)}, u32[]{:S(2)}, u32[]{:S(2)}) collective-permute-start(bf16[448,768]{1,0:T(8,128)(2,1)} %get-tuple-element.404), channel_id=1, source_target_pairs={{0,4},{1,5},{2,6},{3,7},{4,0},{5,1},{6,2},{7,3},{8,12},{9,13},{10,... | collective-permute-start | bytes 2064392 | tf_op jit(solution)/shard_map/ppermute | solution.py:691
  230.4 21.7 %collective-permute-start.34 = (bf16[512,192]{1,0:T(8,128)(2,1)}, bf16[512,192]{1,0:T(8,128)(2,1)S(1)}, u32[]{:S(2)}, u32[]{:S(2)}) collective-permute-start(bf16[512,192]{1,0:T(8,128)(2,1)} %get-tuple-element.412.refs_9_), channel_id=1, source_target_pairs={{0,24},{8,0},{16,8},{24,16},{1,25},{9,1},{17,9},{25,17},{2,26},{10... | collective-permute-start | bytes 589832 | tf_op jit(solution)/shard_map/ppermute | solution.py:682
  235.8 24.2 %collective-permute-start.35 = (bf16[512,192]{1,0:T(8,128)(2,1)}, bf16[512,192]{1,0:T(8,128)(2,1)S(1)}, u32[]{:S(2)}, u32[]{:S(2)}) collective-permute-start(bf16[512,192]{1,0:T(8,128)(2,1)} %get-tuple-element.413.refs_10_), channel_id=1, source_target_pairs={{0,16},{8,24},{16,0},{24,8},{1,17},{9,25},{17,1},{25,9},{2,18},{10... | collective-permute-start | bytes 589832 | tf_op jit(solution)/shard_map/ppermute | solution.py:682
  237.9 22.1 %collective-permute-start.36 = (bf16[512,192]{1,0:T(8,128)(2,1)}, bf16[512,192]{1,0:T(8,128)(2,1)}, u32[]{:S(2)}, u32[]{:S(2)}) collective-permute-start(bf16[512,192]{1,0:T(8,128)(2,1)} %get-tuple-element.414.refs_11_), channel_id=1, source_target_pairs={{0,8},{8,16},{16,24},{24,0},{1,9},{9,17},{17,25},{25,1},{2,10},{10... | collective-permute-start | bytes 589832 | tf_op jit(solution)/shard_map/ppermute | solution.py:682
  261.0 23.7 %collective-permute-start.39 = (bf16[2,224,768]{2,1,0:T(8,128)(2,1)S(1)}, bf16[2,224,768]{2,1,0:T(8,128)(2,1)S(1)}, u32[]{:S(2)}, u32[]{:S(2)}) collective-permute-start(bf16[2,224,768]{2,1,0:T(8,128)(2,1)S(1)} %pad_maximum_fusion.9), channel_id=1, source_target_pairs={{0,8},{8,0},{16,24},{24,16},{1,9},{9,1},{17,25},{25,17},{2,10},{10... | collective-permute-start | bytes 2064392 | tf_op jit(solution)/shard_map/ppermute | solution.py:732
  261.1 26.5 %collective-permute-start.40 = (bf16[512,192]{1,0:T(8,128)(2,1)}, bf16[512,192]{1,0:T(8,128)(2,1)S(1)}, u32[]{:S(2)}, u32[]{:S(2)}) collective-permute-start(bf16[512,192]{1,0:T(8,128)(2,1)} %get-tuple-element.416.refs_13_), channel_id=1, source_target_pairs={{0,24},{8,0},{16,8},{24,16},{1,25},{9,1},{17,9},{25,17},{2,26},{10... | collective-permute-start | bytes 589832 | tf_op jit(solution)/shard_map/ppermute | solution.py:682
  262.8 25.5 %collective-permute-start.41 = (bf16[512,192]{1,0:T(8,128)(2,1)}, bf16[512,192]{1,0:T(8,128)(2,1)S(1)}, u32[]{:S(2)}, u32[]{:S(2)}) collective-permute-start(bf16[512,192]{1,0:T(8,128)(2,1)} %get-tuple-element.417.refs_14_), channel_id=1, source_target_pairs={{0,16},{8,24},{16,0},{24,8},{1,17},{9,25},{17,1},{25,9},{2,18},{10... | collective-permute-start | bytes 589832 | tf_op jit(solution)/shard_map/ppermute | solution.py:682
  264.5 30.4 %collective-permute-start.42 = (bf16[512,192]{1,0:T(8,128)(2,1)S(1)}, bf16[512,192]{1,0:T(8,128)(2,1)S(1)}, u32[]{:S(2)}, u32[]{:S(2)}) collective-permute-start(bf16[512,192]{1,0:T(8,128)(2,1)S(1)} %copy-done.37), channel_id=1, source_target_pairs={{0,8},{8,16},{16,24},{24,0},{1,9},{9,17},{17,25},{25,1},{2,10},{10... | collective-permute-start | bytes 589832 | tf_op jit(solution)/shard_map/ppermute | solution.py:682
  271.8 23.1 %copy-start.46 = (bf16[4,112,576]{2,1,0:T(8,128)(2,1)S(1)}, bf16[4,112,576]{2,1,0:T(8,128)(2,1)}, u32[]{:S(2)}) copy-start(bf16[4,112,576]{2,1,0:T(8,128)(2,1)} %get-tuple-element.424) | copy-start | bytes 1548292
  271.8 25.1 %copy-start.34 = (bf16[4,112,576]{2,1,0:T(8,128)(2,1)S(1)}, bf16[4,112,576]{2,1,0:T(8,128)(2,1)}, u32[]{:S(2)}) copy-start(bf16[4,112,576]{2,1,0:T(8,128)(2,1)} %get-tuple-element.423) | copy-start | bytes 1548292
  294.9 2.0 collective-permute-start.44
  297.1 8.9 %collective-permute-start.45 = (bf16[2,112,576]{2,1,0:T(8,128)(2,1)S(1)}, bf16[2,112,576]{2,1,0:T(8,128)(2,1)S(1)}, u32[]{:S(2)}, u32[]{:S(2)}) collective-permute-start(bf16[2,112,576]{2,1,0:T(8,128)(2,1)S(1)} %slice.143), channel_id=1, source_target_pairs={{0,2},{1,3},{2,0},{3,1},{4,6},{5,7},{6,4},{7,5},{8,10},{9,11},{10,... | collective-permute-start | bytes 774152 | tf_op jit(solution)/shard_map/ppermute | solution.py:691
  298.5 16.2 %collective-permute-start.43 = (bf16[224,768]{1,0:T(8,128)(2,1)S(1)}, bf16[224,768]{1,0:T(8,128)(2,1)S(1)}, u32[]{:S(2)}, u32[]{:S(2)}) collective-permute-start(bf16[224,768]{1,0:T(8,128)(2,1)S(1)} %get-tuple-element.422), channel_id=1, source_target_pairs={{0,16},{8,24},{16,0},{24,8},{1,17},{9,25},{17,1},{25,9},{2,18},{10... | collective-permute-start | bytes 1032200 | tf_op jit(solution)/shard_map/ppermute | solution.py:732
  306.1 8.6 %collective-permute-start.46 = (bf16[112,576]{1,0:T(8,128)(2,1)S(1)}, bf16[112,576]{1,0:T(8,128)(2,1)S(1)}, u32[]{:S(2)}, u32[]{:S(2)}) collective-permute-start(bf16[112,576]{1,0:T(8,128)(2,1)S(1)} %slice_bitcast_fusion.8), channel_id=1, source_target_pairs={{0,4},{1,5},{2,6},{3,7},{4,0},{5,1},{6,2},{7,3},{8,12},{9,13},{10,... | collective-permute-start | bytes 387080 | tf_op jit(solution)/shard_map/ppermute | solution.py:691
  314.8 46.6 %copy-start.32 = (bf16[112,576]{1,0:T(8,128)(2,1)}, bf16[112,576]{1,0:T(8,128)(2,1)S(1)}, u32[]{:S(2)}) copy-start(bf16[112,576]{1,0:T(8,128)(2,1)S(1)} %fusion.7.refs_0_) | copy-start | bytes 387076
  314.8 20.1 %collective-permute-start.47 = (bf16[224,768]{1,0:T(8,128)(2,1)S(1)}, bf16[224,768]{1,0:T(8,128)(2,1)S(1)}, u32[]{:S(2)}, u32[]{:S(2)}) collective-permute-start(bf16[224,768]{1,0:T(8,128)(2,1)S(1)} %add_convert_fusion.13), channel_id=1, source_target_pairs={{0,16},{8,24},{16,0},{24,8},{1,17},{9,25},{17,1},{25,9},{2,18},{10... | collective-permute-start | bytes 1032200 | tf_op jit(solution)/shard_map/ppermute | solution.py:732
  314.9 23.0 %collective-permute-start.48 = (bf16[112,576]{1,0:T(8,128)(2,1)S(1)}, bf16[112,576]{1,0:T(8,128)(2,1)S(1)}, u32[]{:S(2)}, u32[]{:S(2)}) collective-permute-start(bf16[112,576]{1,0:T(8,128)(2,1)S(1)} %fusion.7.refs_0_), channel_id=1, source_target_pairs={{0,16},{8,24},{16,0},{24,8},{1,17},{9,25},{17,1},{25,9},{2,18},{10... | collective-permute-start | bytes 387080 | tf_op jit(solution)/shard_map/ppermute | solution.py:732
  335.0 29.6 %copy-start.17 = (bf16[2,224,768]{2,1,0:T(8,128)(2,1)}, bf16[2,224,768]{2,1,0:T(8,128)(2,1)S(1)}, u32[]{:S(2)}) copy-start(bf16[2,224,768]{2,1,0:T(8,128)(2,1)S(1)} %pad_maximum_fusion.10.near_ref) | copy-start | bytes 2064388
  337.9 23.5 %copy-start.42 = (bf16[112,576]{1,0:T(8,128)(2,1)}, bf16[112,576]{1,0:T(8,128)(2,1)S(1)}, u32[]{:S(2)}) copy-start(bf16[112,576]{1,0:T(8,128)(2,1)S(1)} %collective-permute-done.48.refs_1_) | copy-start | bytes 387076
  337.9 26.7 %collective-permute-start.51 = (bf16[2,224,768]{2,1,0:T(8,128)(2,1)S(1)}, bf16[2,224,768]{2,1,0:T(8,128)(2,1)S(1)}, u32[]{:S(2)}, u32[]{:S(2)}) collective-permute-start(bf16[2,224,768]{2,1,0:T(8,128)(2,1)S(1)} %pad_maximum_fusion.10.near_ref), channel_id=1, source_target_pairs={{0,8},{8,0},{16,24},{24,16},{1,9},{9,1},{17,25},{25,17},{2,10},{10... | collective-permute-start | bytes 2064392 | tf_op jit(solution)/shard_map/ppermute | solution.py:732
  337.9 21.4 %collective-permute-start.49 = (bf16[112,576]{1,0:T(8,128)(2,1)S(1)}, bf16[112,576]{1,0:T(8,128)(2,1)S(1)}, u32[]{:S(2)}, u32[]{:S(2)}) collective-permute-start(bf16[112,576]{1,0:T(8,128)(2,1)S(1)} %fusion.7.refs_0_), channel_id=1, source_target_pairs={{0,8},{8,0},{16,24},{24,16},{1,9},{9,1},{17,25},{25,17},{2,10},{10... | collective-permute-start | bytes 387080 | tf_op jit(solution)/shard_map/ppermute | solution.py:732
  340.0 21.5 %collective-permute-start.50 = (bf16[112,576]{1,0:T(8,128)(2,1)S(1)}, bf16[112,576]{1,0:T(8,128)(2,1)S(1)}, u32[]{:S(2)}, u32[]{:S(2)}) collective-permute-start(bf16[112,576]{1,0:T(8,128)(2,1)S(1)} %collective-permute-done.48.refs_1_), channel_id=1, source_target_pairs={{0,8},{8,0},{16,24},{24,16},{1,9},{9,1},{17,25},{25,17},{2,10},{10... | collective-permute-start | bytes 387080 | tf_op jit(solution)/shard_map/ppermute | solution.py:732
  (38 other events, 263.7 us)
where the time goes:
time: 372 us; the launch traced here: 369 us
  waiting for transfers between devices  136 us (37%)
  Pallas kernels  127 us (34%)
  starting transfers between devices  70.9 us (19%)
  other arithmetic  21.8 us (6%)
  local copies, waits for them, and re-layouts  6.95 us (2%)
  matrix products  4.32 us (1%)
    ppermute x7, waiting for transfers between devices, swap_seq(): lax.ppermute(v, 'seq', [(i, i ^ bits) for i in range(lax.axis_size('seq'))])  61.3 us
    pallas_call x3, Pallas kernels, attend_backward(): pl.pallas_call(functools.partial(attend_backward_kernel, parts, h), out_s...  41.2 us
    ppermute x15, waiting for transfers between devices, send(): lax.ppermute(v, 'seq', [(i, (i + shift) % parts) for i in range(parts)])  36.4 us
    pallas_call x1, Pallas kernels, feed_forward(): pl.pallas_call(functools.partial(ffn_kernel, parts, hidden // 2, wide_fro...  29.4 us
    ppermute x15, starting transfers between devices, send(): lax.ppermute(v, 'seq', [(i, (i + shift) % parts) for i in range(parts)])  29.3 us
    pallas_call x4, Pallas kernels, attend_forward(): pl.pallas_call(functools.partial(attend_forward_kernel, parts, block, hea...  20.4 us
    ppermute x6, waiting for transfers between devices, hop(): lax.ppermute(v, 'seq', [(i, i + step) for i in range(parts) if 0 <= i + s...  20.2 us
    ppermute x6, starting transfers between devices, hop(): lax.ppermute(v, 'seq', [(i, i + step) for i in range(parts) if 0 <= i + s...  19 us
  transfers between devices with their start and end apart: 52, of which 26 were waited for; matrix products, arithmetic and copies ran while one was open for 6% of the time, Pallas kernels for 34%

commit v1 on v0

--- a/solution.py
+++ b/solution.py
@@ -218,7 +218,7 @@
         total_ref[...] += dot(active, shrink_ref[pl.ds(at, step), :], NN)
         return carry
 
-    lax.fori_loop(0, chunks, forward, 0)
+    lax.fori_loop(0, chunks, forward, 0, unroll=True)
 
     normed_two, scale_two = standardize(total_ref[...])
     second_low = (normed_two * vec(6) + vec(7)).astype(bf16)
@@ -249,7 +249,7 @@
         total_ref[...] += dot(low, expand_ref[:, pl.ds(at, step)], NT)
         return carry
 
-    lax.fori_loop(0, chunks, backward, 0)
+    lax.fori_loop(0, chunks, backward, 0, unroll=True)
     for c in range(hidden // width):
         sums_ref[6 + c : 7 + c, :] = jnp.sum(
             lifted_ref[:, c * width : (c + 1) * width].astype(f32), axis=0, keepdims=True
@@ -282,7 +282,7 @@
     M = pl.BlockSpec(memory_space=pltpu.SMEM)
     S = jax.ShapeDtypeStruct
     return pl.pallas_call(
-        functools.partial(ffn_kernel, parts, hidden // 2, wide_from, shrink_from),
+        functools.partial(ffn_kernel, parts, hidden // 4, wide_from, shrink_from),
         out_shape=[
             S((tokens, emb), f32),
             S((tokens, width), f32),
@@ -575,14 +575,15 @@
 FOUR = (0, 2, 1, 3)
 
 
-def unpack_kernel(slabs, place_ref, turn_ref, near_ref, far_ref, *refs):
-    outs, all_ref = refs[:-1], refs[-1]
+def unpack_kernel(slabs, place_ref, turn_ref, *refs):
+    pairs, outs, all_ref = refs[:4], refs[4:-1], refs[-1]
     shrink_ref, expand_ref, mixer_ref, project_ref = outs[:4]
-    count, width = near_ref.shape[1:]
-    for i, k in enumerate(FOUR):
-        j = lax.bitwise_xor(place_ref[0], k)
-        piece = (near_ref, far_ref)[i // 2][i % 2]
-        all_ref[pl.ds(pl.multiple_of(j * count, count), count), :] = piece.astype(f32)
+    count, width = pairs[0].shape[1:]
+    for half in range(2):
+        for i, k in enumerate(FOUR):
+            at = (4 * half + lax.bitwise_xor(place_ref[0], k)) * count
+            piece = pairs[2 * half + i // 2][i % 2]
+            all_ref[pl.ds(pl.multiple_of(at, count), count), :] = piece.astype(f32)
     lines, emb = project_ref.shape
     at = shrink_ref.shape[0]
     shrink_ref[...] = all_ref[:at, :]
@@ -622,9 +623,9 @@
         ]
         + [S((lines,), f32)] * 6
         + [S((hlines,), f32)],
-        in_specs=[M, M, V, V],
+        in_specs=[M, M] + [V] * 4,
         out_specs=[V] * 11,
-        scratch_shapes=[pltpu.VMEM((4 * count, width), f32)],
+        scratch_shapes=[pltpu.VMEM((8 * count, width), f32)],
         cost_estimate=SHORT,
         name="unpack",
     )(place, turn, *pairs)
@@ -706,10 +707,13 @@
 def sum_dp_core(keep, other):
     half = keep.shape[1] // 32 * 16
     a, b = slice(0, half), slice(half, None)
-    pick = lambda rows, *slots: jnp.concatenate(
-        [add(keep[i : i + 1, rows], other[i : i + 1, rows]) for i in slots]
+    pick = lambda slots, rows: add(keep[slots, rows], other[slots, rows])
+    return (
+        pick(slice(0, 2), a),
+        pick(slice(2, 4), a),
+        pick(slice(0, 4, 2), b),
+        pick(slice(1, 4, 2), b),
     )
-    return (pick(a, 0, 1), pick(a, 2, 3), pick(b, 0, 2), pick(b, 1, 3))
 
 
 def sum_dp_first(sums):
@@ -814,17 +818,14 @@
         x_first, y_first = [(0, 2), (4, 6), (1, 3), (5, 7)], [(0, 4), (2, 6), (1, 5), (3, 7)]
         below, above = [rows, hop(rows, 1)], [rows, hop(rows, -1)]
         own = [own] + [swap(own, k) for k in (2, 4, 6)]
-        own, below[1], above[1], wide, shrink = lax.optimization_barrier(
-            (own, below[1], above[1], wide, shrink)
-        )
+        own, above[1], wide = together(own, above[1], wide)
+        below[1], shrink = together(below[1], shrink)
         below.append(hop(below[1], 1))
         above.append(hop(above[1], -1))
         own = jnp.stack(own)
         own = [own, swap(own, 1)]
         wide, shrink = double(wide, 2), double(shrink, 4)
-        below[2], above[2], wide, shrink, own = lax.optimization_barrier(
-            (below[2], above[2], wide, shrink, own)
-        )
+        above[2], wide, shrink, own = together(above[2], wide, shrink, own)
         below.append(hop(below[2], 1))
         above.append(hop(above[2], -1))
         w_wide = [wide, swap(wide, 4)]
@@ -860,17 +861,20 @@
     for i, r in enumerate(order):
         if i > 0:
             joined, mixed_own[order[i - 1]] = together(joined, mixed_own[order[i - 1]])
+        if fast and i == 3:
+            joined, arrived[order[0]], w_wide[1], w_shrink[1] = together(
+                joined, arrived[order[0]], w_wide[1], w_shrink[1]
+            )
+            late = [swap(w_wide[1], 1), swap(w_shrink[1], 1)]
         if fast and i == 0:
             early = [swap(w_wide[0], 1), swap(w_shrink[0], 1)]
             joined, early = together(joined, early)
         mixed_own[r], stats[r] = attend_forward(joined, r, heads)
         arrived[r] = send(mixed_own[r], -r)
     if fast:
-        w_wide[1], w_shrink[1], mixed_own[0], arrived[2], arrived[3] = lax.optimization_barrier(
-            (w_wide[1], w_shrink[1], mixed_own[0], arrived[2], arrived[3])
-        )
-        w_wide += [early[0], swap(w_wide[1], 1)]
-        w_shrink += [early[1], swap(w_shrink[1], 1)]
+        late, mixed_own[0], arrived = together(late, mixed_own[0], arrived)
+        w_wide += [early[0], late[0]]
+        w_shrink += [early[1], late[1]]
         rest, arrived, w_wide[3], w_shrink[3] = together(rest[None], arrived, w_wide[3], w_shrink[3])
         rest = double(rest, 2)
     results = feed_forward(
@@ -916,28 +920,30 @@
         inputs, batch, w_rest = together(inputs, batch, w_rest)
         batch = sum_dp_first(batch)
         backward(1, inputs)
-        batch, landed[0], backs[1] = together(batch, landed[0], backs[1])
+        inputs, landed[0], backs[1] = together(inputs, landed[0], backs[1])
+        backward(2, inputs)
+        batch, landed[1], backs = together(batch, landed[1], backs)
         batch = sum_dp_second(batch)
-        inputs, batch = together(inputs, batch)
+        backs, batch = together(backs, batch)
         batch = sum_dp_last(batch)
-        backward(2, inputs)
-        batch = jnp.concatenate([add(batch[0], batch[1]), add(batch[2], batch[3])])
-        backs, landed[1], batch = together(backs, landed[1], batch)
-        batch = sum_seq_first(batch)
         keep, give = triple_grads(turn, blocks, backs, dp)
         give, batch, landed[2] = together(give, batch, landed[2])
+        halves = [add(batch[0], batch[1]), add(batch[2], batch[3])]
+        halves = [sum_seq_first(v) for v in halves]
         last = add(keep, swap(give, 1))
         last = add(last[:2], swap(last[2:], 2))
         last = add(last[0], swap(last[1], 4))
-        batch = sum_seq_second(batch)
-        input_grad = input_gradient(turn, grad_resid_one, w_own, landed, w_rest, x_first)
-        batch, last, input_grad = together(batch, last, input_grad)
+        halves = [sum_seq_second(v) for v in halves]
+        halves[1], last = together(halves[1], last)
         last = [last, swap_seq(last, 2)]
-        both = jnp.stack([batch, swap_seq(batch, 2)])
-        both, last = together(both, last)
+        pairs = [jnp.stack([v, swap_seq(v, 2)]) for v in halves]
+        pairs[1], last = together(pairs[1], last)
         last += [swap_seq(v, 1) for v in last]
         r_triple, r_queries, r_values = unpack_triple(where, turn, last, heads)
-        outs = unpack(where, turn, [both, swap_seq(both, 1)], dp, hidden, emb)
+        pairs = [v for pair in pairs for v in (pair, swap_seq(pair, 1))]
+        input_grad = input_gradient(turn, grad_resid_one, w_own, landed, w_rest, x_first)
+        pairs, r_triple, input_grad = together(pairs, r_triple, input_grad)
+        outs = unpack(where, turn, pairs, dp, hidden, emb)
         r_shrink, r_expand, r_mixer, r_project = outs[:4]
         r_offset, r_gamma, r_beta, r_settle, r_gain, r_shift, r_lift = outs[4:]
     else:

time: 372 us -> 354 us (0.952)
  waiting for transfers between devices: 136 us -> 117 us
  starting transfers between devices: 70.9 us -> 76.1 us
    ppermute x7 -> x11, waiting for transfers between devices: 61.3 us -> 51.2 us  [swap_seq(): lax.ppermute(v, 'seq', [(i, i ^ bits) for i in range(lax.axis_size('seq'))])]
    ppermute x6, waiting for transfers between devices: 20.2 us -> 15 us  [hop(): lax.ppermute(v, 'seq', [(i, i + step) for i in range(parts) if 0 <= i + s...]
    ppermute x24, waiting for transfers between devices: 17.9 us -> 13.2 us  [swap(): lax.ppermute(v, 'dp', [(i, i ^ bits) for i in range(lax.axis_size('dp'))])]
    ppermute x7 -> x11, starting transfers between devices: 5.13 us -> 8.93 us  [swap_seq(): lax.ppermute(v, 'seq', [(i, i ^ bits) for i in range(lax.axis_size('seq'))])]
    convert_element_type x10 -> x11, other arithmetic: 7.65 us -> 9.84 us  [add(): return (a.astype(f32) + b.astype(f32)).astype(bf16)]
  transfers between devices with their start and end apart: 52 -> 56, of which waited for: 26 -> 24; matrix products, arithmetic and copies ran while one was open for 6% -> 6% of each run, Pallas kernels for 34% -> 35%
where the time goes in v1:
time: 354 us; the launch traced here: 351 us
  Pallas kernels  125 us (35%)
  waiting for transfers between devices  117 us (33%)
  starting transfers between devices  76.1 us (21%)
  other arithmetic  20.9 us (6%)
  local copies, waits for them, and re-layouts  5.5 us (2%)
  matrix products  4.32 us (1%)
    ppermute x11, waiting for transfers between devices, swap_seq(): lax.ppermute(v, 'seq', [(i, i ^ bits) for i in range(lax.axis_size('seq'))])  51.2 us
    pallas_call x3, Pallas kernels, attend_backward(): pl.pallas_call(functools.partial(attend_backward_kernel, parts, h), out_s...  41.2 us
    ppermute x15, waiting for transfers between devices, send(): lax.ppermute(v, 'seq', [(i, (i + shift) % parts) for i in range(parts)])  37.8 us
    ppermute x15, starting transfers between devices, send(): lax.ppermute(v, 'seq', [(i, (i + shift) % parts) for i in range(parts)])  27.9 us
    pallas_call x1, Pallas kernels, feed_forward(): pl.pallas_call(functools.partial(ffn_kernel, parts, hidden // 4, wide_fro...  27.2 us
    ppermute x6, starting transfers between devices, hop(): lax.ppermute(v, 'seq', [(i, i + step) for i in range(parts) if 0 <= i + s...  20.7 us
    pallas_call x4, Pallas kernels, attend_forward(): pl.pallas_call(functools.partial(attend_forward_kernel, parts, block, hea...  20.4 us
    ppermute x24, starting transfers between devices, swap(): lax.ppermute(v, 'dp', [(i, i ^ bits) for i in range(lax.axis_size('dp'))])  18.6 us
  transfers between devices with their start and end apart: 56, of which 24 were waited for; matrix products, arithmetic and copies ran while one was open for 6% of the time, Pallas kernels for 35%

profile of v1, /device:TPU:0, one launch (start us, length us, event | category | flops | bytes accessed | tf_op | source)
XLA Modules:
  0.0 350.9 jit_solution(6658084551321289663)
XLA Ops:
  0.7 1.4 collective-permute-start.3
  2.1 6.5 %collective-permute-start.6 = (bf16[512,768]{1,0:T(8,128)(2,1)}, bf16[512,768]{1,0:T(8,128)(2,1)}, u32[]{:S(2)}, u32[]{:S(2)}) collective-permute-start(bf16[512,768]{1,0:T(8,128)(2,1)} %bitcast.77), channel_id=1, source_target_pairs={{0,8},{8,16},{16,24},{1,9},{9,17},{17,25},{2,10},{10,18},{18,26},{... | collective-permute-start | bytes 2359304 | tf_op jit(solution)/shard_map/ppermute | solution.py:688
  8.6 2.5 prepare.1
  11.1 1.9 collective-permute-start
  13.1 1.5 collective-permute-start.1
  14.6 2.1 maximum_bitcast_fusion
  17.4 4.1 %collective-permute-done.1 = bf16[112,576]{1,0:T(8,128)(2,1)S(1)} collective-permute-done((bf16[112,576]{1,0:T(8,128)(2,1)}, bf16[112,576]{1,0:T(8,128)(2,1)S(1)}, u32[]{:S(2)}, u32[]{:S(2)}) %collective-permute-start.1) | collective-permute-done | bytes 129056 | tf_op jit(solution)/shard_map/ppermute | solution.py:692
  21.5 2.1 collective-permute-done.3
  23.6 1.6 collective-permute-start.5
  25.2 1.5 collective-permute-start.7
  28.0 5.7 %collective-permute-start.10 = (bf16[512,768]{1,0:T(8,128)(2,1)}, bf16[512,768]{1,0:T(8,128)(2,1)}, u32[]{:S(2)}, u32[]{:S(2)}) collective-permute-start(bf16[512,768]{1,0:T(8,128)(2,1)} %collective-permute-done.6), channel_id=1, source_target_pairs={{0,8},{8,16},{16,24},{1,9},{9,17},{17,25},{2,10},{10,18},{18,26},{... | collective-permute-start | bytes 2359304 | tf_op jit(solution)/shard_map/ppermute | solution.py:688
  33.9 5.2 %collective-permute-done.7 = bf16[1,384,768]{2,1,0:T(8,128)(2,1)S(1)} collective-permute-done((bf16[1,384,768]{2,1,0:T(8,128)(2,1)S(1)}, bf16[1,384,768]{2,1,0:T(8,128)(2,1)S(1)}, u32[]{:S(2)}, u32[]{:S(2)}) %collective-permute-start.7) | collective-permute-done | bytes 589856 | tf_op jit(solution)/shard_map/ppermute | solution.py:692
  39.3 2.8 collective-permute-done.5
  42.1 2.6 pad_maximum_fusion.refs_9_
  44.7 2.5 collective-permute-done.4
  49.5 2.3 assemble.1
  52.5 4.6 %collective-permute-start.11 = (bf16[512,768]{1,0:T(8,128)(2,1)}, bf16[512,768]{1,0:T(8,128)(2,1)S(1)}, u32[]{:S(2)}, u32[]{:S(2)}) collective-permute-start(bf16[512,768]{1,0:T(8,128)(2,1)} %collective-permute-done.10), channel_id=1, source_target_pairs={{0,8},{8,16},{16,24},{1,9},{9,17},{17,25},{2,10},{10,18},{18,26},{... | collective-permute-start | bytes 2359304 | tf_op jit(solution)/shard_map/ppermute | solution.py:688
  57.1 2.0 fusion.4.refs_0_
  59.1 1.5 broadcast_select_fusion.1.refs_2_
  61.7 8.1 %collective-permute-done.9 = bf16[512,768]{1,0:T(8,128)(2,1)} collective-permute-done((bf16[512,768]{1,0:T(8,128)(2,1)}, bf16[512,768]{1,0:T(8,128)(2,1)}, u32[]{:S(2)}, u32[]{:S(2)}) %collective-permute-start.9) | collective-permute-done | bytes 786464 | tf_op jit(solution)/shard_map/ppermute | solution.py:688
  72.3 2.3 collective-permute-done.11
  77.5 5.0 %attend_forward.4 = (bf16[512,192]{1,0:T(8,128)(2,1)S(1)}, f32[512,8]{1,0:T(8,128)S(1)}) custom-call(bf16[512,576]{1,0:T(8,128)(2,1)S(1)} %fusion.4.refs_0_, bf16[512,576]{1,0:T(8,128)(2,1)S(1)} %fusion.refs_1_, bf16[512,576]{1,0:T(8,128)(2,1)S(1)} %fusion.1.refs_2_, bf16[512,576]{1,0:T(8,128)(2,1)S(1)} %fusion.2.refs_3_), custom_call_target="tpu_custom_call" | custom-call | tf_op jit(solution)/shard_map/attend_forward/pallas_call | solution.py:53
  82.6 3.6 %collective-permute-start.14 = (bf16[512,192]{1,0:T(8,128)(2,1)S(1)}, bf16[512,192]{1,0:T(8,128)(2,1)S(1)}, u32[]{:S(2)}, u32[]{:S(2)}) collective-permute-start(bf16[512,192]{1,0:T(8,128)(2,1)S(1)} %get-tuple-element.423.refs_10_), channel_id=1, source_target_pairs={{0,16},{8,24},{16,0},{24,8},{1,17},{9,25},{17,1},{25,9},{2,18},{10... | collective-permute-start | bytes 589832 | tf_op jit(solution)/shard_map/ppermute | solution.py:683
  86.2 5.4 %attend_forward.5 = (bf16[512,192]{1,0:T(8,128)(2,1)S(1)}, f32[512,8]{1,0:T(8,128)S(1)}) custom-call(bf16[512,576]{1,0:T(8,128)(2,1)S(1)} %fusion.4.refs_0_, bf16[512,576]{1,0:T(8,128)(2,1)S(1)} %fusion.refs_1_, bf16[512,576]{1,0:T(8,128)(2,1)S(1)} %fusion.1.refs_2_, bf16[512,576]{1,0:T(8,128)(2,1)S(1)} %fusion.2.refs_3_), custom_call_target="tpu_custom_call" | custom-call | tf_op jit(solution)/shard_map/attend_forward/pallas_call | solution.py:53
  91.6 5.0 %attend_forward.6 = (bf16[512,192]{1,0:T(8,128)(2,1)S(1)}, f32[512,8]{1,0:T(8,128)S(1)}) custom-call(bf16[512,576]{1,0:T(8,128)(2,1)S(1)} %fusion.4.refs_0_, bf16[512,576]{1,0:T(8,128)(2,1)S(1)} %fusion.refs_1_, bf16[512,576]{1,0:T(8,128)(2,1)S(1)} %fusion.1.refs_2_, bf16[512,576]{1,0:T(8,128)(2,1)S(1)} %fusion.2.refs_3_), custom_call_target="tpu_custom_call" | custom-call | tf_op jit(solution)/shard_map/attend_forward/pallas_call | solution.py:53
  98.6 3.3 collective-permute-start.19
  102.0 5.0 %attend_forward.7 = (bf16[512,192]{1,0:T(8,128)(2,1)S(1)}, f32[512,8]{1,0:T(8,128)S(1)}) custom-call(bf16[512,576]{1,0:T(8,128)(2,1)S(1)} %fusion.4.refs_0_, bf16[512,576]{1,0:T(8,128)(2,1)S(1)} %fusion.refs_1_, bf16[512,576]{1,0:T(8,128)(2,1)S(1)} %fusion.1.refs_2_, bf16[512,576]{1,0:T(8,128)(2,1)S(1)} %fusion.2.refs_3_), custom_call_target="tpu_custom_call" | custom-call | tf_op jit(solution)/shard_map/attend_forward/pallas_call | solution.py:53
  108.7 5.4 %collective-permute-done.20.refs_4_.refs_3_ = bf16[512,192]{1,0:T(8,128)(2,1)S(1)} collective-permute-done((bf16[512,192]{1,0:T(8,128)(2,1)S(1)}, bf16[512,192]{1,0:T(8,128)(2,1)S(1)}, u32[]{:S(2)}, u32[]{:S(2)}) %collective-permute-start.20) | collective-permute-done | bytes 196640 | tf_op jit(solution)/shard_map/ppermute | solution.py:683
  114.7 1.5 collective-permute-start.24
  117.1 27.2 %feed_forward.1 = (f32[512,128]{1,0:T(8,128)}, f32[512,768]{1,0:T(8,128)}, bf16[512,768]{1,0:T(8,128)(2,1)}, bf16[512,3072]{1,0:T(8,128)(2,1)}, bf16[512,768]{1,...) custom-call(s32[1]{0:T(128)} %bitcast.place_ref, ...), custom_call_target="tpu_custom_call" | custom-call | tf_op jit(solution)/shard_map/feed_forward/pallas_call | solution.py:284
  145.6 1.6 collective-permute-start.25
  147.2 1.8 collective-permute-start.21
  149.5 1.9 collective-permute-start.23
  151.4 11.9 %weight_grads.1 = (bf16[4,896,768]{2,1,0:T(8,128)(2,1)}, bf16[4,896,768]{2,1,0:T(8,128)(2,1)}) custom-call(s32[1]{0:T(128)} %bitcast.1.turn_ref, s32[1]{0:T(128)} %bitcast.place_ref, bf16[512,192]{1,0:T(8,128)(2,1)} %copy-done.4, bf16[512,192]{1,0:T(8,128)(2,1)} %copy-done.28, bf16[512,192]{1,0:T(8,128)(2,1)} %copy-done.27, bf16[512,192]{1,0:T(8,128)(2,1)} %copy-done.29, ...), custom_call_target="tpu_custom_call" | custom-call | tf_op jit(solution)/shard_map/weight_grads/pallas_call | solution.py:526
  163.4 4.1 %collective-permute-done.22.refs_6_ = bf16[512,192]{1,0:T(8,128)(2,1)S(1)} collective-permute-done((bf16[512,192]{1,0:T(8,128)(2,1)S(1)}, bf16[512,192]{1,0:T(8,128)(2,1)S(1)}, u32[]{:S(2)}, u32[]{:S(2)}) %collective-permute-start.22) | collective-permute-done | bytes 196640 | tf_op jit(solution)/shard_map/ppermute | solution.py:683
  168.3 13.7 %attend_backward.3 = (bf16[512,192]{1,0:T(8,128)(2,1)}, bf16[512,192]{1,0:T(8,128)(2,1)}, bf16[512,192]{1,0:T(8,128)(2,1)}, bf16[512,192]{1,0:T(8,128)(2,1)}) custom-call(bf16[512,576]{1,0:T(8,128)(2,1)} %copy-done, bf16[512,576]{1,0:T(8,128)(2,1)} %copy-done.2, bf16[512,576]{1,0:T(8,128)(2,1)} %copy-done.1, bf16[512,576]{1,0:T(8,128)(2,1)} %copy-done.3, ...), custom_call_target="tpu_custom_call" | custom-call | tf_op jit(solution)/shard_map/attend_backward/pallas_call | solution.py:113
  182.0 6.0 %add_convert_fusion.2 = (bf16[2,448,768]{2,1,0:T(8,128)(2,1)}, bf16[2,448,768]{2,1,0:T(8,128)(2,1)S(1)}, bf16[2,448,768]{2,1,0:T(8,128)(2,1)}, bf16[2,448,768]{2,1,0:T(8,128)(2,1)S(1)}) fusion(bf16[4,896,768]{2,1,0:T(8,128)(2,1)} %collective-permute-done.26, bf16[4,896,768]{2,1,0:T(8,128)(2,1)} %get-tuple-element.377), kind=kLoop, calls=%fused_computation.2 | loop fusion | flops 11010048 | bytes 16515072 | tf_op jit(solution)/shard_map/convert_element_type | solution.py:704
  189.1 5.8 %collective-permute-start.34 = (bf16[512,192]{1,0:T(8,128)(2,1)}, bf16[512,192]{1,0:T(8,128)(2,1)}, u32[]{:S(2)}, u32[]{:S(2)}) collective-permute-start(bf16[512,192]{1,0:T(8,128)(2,1)} %get-tuple-element.450.refs_5_), channel_id=1, source_target_pairs={{0,24},{8,0},{16,8},{24,16},{1,25},{9,1},{17,9},{25,17},{2,26},{10... | collective-permute-start | bytes 589832 | tf_op jit(solution)/shard_map/ppermute | solution.py:683
  194.9 1.7 collective-permute-start.35
  196.6 13.9 %attend_backward.4 = (bf16[512,192]{1,0:T(8,128)(2,1)}, bf16[512,192]{1,0:T(8,128)(2,1)}, bf16[512,192]{1,0:T(8,128)(2,1)}, bf16[512,192]{1,0:T(8,128)(2,1)}) custom-call(bf16[512,576]{1,0:T(8,128)(2,1)} %copy-done, bf16[512,576]{1,0:T(8,128)(2,1)} %copy-done.2, bf16[512,576]{1,0:T(8,128)(2,1)} %copy-done.1, bf16[512,576]{1,0:T(8,128)(2,1)} %copy-done.3, ...), custom_call_target="tpu_custom_call" | custom-call | tf_op jit(solution)/shard_map/attend_backward/pallas_call | solution.py:113
  210.5 3.9 %collective-permute-start.31 = (bf16[512,192]{1,0:T(8,128)(2,1)}, bf16[512,192]{1,0:T(8,128)(2,1)}, u32[]{:S(2)}, u32[]{:S(2)}) collective-permute-start(bf16[512,192]{1,0:T(8,128)(2,1)} %get-tuple-element.454.refs_9_), channel_id=1, source_target_pairs={{0,24},{8,0},{16,8},{24,16},{1,25},{9,1},{17,9},{25,17},{2,26},{10... | collective-permute-start | bytes 589832 | tf_op jit(solution)/shard_map/ppermute | solution.py:683
  214.4 15.0 %collective-permute-done.35.refs_2_ = bf16[512,192]{1,0:T(8,128)(2,1)} collective-permute-done((bf16[512,192]{1,0:T(8,128)(2,1)}, bf16[512,192]{1,0:T(8,128)(2,1)}, u32[]{:S(2)}, u32[]{:S(2)}) %collective-permute-start.35) | collective-permute-done | bytes 196640 | tf_op jit(solution)/shard_map/ppermute | solution.py:683
  229.6 13.5 %attend_backward.5 = (bf16[512,192]{1,0:T(8,128)(2,1)}, bf16[512,192]{1,0:T(8,128)(2,1)}, bf16[512,192]{1,0:T(8,128)(2,1)}, bf16[512,192]{1,0:T(8,128)(2,1)}) custom-call(bf16[512,576]{1,0:T(8,128)(2,1)} %copy-done, bf16[512,576]{1,0:T(8,128)(2,1)} %copy-done.2, bf16[512,576]{1,0:T(8,128)(2,1)} %copy-done.1, bf16[512,576]{1,0:T(8,128)(2,1)} %copy-done.3, ...), custom_call_target="tpu_custom_call" | custom-call | tf_op jit(solution)/shard_map/attend_backward/pallas_call | solution.py:113
  243.1 2.0 add_convert_fusion
  245.3 1.6 collective-permute-start.37
  246.9 1.5 collective-permute-start.38
  248.4 3.8 %collective-permute-start.39 = (bf16[512,192]{1,0:T(8,128)(2,1)}, bf16[512,192]{1,0:T(8,128)(2,1)}, u32[]{:S(2)}, u32[]{:S(2)}) collective-permute-start(bf16[512,192]{1,0:T(8,128)(2,1)} %get-tuple-element.458.refs_13_), channel_id=1, source_target_pairs={{0,24},{8,0},{16,8},{24,16},{1,25},{9,1},{17,9},{25,17},{2,26},{10... | collective-permute-start | bytes 589832 | tf_op jit(solution)/shard_map/ppermute | solution.py:683
  253.6 7.0 %triple_grads.1 = (bf16[4,112,576]{2,1,0:T(8,128)(2,1)}, bf16[4,112,576]{2,1,0:T(8,128)(2,1)}) custom-call(s32[1]{0:T(128)} %bitcast.1.turn_ref, bf16[512,768]{1,0:T(8,128)(2,1)} %bitcast.79, bf16[512,768]{1,0:T(8,128)(2,1)} %copy-done.15, bf16[512,768]{1,0:T(8,128)(2,1)} %copy-done.14, bf16[512,768]{1,0:T(8,128)(2,1)} %copy-done.16, ...), custom_call_target="tpu_custom_call" | custom-call | tf_op jit(solution)/shard_map/triple_grads/pallas_call | solution.py:564
  260.6 11.3 %collective-permute-done.40.refs_10_ = bf16[512,192]{1,0:T(8,128)(2,1)} collective-permute-done((bf16[512,192]{1,0:T(8,128)(2,1)}, bf16[512,192]{1,0:T(8,128)(2,1)}, u32[]{:S(2)}, u32[]{:S(2)}) %collective-permute-start.40) | collective-permute-done | bytes 196640 | tf_op jit(solution)/shard_map/ppermute | solution.py:683
  274.6 1.4 collective-permute-start.46
  276.1 9.5 %collective-permute-done.42 = bf16[2,112,768]{2,1,0:T(8,128)(2,1)S(1)} collective-permute-done((bf16[2,112,768]{2,1,0:T(8,128)(2,1)S(1)}, bf16[2,112,768]{2,1,0:T(8,128)(2,1)S(1)}, u32[]{:S(2)}, u32[]{:S(2)}) %collective-permute-start.42) | collective-permute-done | bytes 344096 | tf_op jit(solution)/shard_map/ppermute | solution.py:736
  286.5 3.5 collective-permute-done.46
  290.0 2.2 collective-permute-start.47
  292.2 9.2 %collective-permute-done.43 = bf16[112,768]{1,0:T(8,128)(2,1)S(1)} collective-permute-done((bf16[112,768]{1,0:T(8,128)(2,1)S(1)}, bf16[112,768]{1,0:T(8,128)(2,1)S(1)}, u32[]{:S(2)}, u32[]{:S(2)}) %collective-permute-start.43) | collective-permute-done | bytes 172064 | tf_op jit(solution)/shard_map/ppermute | solution.py:736
  302.2 11.5 %collective-permute-done.47 = bf16[112,768]{1,0:T(8,128)(2,1)S(1)} collective-permute-done((bf16[112,768]{1,0:T(8,128)(2,1)S(1)}, bf16[112,768]{1,0:T(8,128)(2,1)S(1)}, u32[]{:S(2)}, u32[]{:S(2)}) %collective-permute-start.47) | collective-permute-done | bytes 172064 | tf_op jit(solution)/shard_map/ppermute | solution.py:736
  313.9 2.9 collective-permute-start.52
  317.5 3.6 %collective-permute-done.51 = bf16[112,768]{1,0:T(8,128)(2,1)S(1)} collective-permute-done((bf16[112,768]{1,0:T(8,128)(2,1)S(1)}, bf16[112,768]{1,0:T(8,128)(2,1)S(1)}, u32[]{:S(2)}, u32[]{:S(2)}) %collective-permute-start.51) | collective-permute-done | bytes 172064 | tf_op jit(solution)/shard_map/ppermute | solution.py:736
  321.2 1.5 collective-permute-done.52.refs_1_
  322.7 2.0 collective-permute-start.54
  324.8 6.9 %input_gradient.1 = f32[512,768]{1,0:T(8,128)} custom-call(s32[1]{0:T(128)} %bitcast.1.turn_ref, f32[512,768]{1,0:T(8,128)} %get-tuple-element.478.resid_ref, bf16[768,576]{1,0:T(8,128)(2,1)} %get-tuple-element.276.own_ref, bf16[512,192]{1,0:T(8,128)(2,1)} %get-tuple-element.479.refs_4_.refs_0_, bf16[512,192]{1,0:T(8,128)(2,1)} %collective-permute-done.34.refs_1_, ...), custom_call_target="tpu_custom_call" | custom-call | tf_op jit(solution)/shard_map/input_gradient/pallas_call | solution.py:422
  331.7 8.8 %collective-permute-done.54.refs_2_ = bf16[112,576]{1,0:T(8,128)(2,1)S(1)} collective-permute-done((bf16[112,576]{1,0:T(8,128)(2,1)S(1)}, bf16[112,576]{1,0:T(8,128)(2,1)S(1)}, u32[]{:S(2)}, u32[]{:S(2)}) %collective-permute-start.54) | collective-permute-done | bytes 129056 | tf_op jit(solution)/shard_map/ppermute | solution.py:736
  340.5 3.0 collective-permute-done.55.refs_3_
  344.1 2.5 unpack_triple.1
  347.5 3.1 unpack.1
  (195 shorter events, 29.2 us)
Async XLA Ops:
  0.6 24.6 %copy-start.31 = (bf16[384,768]{1,0:T(8,128)(2,1)S(1)}, bf16[384,768]{1,0:T(8,128)(2,1)}, u32[]{:S(2)}) copy-start(bf16[384,768]{1,0:T(8,128)(2,1)} %param.27) | copy-start | bytes 1769476
  0.7 22.9 %collective-permute-start.3 = (bf16[512,768]{1,0:T(8,128)(2,1)}, bf16[512,768]{1,0:T(8,128)(2,1)}, u32[]{:S(2)}, u32[]{:S(2)}) collective-permute-start(bf16[512,768]{1,0:T(8,128)(2,1)} %bitcast.76), channel_id=1, source_target_pairs={{8,0},{16,8},{24,16},{9,1},{17,9},{25,17},{10,2},{18,10},{26,18},{... | collective-permute-start | bytes 2359304 | tf_op jit(solution)/shard_map/ppermute | solution.py:688
  2.1 23.1 %collective-permute-start.6 = (bf16[512,768]{1,0:T(8,128)(2,1)}, bf16[512,768]{1,0:T(8,128)(2,1)}, u32[]{:S(2)}, u32[]{:S(2)}) collective-permute-start(bf16[512,768]{1,0:T(8,128)(2,1)} %bitcast.77), channel_id=1, source_target_pairs={{0,8},{8,16},{16,24},{1,9},{9,17},{17,25},{2,10},{10,18},{18,26},{... | collective-permute-start | bytes 2359304 | tf_op jit(solution)/shard_map/ppermute | solution.py:688
  11.1 22.6 %copy-start.37 = (bf16[112,576]{1,0:T(8,128)(2,1)S(1)}, bf16[112,576]{1,0:T(8,128)(2,1)}, u32[]{:S(2)}) copy-start(bf16[112,576]{1,0:T(8,128)(2,1)} %get-tuple-element.270) | copy-start | bytes 387076
  11.1 6.2 %collective-permute-start = (bf16[112,576]{1,0:T(8,128)(2,1)}, bf16[112,576]{1,0:T(8,128)(2,1)S(1)}, u32[]{:S(2)}, u32[]{:S(2)}) collective-permute-start(bf16[112,576]{1,0:T(8,128)(2,1)} %get-tuple-element.270), channel_id=1, source_target_pairs={{0,2},{1,3},{2,0},{3,1},{4,6},{5,7},{6,4},{7,5},{8,10},{9,11},{10,... | collective-permute-start | bytes 387080 | tf_op jit(solution)/shard_map/ppermute | solution.py:692
  13.1 8.4 %collective-permute-start.1 = (bf16[112,576]{1,0:T(8,128)(2,1)}, bf16[112,576]{1,0:T(8,128)(2,1)S(1)}, u32[]{:S(2)}, u32[]{:S(2)}) collective-permute-start(bf16[112,576]{1,0:T(8,128)(2,1)} %get-tuple-element.270), channel_id=1, source_target_pairs={{0,4},{1,5},{2,6},{3,7},{4,0},{5,1},{6,2},{7,3},{8,12},{9,13},{10,... | collective-permute-start | bytes 387080 | tf_op jit(solution)/shard_map/ppermute | solution.py:692
  14.6 6.9 %collective-permute-start.2 = (bf16[112,576]{1,0:T(8,128)(2,1)}, bf16[112,576]{1,0:T(8,128)(2,1)S(1)}, u32[]{:S(2)}, u32[]{:S(2)}) collective-permute-start(bf16[112,576]{1,0:T(8,128)(2,1)} %get-tuple-element.270), channel_id=1, source_target_pairs={{0,6},{1,7},{2,4},{3,5},{4,2},{5,3},{6,0},{7,1},{8,14},{9,15},{10,... | collective-permute-start | bytes 387080 | tf_op jit(solution)/shard_map/ppermute | solution.py:692
  23.6 18.5 %collective-permute-start.5 = (bf16[1,96,3968]{2,1,0:T(8,128)(2,1)}, bf16[1,96,3968]{2,1,0:T(8,128)(2,1)}, u32[]{:S(2)}, u32[]{:S(2)}) collective-permute-start(bf16[1,96,3968]{2,1,0:T(8,128)(2,1)} %maximum_bitcast_fusion), channel_id=1, source_target_pairs={{0,2},{1,3},{2,0},{3,1},{4,6},{5,7},{6,4},{7,5},{8,10},{9,11},{10,... | collective-permute-start | bytes 2285576 | tf_op jit(solution)/shard_map/ppermute | solution.py:692
  25.2 13.9 %collective-permute-start.7 = (bf16[1,384,768]{2,1,0:T(8,128)(2,1)S(1)}, bf16[1,384,768]{2,1,0:T(8,128)(2,1)S(1)}, u32[]{:S(2)}, u32[]{:S(2)}) collective-permute-start(bf16[1,384,768]{2,1,0:T(8,128)(2,1)S(1)} %bitcast.83), channel_id=1, source_target_pairs={{0,4},{1,5},{2,6},{3,7},{4,0},{5,1},{6,2},{7,3},{8,12},{9,13},{10,... | collective-permute-start | bytes 1769480 | tf_op jit(solution)/shard_map/ppermute | solution.py:692
  26.8 20.4 %collective-permute-start.4 = (bf16[512,768]{1,0:T(8,128)(2,1)}, bf16[512,768]{1,0:T(8,128)(2,1)}, u32[]{:S(2)}, u32[]{:S(2)}) collective-permute-start(bf16[512,768]{1,0:T(8,128)(2,1)} %collective-permute-done.3), channel_id=1, source_target_pairs={{8,0},{16,8},{24,16},{9,1},{17,9},{25,17},{10,2},{18,10},{26,18},{... | collective-permute-start | bytes 2359304 | tf_op jit(solution)/shard_map/ppermute | solution.py:688
  28.0 24.5 %collective-permute-start.10 = (bf16[512,768]{1,0:T(8,128)(2,1)}, bf16[512,768]{1,0:T(8,128)(2,1)}, u32[]{:S(2)}, u32[]{:S(2)}) collective-permute-start(bf16[512,768]{1,0:T(8,128)(2,1)} %collective-permute-done.6), channel_id=1, source_target_pairs={{0,8},{8,16},{16,24},{1,9},{9,17},{17,25},{2,10},{10,18},{18,26},{... | collective-permute-start | bytes 2359304 | tf_op jit(solution)/shard_map/ppermute | solution.py:688
  33.8 10.9 %collective-permute-start.8 = (bf16[4,112,576]{2,1,0:T(8,128)(2,1)S(1)}, bf16[4,112,576]{2,1,0:T(8,128)(2,1)S(1)}, u32[]{:S(2)}, u32[]{:S(2)}) collective-permute-start(bf16[4,112,576]{2,1,0:T(8,128)(2,1)S(1)} %pad_maximum_fusion.5.refs_0_), channel_id=1, source_target_pairs={{0,1},{1,0},{2,3},{3,2},{4,5},{5,4},{6,7},{7,6},{8,9},{9,8},{10,11... | collective-permute-start | bytes 1548296 | tf_op jit(solution)/shard_map/ppermute | solution.py:692
  39.3 30.5 %copy-start.12 = (bf16[2,384,768]{2,1,0:T(8,128)(2,1)}, bf16[2,384,768]{2,1,0:T(8,128)(2,1)S(1)}, u32[]{:S(2)}) copy-start(bf16[2,384,768]{2,1,0:T(8,128)(2,1)S(1)} %pad_maximum_fusion.1.refs_13_) | copy-start | bytes 3538948
  47.2 30.3 %collective-permute-start.12 = (bf16[2,96,3968]{2,1,0:T(8,128)(2,1)}, bf16[2,96,3968]{2,1,0:T(8,128)(2,1)}, u32[]{:S(2)}, u32[]{:S(2)}) collective-permute-start(bf16[2,96,3968]{2,1,0:T(8,128)(2,1)} %pad_maximum_fusion.refs_9_), channel_id=1, source_target_pairs={{0,1},{1,0},{2,3},{3,2},{4,5},{5,4},{6,7},{7,6},{8,9},{9,8},{10,11... | collective-permute-start | bytes 4571144 | tf_op jit(solution)/shard_map/ppermute | solution.py:692
  47.2 49.8 %collective-permute-start.15 = (bf16[2,96,3968]{2,1,0:T(8,128)(2,1)}, bf16[2,96,3968]{2,1,0:T(8,128)(2,1)}, u32[]{:S(2)}, u32[]{:S(2)}) collective-permute-start(bf16[2,96,3968]{2,1,0:T(8,128)(2,1)} %pad_maximum_fusion.refs_9_), channel_id=1, source_target_pairs={{0,4},{1,5},{2,6},{3,7},{4,0},{5,1},{6,2},{7,3},{8,12},{9,13},{10,... | collective-permute-start | bytes 4571144 | tf_op jit(solution)/shard_map/ppermute | solution.py:692
  47.9 21.9 %collective-permute-start.9 = (bf16[512,768]{1,0:T(8,128)(2,1)}, bf16[512,768]{1,0:T(8,128)(2,1)}, u32[]{:S(2)}, u32[]{:S(2)}) collective-permute-start(bf16[512,768]{1,0:T(8,128)(2,1)} %collective-permute-done.4), channel_id=1, source_target_pairs={{8,0},{16,8},{24,16},{9,1},{17,9},{25,17},{10,2},{18,10},{26,18},{... | collective-permute-start | bytes 2359304 | tf_op jit(solution)/shard_map/ppermute | solution.py:688
  49.2 28.4 %collective-permute-start.13 = (bf16[2,384,768]{2,1,0:T(8,128)(2,1)S(1)}, bf16[2,384,768]{2,1,0:T(8,128)(2,1)}, u32[]{:S(2)}, u32[]{:S(2)}) collective-permute-start(bf16[2,384,768]{2,1,0:T(8,128)(2,1)S(1)} %pad_maximum_fusion.1.refs_13_), channel_id=1, source_target_pairs={{0,1},{1,0},{2,3},{3,2},{4,5},{5,4},{6,7},{7,6},{8,9},{9,8},{10,11... | collective-permute-start | bytes 3538952 | tf_op jit(solution)/shard_map/ppermute | solution.py:692
  52.5 22.1 %collective-permute-start.11 = (bf16[512,768]{1,0:T(8,128)(2,1)}, bf16[512,768]{1,0:T(8,128)(2,1)S(1)}, u32[]{:S(2)}, u32[]{:S(2)}) collective-permute-start(bf16[512,768]{1,0:T(8,128)(2,1)} %collective-permute-done.10), channel_id=1, source_target_pairs={{0,8},{8,16},{16,24},{1,9},{9,17},{17,25},{2,10},{10,18},{18,26},{... | collective-permute-start | bytes 2359304 | tf_op jit(solution)/shard_map/ppermute | solution.py:688
  59.1 42.9 %copy-start = (bf16[512,576]{1,0:T(8,128)(2,1)}, bf16[512,576]{1,0:T(8,128)(2,1)S(1)}, u32[]{:S(2)}) copy-start(bf16[512,576]{1,0:T(8,128)(2,1)S(1)} %fusion.4.refs_0_) | copy-start | bytes 1769476
  61.6 40.3 %copy-start.1 = (bf16[512,576]{1,0:T(8,128)(2,1)}, bf16[512,576]{1,0:T(8,128)(2,1)S(1)}, u32[]{:S(2)}) copy-start(bf16[512,576]{1,0:T(8,128)(2,1)S(1)} %fusion.1.refs_2_) | copy-start | bytes 1769476
  69.7 27.3 %collective-permute-start.16 = (bf16[2,384,768]{2,1,0:T(8,128)(2,1)S(1)}, bf16[2,384,768]{2,1,0:T(8,128)(2,1)S(1)}, u32[]{:S(2)}, u32[]{:S(2)}) collective-permute-start(bf16[2,384,768]{2,1,0:T(8,128)(2,1)S(1)} %pad_maximum_fusion.1.refs_13_), channel_id=1, source_target_pairs={{0,2},{1,3},{2,0},{3,1},{4,6},{5,7},{6,4},{7,5},{8,10},{9,11},{10,... | collective-permute-start | bytes 3538952 | tf_op jit(solution)/shard_map/ppermute | solution.py:692
  76.7 25.2 %copy-start.2 = (bf16[512,576]{1,0:T(8,128)(2,1)}, bf16[512,576]{1,0:T(8,128)(2,1)S(1)}, u32[]{:S(2)}) copy-start(bf16[512,576]{1,0:T(8,128)(2,1)S(1)} %fusion.refs_1_) | copy-start | bytes 1769476
  77.5 24.4 %copy-start.3 = (bf16[512,576]{1,0:T(8,128)(2,1)}, bf16[512,576]{1,0:T(8,128)(2,1)S(1)}, u32[]{:S(2)}) copy-start(bf16[512,576]{1,0:T(8,128)(2,1)S(1)} %fusion.2.refs_3_) | copy-start | bytes 1769476
  82.6 15.5 %collective-permute-start.14 = (bf16[512,192]{1,0:T(8,128)(2,1)S(1)}, bf16[512,192]{1,0:T(8,128)(2,1)S(1)}, u32[]{:S(2)}, u32[]{:S(2)}) collective-permute-start(bf16[512,192]{1,0:T(8,128)(2,1)S(1)} %get-tuple-element.423.refs_10_), channel_id=1, source_target_pairs={{0,16},{8,24},{16,0},{24,8},{1,17},{9,25},{17,1},{25,9},{2,18},{10... | collective-permute-start | bytes 589832 | tf_op jit(solution)/shard_map/ppermute | solution.py:683
  98.1 15.9 %collective-permute-start.17 = (bf16[2,96,3968]{2,1,0:T(8,128)(2,1)}, bf16[2,96,3968]{2,1,0:T(8,128)(2,1)S(1)}, u32[]{:S(2)}, u32[]{:S(2)}) collective-permute-start(bf16[2,96,3968]{2,1,0:T(8,128)(2,1)} %collective-permute-done.15.refs_10_), channel_id=1, source_target_pairs={{0,1},{1,0},{2,3},{3,2},{4,5},{5,4},{6,7},{7,6},{8,9},{9,8},{10,11... | collective-permute-start | bytes 4571144 | tf_op jit(solution)/shard_map/ppermute | solution.py:692
  98.1 15.9 %collective-permute-start.18 = (bf16[2,384,768]{2,1,0:T(8,128)(2,1)S(1)}, bf16[2,384,768]{2,1,0:T(8,128)(2,1)S(1)}, u32[]{:S(2)}, u32[]{:S(2)}) collective-permute-start(bf16[2,384,768]{2,1,0:T(8,128)(2,1)S(1)} %collective-permute-done.16.refs_14_), channel_id=1, source_target_pairs={{0,1},{1,0},{2,3},{3,2},{4,5},{5,4},{6,7},{7,6},{8,9},{9,8},{10,11... | collective-permute-start | bytes 3538952 | tf_op jit(solution)/shard_map/ppermute | solution.py:692
  98.6 10.0 %collective-permute-start.19 = (bf16[512,192]{1,0:T(8,128)(2,1)S(1)}, bf16[512,192]{1,0:T(8,128)(2,1)S(1)}, u32[]{:S(2)}, u32[]{:S(2)}) collective-permute-start(bf16[512,192]{1,0:T(8,128)(2,1)S(1)} %get-tuple-element.422.refs_9_), channel_id=1, source_target_pairs={{0,24},{8,0},{16,8},{24,16},{1,25},{9,1},{17,9},{25,17},{2,26},{10... | collective-permute-start | bytes 589832 | tf_op jit(solution)/shard_map/ppermute | solution.py:683
  101.9 12.1 %collective-permute-start.20 = (bf16[512,192]{1,0:T(8,128)(2,1)S(1)}, bf16[512,192]{1,0:T(8,128)(2,1)S(1)}, u32[]{:S(2)}, u32[]{:S(2)}) collective-permute-start(bf16[512,192]{1,0:T(8,128)(2,1)S(1)} %get-tuple-element.424.refs_11_), channel_id=1, source_target_pairs={{0,8},{8,16},{16,24},{24,0},{1,9},{9,17},{17,25},{25,1},{2,10},{10... | collective-permute-start | bytes 589832 | tf_op jit(solution)/shard_map/ppermute | solution.py:683
  107.7 36.7 %copy-start.11 = (f32[512,8]{1,0:T(8,128)}, f32[512,8]{1,0:T(8,128)S(1)}, u32[]{:S(2)}) copy-start(f32[512,8]{1,0:T(8,128)S(1)} %get-tuple-element.425.refs_12_) | copy-start | bytes 49156
  114.7 29.6 %collective-permute-start.24 = (bf16[1,96,1728]{2,1,0:T(8,128)(2,1)}, bf16[1,96,1728]{2,1,0:T(8,128)(2,1)}, u32[]{:S(2)}, u32[]{:S(2)}) collective-permute-start(bf16[1,96,1728]{2,1,0:T(8,128)(2,1)} %bitcast.3), channel_id=1, source_target_pairs={{0,2},{1,3},{2,0},{3,1},{4,6},{5,7},{6,4},{7,5},{8,10},{9,11},{10,... | collective-permute-start | bytes 995336 | tf_op jit(solution)/shard_map/ppermute | solution.py:692
  145.6 21.9 %collective-permute-start.25 = (bf16[2,96,1728]{2,1,0:T(8,128)(2,1)S(1)}, bf16[2,96,1728]{2,1,0:T(8,128)(2,1)}, u32[]{:S(2)}, u32[]{:S(2)}) collective-permute-start(bf16[2,96,1728]{2,1,0:T(8,128)(2,1)S(1)} %pad_maximum_fusion.2.refs_12_), channel_id=1, source_target_pairs={{0,4},{1,5},{2,6},{3,7},{4,0},{5,1},{6,2},{7,3},{8,12},{9,13},{10,... | collective-permute-start | bytes 1990664 | tf_op jit(solution)/shard_map/ppermute | solution.py:692
  147.2 16.2 %collective-permute-start.21 = (bf16[512,192]{1,0:T(8,128)(2,1)S(1)}, bf16[512,192]{1,0:T(8,128)(2,1)S(1)}, u32[]{:S(2)}, u32[]{:S(2)}) collective-permute-start(bf16[512,192]{1,0:T(8,128)(2,1)S(1)} %copy-done.45), channel_id=1, source_target_pairs={{0,8},{8,16},{16,24},{24,0},{1,9},{9,17},{17,25},{25,1},{2,10},{10... | collective-permute-start | bytes 589832 | tf_op jit(solution)/shard_map/ppermute | solution.py:683
  149.0 18.5 %collective-permute-start.22 = (bf16[512,192]{1,0:T(8,128)(2,1)S(1)}, bf16[512,192]{1,0:T(8,128)(2,1)S(1)}, u32[]{:S(2)}, u32[]{:S(2)}) collective-permute-start(bf16[512,192]{1,0:T(8,128)(2,1)S(1)} %copy-done.44), channel_id=1, source_target_pairs={{0,16},{8,24},{16,0},{24,8},{1,17},{9,25},{17,1},{25,9},{2,18},{10... | collective-permute-start | bytes 589832 | tf_op jit(solution)/shard_map/ppermute | solution.py:683
  149.5 18.0 %collective-permute-start.23 = (bf16[512,192]{1,0:T(8,128)(2,1)S(1)}, bf16[512,192]{1,0:T(8,128)(2,1)S(1)}, u32[]{:S(2)}, u32[]{:S(2)}) collective-permute-start(bf16[512,192]{1,0:T(8,128)(2,1)S(1)} %copy-done.43), channel_id=1, source_target_pairs={{0,24},{8,0},{16,8},{24,16},{1,25},{9,1},{17,9},{25,17},{2,26},{10... | collective-permute-start | bytes 589832 | tf_op jit(solution)/shard_map/ppermute | solution.py:683
  167.5 14.5 %collective-permute-start.26 = (bf16[4,896,768]{2,1,0:T(8,128)(2,1)}, bf16[4,896,768]{2,1,0:T(8,128)(2,1)}, u32[]{:S(2)}, u32[]{:S(2)}) collective-permute-start(bf16[4,896,768]{2,1,0:T(8,128)(2,1)} %get-tuple-element.372), channel_id=1, source_target_pairs={{0,1},{1,0},{2,3},{3,2},{4,5},{5,4},{6,7},{7,6},{8,9},{9,8},{10,11... | collective-permute-start | bytes 16515080 | tf_op jit(solution)/shard_map/ppermute | solution.py:692
  167.6 20.4 %collective-permute-start.27 = (bf16[2,96,1728]{2,1,0:T(8,128)(2,1)S(1)}, bf16[2,96,1728]{2,1,0:T(8,128)(2,1)}, u32[]{:S(2)}, u32[]{:S(2)}) collective-permute-start(bf16[2,96,1728]{2,1,0:T(8,128)(2,1)S(1)} %pad_maximum_fusion.2.refs_12_), channel_id=1, source_target_pairs={{0,1},{1,0},{2,3},{3,2},{4,5},{5,4},{6,7},{7,6},{8,9},{9,8},{10,11... | collective-permute-start | bytes 1990664 | tf_op jit(solution)/shard_map/ppermute | solution.py:692
  168.1 19.9 %collective-permute-start.28 = (bf16[2,96,1728]{2,1,0:T(8,128)(2,1)}, bf16[2,96,1728]{2,1,0:T(8,128)(2,1)}, u32[]{:S(2)}, u32[]{:S(2)}) collective-permute-start(bf16[2,96,1728]{2,1,0:T(8,128)(2,1)} %collective-permute-done.25.refs_13_), channel_id=1, source_target_pairs={{0,1},{1,0},{2,3},{3,2},{4,5},{5,4},{6,7},{7,6},{8,9},{9,8},{10,11... | collective-permute-start | bytes 1990664 | tf_op jit(solution)/shard_map/ppermute | solution.py:692
  188.0 55.1 %collective-permute-start.29 = (bf16[2,448,768]{2,1,0:T(8,128)(2,1)}, bf16[2,448,768]{2,1,0:T(8,128)(2,1)S(1)}, u32[]{:S(2)}, u32[]{:S(2)}) collective-permute-start(bf16[2,448,768]{2,1,0:T(8,128)(2,1)} %get-tuple-element.382), channel_id=1, source_target_pairs={{0,2},{1,3},{2,0},{3,1},{4,6},{5,7},{6,4},{7,5},{8,10},{9,11},{10,... | collective-permute-start | bytes 4128776 | tf_op jit(solution)/shard_map/ppermute | solution.py:692
  188.6 54.5 %collective-permute-start.30 = (bf16[2,448,768]{2,1,0:T(8,128)(2,1)}, bf16[2,448,768]{2,1,0:T(8,128)(2,1)}, u32[]{:S(2)}, u32[]{:S(2)}) collective-permute-start(bf16[2,448,768]{2,1,0:T(8,128)(2,1)} %get-tuple-element.384), channel_id=1, source_target_pairs={{0,4},{1,5},{2,6},{3,7},{4,0},{5,1},{6,2},{7,3},{8,12},{9,13},{10,... | collective-permute-start | bytes 4128776 | tf_op jit(solution)/shard_map/ppermute | solution.py:692
  189.1 21.4 %collective-permute-start.34 = (bf16[512,192]{1,0:T(8,128)(2,1)}, bf16[512,192]{1,0:T(8,128)(2,1)}, u32[]{:S(2)}, u32[]{:S(2)}) collective-permute-start(bf16[512,192]{1,0:T(8,128)(2,1)} %get-tuple-element.450.refs_5_), channel_id=1, source_target_pairs={{0,24},{8,0},{16,8},{24,16},{1,25},{9,1},{17,9},{25,17},{2,26},{10... | collective-permute-start | bytes 589832 | tf_op jit(solution)/shard_map/ppermute | solution.py:683
  194.9 34.5 %collective-permute-start.35 = (bf16[512,192]{1,0:T(8,128)(2,1)}, bf16[512,192]{1,0:T(8,128)(2,1)}, u32[]{:S(2)}, u32[]{:S(2)}) collective-permute-start(bf16[512,192]{1,0:T(8,128)(2,1)} %get-tuple-element.451.refs_6_), channel_id=1, source_target_pairs={{0,16},{8,24},{16,0},{24,8},{1,17},{9,25},{17,1},{25,9},{2,18},{10... | collective-permute-start | bytes 589832 | tf_op jit(solution)/shard_map/ppermute | solution.py:683
  196.6 32.8 %collective-permute-start.36 = (bf16[512,192]{1,0:T(8,128)(2,1)}, bf16[512,192]{1,0:T(8,128)(2,1)}, u32[]{:S(2)}, u32[]{:S(2)}) collective-permute-start(bf16[512,192]{1,0:T(8,128)(2,1)} %get-tuple-element.452.refs_7_), channel_id=1, source_target_pairs={{0,8},{8,16},{16,24},{24,0},{1,9},{9,17},{17,25},{25,1},{2,10},{10... | collective-permute-start | bytes 589832 | tf_op jit(solution)/shard_map/ppermute | solution.py:683
  210.5 32.6 %collective-permute-start.31 = (bf16[512,192]{1,0:T(8,128)(2,1)}, bf16[512,192]{1,0:T(8,128)(2,1)}, u32[]{:S(2)}, u32[]{:S(2)}) collective-permute-start(bf16[512,192]{1,0:T(8,128)(2,1)} %get-tuple-element.454.refs_9_), channel_id=1, source_target_pairs={{0,24},{8,0},{16,8},{24,16},{1,25},{9,1},{17,9},{25,17},{2,26},{10... | collective-permute-start | bytes 589832 | tf_op jit(solution)/shard_map/ppermute | solution.py:683
  229.3 13.7 %collective-permute-start.32 = (bf16[512,192]{1,0:T(8,128)(2,1)}, bf16[512,192]{1,0:T(8,128)(2,1)}, u32[]{:S(2)}, u32[]{:S(2)}) collective-permute-start(bf16[512,192]{1,0:T(8,128)(2,1)} %get-tuple-element.455.refs_10_), channel_id=1, source_target_pairs={{0,16},{8,24},{16,0},{24,8},{1,17},{9,25},{17,1},{25,9},{2,18},{10... | collective-permute-start | bytes 589832 | tf_op jit(solution)/shard_map/ppermute | solution.py:683
  229.4 13.8 %collective-permute-start.33 = (bf16[512,192]{1,0:T(8,128)(2,1)}, bf16[512,192]{1,0:T(8,128)(2,1)}, u32[]{:S(2)}, u32[]{:S(2)}) collective-permute-start(bf16[512,192]{1,0:T(8,128)(2,1)} %get-tuple-element.456.refs_11_), channel_id=1, source_target_pairs={{0,8},{8,16},{16,24},{24,0},{1,9},{9,17},{17,25},{25,1},{2,10},{10... | collective-permute-start | bytes 589832 | tf_op jit(solution)/shard_map/ppermute | solution.py:683
  245.3 26.6 %collective-permute-start.37 = (bf16[448,768]{1,0:T(8,128)(2,1)S(1)}, bf16[448,768]{1,0:T(8,128)(2,1)}, u32[]{:S(2)}, u32[]{:S(2)}) collective-permute-start(bf16[448,768]{1,0:T(8,128)(2,1)S(1)} %get-tuple-element.463), channel_id=1, source_target_pairs={{0,4},{1,5},{2,6},{3,7},{4,0},{5,1},{6,2},{7,3},{8,12},{9,13},{10,... | collective-permute-start | bytes 2064392 | tf_op jit(solution)/shard_map/ppermute | solution.py:692
  246.9 25.0 %collective-permute-start.38 = (bf16[448,768]{1,0:T(8,128)(2,1)S(1)}, bf16[448,768]{1,0:T(8,128)(2,1)S(1)}, u32[]{:S(2)}, u32[]{:S(2)}) collective-permute-start(bf16[448,768]{1,0:T(8,128)(2,1)S(1)} %get-tuple-element.465), channel_id=1, source_target_pairs={{0,2},{1,3},{2,0},{3,1},{4,6},{5,7},{6,4},{7,5},{8,10},{9,11},{10,... | collective-permute-start | bytes 2064392 | tf_op jit(solution)/shard_map/ppermute | solution.py:692
  248.4 12.2 %collective-permute-start.39 = (bf16[512,192]{1,0:T(8,128)(2,1)}, bf16[512,192]{1,0:T(8,128)(2,1)}, u32[]{:S(2)}, u32[]{:S(2)}) collective-permute-start(bf16[512,192]{1,0:T(8,128)(2,1)} %get-tuple-element.458.refs_13_), channel_id=1, source_target_pairs={{0,24},{8,0},{16,8},{24,16},{1,25},{9,1},{17,9},{25,17},{2,26},{10... | collective-permute-start | bytes 589832 | tf_op jit(solution)/shard_map/ppermute | solution.py:683
  252.2 19.7 %collective-permute-start.40 = (bf16[512,192]{1,0:T(8,128)(2,1)}, bf16[512,192]{1,0:T(8,128)(2,1)}, u32[]{:S(2)}, u32[]{:S(2)}) collective-permute-start(bf16[512,192]{1,0:T(8,128)(2,1)} %get-tuple-element.459.refs_14_), channel_id=1, source_target_pairs={{0,16},{8,24},{16,0},{24,8},{1,17},{9,25},{17,1},{25,9},{2,18},{10... | collective-permute-start | bytes 589832 | tf_op jit(solution)/shard_map/ppermute | solution.py:683
  253.3 18.6 %collective-permute-start.41 = (bf16[512,192]{1,0:T(8,128)(2,1)}, bf16[512,192]{1,0:T(8,128)(2,1)}, u32[]{:S(2)}, u32[]{:S(2)}) collective-permute-start(bf16[512,192]{1,0:T(8,128)(2,1)} %get-tuple-element.460.refs_15_), channel_id=1, source_target_pairs={{0,8},{8,16},{16,24},{24,0},{1,9},{9,17},{17,25},{25,1},{2,10},{10... | collective-permute-start | bytes 589832 | tf_op jit(solution)/shard_map/ppermute | solution.py:683
  273.4 12.1 %collective-permute-start.42 = (bf16[2,112,768]{2,1,0:T(8,128)(2,1)S(1)}, bf16[2,112,768]{2,1,0:T(8,128)(2,1)S(1)}, u32[]{:S(2)}, u32[]{:S(2)}) collective-permute-start(bf16[2,112,768]{2,1,0:T(8,128)(2,1)S(1)} %pad_maximum_fusion.6), channel_id=1, source_target_pairs={{0,8},{8,0},{16,24},{24,16},{1,9},{9,1},{17,25},{25,17},{2,10},{10... | collective-permute-start | bytes 1032200 | tf_op jit(solution)/shard_map/ppermute | solution.py:736
  274.5 11.2 %collective-permute-start.48 = (bf16[4,112,576]{2,1,0:T(8,128)(2,1)S(1)}, bf16[4,112,576]{2,1,0:T(8,128)(2,1)S(1)}, u32[]{:S(2)}, u32[]{:S(2)}) collective-permute-start(bf16[4,112,576]{2,1,0:T(8,128)(2,1)S(1)} %copy-done.42), channel_id=1, source_target_pairs={{0,1},{1,0},{2,3},{3,2},{4,5},{5,4},{6,7},{7,6},{8,9},{9,8},{10,11... | collective-permute-start | bytes 1548296 | tf_op jit(solution)/shard_map/ppermute | solution.py:692
  274.6 15.3 %collective-permute-start.46 = (bf16[2,112,768]{2,1,0:T(8,128)(2,1)S(1)}, bf16[2,112,768]{2,1,0:T(8,128)(2,1)S(1)}, u32[]{:S(2)}, u32[]{:S(2)}) collective-permute-start(bf16[2,112,768]{2,1,0:T(8,128)(2,1)S(1)} %pad_maximum_fusion.8), channel_id=1, source_target_pairs={{0,8},{8,0},{16,24},{24,16},{1,9},{9,1},{17,25},{25,17},{2,10},{10... | collective-permute-start | bytes 1032200 | tf_op jit(solution)/shard_map/ppermute | solution.py:736
  285.6 15.8 %collective-permute-start.43 = (bf16[112,768]{1,0:T(8,128)(2,1)S(1)}, bf16[112,768]{1,0:T(8,128)(2,1)S(1)}, u32[]{:S(2)}, u32[]{:S(2)}) collective-permute-start(bf16[112,768]{1,0:T(8,128)(2,1)S(1)} %fusion.9), channel_id=1, source_target_pairs={{0,16},{8,24},{16,0},{24,8},{1,17},{9,25},{17,1},{25,9},{2,18},{10... | collective-permute-start | bytes 516104 | tf_op jit(solution)/shard_map/ppermute | solution.py:736
  285.9 15.7 %collective-permute-start.49 = (bf16[2,112,576]{2,1,0:T(8,128)(2,1)S(1)}, bf16[2,112,576]{2,1,0:T(8,128)(2,1)S(1)}, u32[]{:S(2)}, u32[]{:S(2)}) collective-permute-start(bf16[2,112,576]{2,1,0:T(8,128)(2,1)S(1)} %slice.161), channel_id=1, source_target_pairs={{0,2},{1,3},{2,0},{3,1},{4,6},{5,7},{6,4},{7,5},{8,10},{9,11},{10,... | collective-permute-start | bytes 774152 | tf_op jit(solution)/shard_map/ppermute | solution.py:692
  290.0 23.7 %collective-permute-start.47 = (bf16[112,768]{1,0:T(8,128)(2,1)S(1)}, bf16[112,768]{1,0:T(8,128)(2,1)S(1)}, u32[]{:S(2)}, u32[]{:S(2)}) collective-permute-start(bf16[112,768]{1,0:T(8,128)(2,1)S(1)} %fusion.11), channel_id=1, source_target_pairs={{0,16},{8,24},{16,0},{24,8},{1,17},{9,25},{17,1},{25,9},{2,18},{10... | collective-permute-start | bytes 516104 | tf_op jit(solution)/shard_map/ppermute | solution.py:736
  301.5 15.9 %collective-permute-start.44 = (bf16[112,768]{1,0:T(8,128)(2,1)S(1)}, bf16[112,768]{1,0:T(8,128)(2,1)S(1)}, u32[]{:S(2)}, u32[]{:S(2)}) collective-permute-start(bf16[112,768]{1,0:T(8,128)(2,1)S(1)} %fusion.6), channel_id=1, source_target_pairs={{0,16},{8,24},{16,0},{24,8},{1,17},{9,25},{17,1},{25,9},{2,18},{10... | collective-permute-start | bytes 516104 | tf_op jit(solution)/shard_map/ppermute | solution.py:736
  301.7 12.1 %collective-permute-start.50 = (bf16[112,576]{1,0:T(8,128)(2,1)S(1)}, bf16[112,576]{1,0:T(8,128)(2,1)S(1)}, u32[]{:S(2)}, u32[]{:S(2)}) collective-permute-start(bf16[112,576]{1,0:T(8,128)(2,1)S(1)} %slice_bitcast_fusion.12), channel_id=1, source_target_pairs={{0,4},{1,5},{2,6},{3,7},{4,0},{5,1},{6,2},{7,3},{8,12},{9,13},{10,... | collective-permute-start | bytes 387080 | tf_op jit(solution)/shard_map/ppermute | solution.py:692
  313.8 7.3 %collective-permute-start.51 = (bf16[112,768]{1,0:T(8,128)(2,1)S(1)}, bf16[112,768]{1,0:T(8,128)(2,1)S(1)}, u32[]{:S(2)}, u32[]{:S(2)}) collective-permute-start(bf16[112,768]{1,0:T(8,128)(2,1)S(1)} %fusion.5), channel_id=1, source_target_pairs={{0,16},{8,24},{16,0},{24,8},{1,17},{9,25},{17,1},{25,9},{2,18},{10... | collective-permute-start | bytes 516104 | tf_op jit(solution)/shard_map/ppermute | solution.py:736
  313.9 8.8 %collective-permute-start.52 = (bf16[112,576]{1,0:T(8,128)(2,1)S(1)}, bf16[112,576]{1,0:T(8,128)(2,1)S(1)}, u32[]{:S(2)}, u32[]{:S(2)}) collective-permute-start(bf16[112,576]{1,0:T(8,128)(2,1)S(1)} %fusion.7.refs_0_), channel_id=1, source_target_pairs={{0,16},{8,24},{16,0},{24,8},{1,17},{9,25},{17,1},{25,9},{2,18},{10... | collective-permute-start | bytes 387080 | tf_op jit(solution)/shard_map/ppermute | solution.py:736
  317.4 29.2 %collective-permute-start.45 = (bf16[2,112,768]{2,1,0:T(8,128)(2,1)S(1)}, bf16[2,112,768]{2,1,0:T(8,128)(2,1)S(1)}, u32[]{:S(2)}, u32[]{:S(2)}) collective-permute-start(bf16[2,112,768]{2,1,0:T(8,128)(2,1)S(1)} %pad_maximum_fusion.7.refs_0_), channel_id=1, source_target_pairs={{0,8},{8,0},{16,24},{24,16},{1,9},{9,1},{17,25},{25,17},{2,10},{10... | collective-permute-start | bytes 1032200 | tf_op jit(solution)/shard_map/ppermute | solution.py:736
  322.7 24.0 %collective-permute-start.53 = (bf16[2,112,768]{2,1,0:T(8,128)(2,1)S(1)}, bf16[2,112,768]{2,1,0:T(8,128)(2,1)S(1)}, u32[]{:S(2)}, u32[]{:S(2)}) collective-permute-start(bf16[2,112,768]{2,1,0:T(8,128)(2,1)S(1)} %pad_maximum_fusion.9.refs_2_), channel_id=1, source_target_pairs={{0,8},{8,0},{16,24},{24,16},{1,9},{9,1},{17,25},{25,17},{2,10},{10... | collective-permute-start | bytes 1032200 | tf_op jit(solution)/shard_map/ppermute | solution.py:736
  322.7 17.8 %collective-permute-start.54 = (bf16[112,576]{1,0:T(8,128)(2,1)S(1)}, bf16[112,576]{1,0:T(8,128)(2,1)S(1)}, u32[]{:S(2)}, u32[]{:S(2)}) collective-permute-start(bf16[112,576]{1,0:T(8,128)(2,1)S(1)} %fusion.7.refs_0_), channel_id=1, source_target_pairs={{0,8},{8,0},{16,24},{24,16},{1,9},{9,1},{17,25},{25,17},{2,10},{10... | collective-permute-start | bytes 387080 | tf_op jit(solution)/shard_map/ppermute | solution.py:736
  324.7 18.8 %collective-permute-start.55 = (bf16[112,576]{1,0:T(8,128)(2,1)S(1)}, bf16[112,576]{1,0:T(8,128)(2,1)S(1)}, u32[]{:S(2)}, u32[]{:S(2)}) collective-permute-start(bf16[112,576]{1,0:T(8,128)(2,1)S(1)} %collective-permute-done.52.refs_1_), channel_id=1, source_target_pairs={{0,8},{8,0},{16,24},{24,16},{1,9},{9,1},{17,25},{25,17},{2,10},{10... | collective-permute-start | bytes 387080 | tf_op jit(solution)/shard_map/ppermute | solution.py:736
  (38 other events, 314.8 us)

commit v2 on v1

--- a/solution.py
+++ b/solution.py
@@ -937,7 +937,7 @@
         halves[1], last = together(halves[1], last)
         last = [last, swap_seq(last, 2)]
         pairs = [jnp.stack([v, swap_seq(v, 2)]) for v in halves]
-        pairs[1], last = together(pairs[1], last)
+        pairs[0], last = together(pairs[0], last)
         last += [swap_seq(v, 1) for v in last]
         r_triple, r_queries, r_values = unpack_triple(where, turn, last, heads)
         pairs = [v for pair in pairs for v in (pair, swap_seq(pair, 1))]

time: 354 us -> 354 us (level)
  transfers between devices with their start and end apart: 56 -> 56, of which waited for: 24 -> 23; matrix products, arithmetic and copies ran while one was open for 6% -> 6% of each run, Pallas kernels for 35% -> 35%
where the time goes in v2:
time: 354 us; the launch traced here: 351 us
  Pallas kernels  125 us (35%)
  waiting for transfers between devices  115 us (32%)
  starting transfers between devices  78 us (22%)
  other arithmetic  20.9 us (6%)
  local copies, waits for them, and re-layouts  5.5 us (2%)
  matrix products  4.32 us (1%)
    ppermute x11, waiting for transfers between devices, swap_seq(): lax.ppermute(v, 'seq', [(i, i ^ bits) for i in range(lax.axis_size('seq'))])  49.3 us
    pallas_call x3, Pallas kernels, attend_backward(): pl.pallas_call(functools.partial(attend_backward_kernel, parts, h), out_s...  41.2 us
    ppermute x15, waiting for transfers between devices, send(): lax.ppermute(v, 'seq', [(i, (i + shift) % parts) for i in range(parts)])  37.8 us
    ppermute x15, starting transfers between devices, send(): lax.ppermute(v, 'seq', [(i, (i + shift) % parts) for i in range(parts)])  27.9 us
    pallas_call x1, Pallas kernels, feed_forward(): pl.pallas_call(functools.partial(ffn_kernel, parts, hidden // 4, wide_fro...  27.2 us
    ppermute x6, starting transfers between devices, hop(): lax.ppermute(v, 'seq', [(i, i + step) for i in range(parts) if 0 <= i + s...  20.7 us
    pallas_call x4, Pallas kernels, attend_forward(): pl.pallas_call(functools.partial(attend_forward_kernel, parts, block, hea...  20.4 us
    ppermute x24, starting transfers between devices, swap(): lax.ppermute(v, 'dp', [(i, i ^ bits) for i in range(lax.axis_size('dp'))])  18.6 us
  transfers between devices with their start and end apart: 56, of which 23 were waited for; matrix products, arithmetic and copies ran while one was open for 6% of the time, Pallas kernels for 35%

profile of v2, /device:TPU:0, one launch (start us, length us, event | category | flops | bytes accessed | tf_op | source)
XLA Modules:
  0.0 351.0 jit_solution(9850175347218570575)
XLA Ops:
  0.7 1.4 collective-permute-start.3
  2.1 6.5 %collective-permute-start.6 = (bf16[512,768]{1,0:T(8,128)(2,1)}, bf16[512,768]{1,0:T(8,128)(2,1)}, u32[]{:S(2)}, u32[]{:S(2)}) collective-permute-start(bf16[512,768]{1,0:T(8,128)(2,1)} %bitcast.77), channel_id=1, source_target_pairs={{0,8},{8,16},{16,24},{1,9},{9,17},{17,25},{2,10},{10,18},{18,26},{... | collective-permute-start | bytes 2359304 | tf_op jit(solution)/shard_map/ppermute | solution.py:688
  8.6 2.5 prepare.1
  11.1 1.9 collective-permute-start
  13.1 1.5 collective-permute-start.1
  14.6 2.1 maximum_bitcast_fusion
  17.4 4.1 %collective-permute-done.1 = bf16[112,576]{1,0:T(8,128)(2,1)S(1)} collective-permute-done((bf16[112,576]{1,0:T(8,128)(2,1)}, bf16[112,576]{1,0:T(8,128)(2,1)S(1)}, u32[]{:S(2)}, u32[]{:S(2)}) %collective-permute-start.1) | collective-permute-done | bytes 129056 | tf_op jit(solution)/shard_map/ppermute | solution.py:692
  21.5 2.1 collective-permute-done.3
  23.6 1.6 collective-permute-start.5
  25.2 1.5 collective-permute-start.7
  28.0 5.7 %collective-permute-start.10 = (bf16[512,768]{1,0:T(8,128)(2,1)}, bf16[512,768]{1,0:T(8,128)(2,1)}, u32[]{:S(2)}, u32[]{:S(2)}) collective-permute-start(bf16[512,768]{1,0:T(8,128)(2,1)} %collective-permute-done.6), channel_id=1, source_target_pairs={{0,8},{8,16},{16,24},{1,9},{9,17},{17,25},{2,10},{10,18},{18,26},{... | collective-permute-start | bytes 2359304 | tf_op jit(solution)/shard_map/ppermute | solution.py:688
  33.9 5.2 %collective-permute-done.7 = bf16[1,384,768]{2,1,0:T(8,128)(2,1)S(1)} collective-permute-done((bf16[1,384,768]{2,1,0:T(8,128)(2,1)S(1)}, bf16[1,384,768]{2,1,0:T(8,128)(2,1)S(1)}, u32[]{:S(2)}, u32[]{:S(2)}) %collective-permute-start.7) | collective-permute-done | bytes 589856 | tf_op jit(solution)/shard_map/ppermute | solution.py:692
  39.3 2.8 collective-permute-done.5
  42.1 2.6 pad_maximum_fusion.refs_9_
  44.7 2.5 collective-permute-done.4
  49.5 2.3 assemble.1
  52.5 4.6 %collective-permute-start.11 = (bf16[512,768]{1,0:T(8,128)(2,1)}, bf16[512,768]{1,0:T(8,128)(2,1)S(1)}, u32[]{:S(2)}, u32[]{:S(2)}) collective-permute-start(bf16[512,768]{1,0:T(8,128)(2,1)} %collective-permute-done.10), channel_id=1, source_target_pairs={{0,8},{8,16},{16,24},{1,9},{9,17},{17,25},{2,10},{10,18},{18,26},{... | collective-permute-start | bytes 2359304 | tf_op jit(solution)/shard_map/ppermute | solution.py:688
  57.1 2.0 fusion.4.refs_0_
  59.1 1.5 broadcast_select_fusion.1.refs_2_
  61.7 8.1 %collective-permute-done.9 = bf16[512,768]{1,0:T(8,128)(2,1)} collective-permute-done((bf16[512,768]{1,0:T(8,128)(2,1)}, bf16[512,768]{1,0:T(8,128)(2,1)}, u32[]{:S(2)}, u32[]{:S(2)}) %collective-permute-start.9) | collective-permute-done | bytes 786464 | tf_op jit(solution)/shard_map/ppermute | solution.py:688
  72.3 2.3 collective-permute-done.11
  77.5 5.0 %attend_forward.4 = (bf16[512,192]{1,0:T(8,128)(2,1)S(1)}, f32[512,8]{1,0:T(8,128)S(1)}) custom-call(bf16[512,576]{1,0:T(8,128)(2,1)S(1)} %fusion.4.refs_0_, bf16[512,576]{1,0:T(8,128)(2,1)S(1)} %fusion.refs_1_, bf16[512,576]{1,0:T(8,128)(2,1)S(1)} %fusion.1.refs_2_, bf16[512,576]{1,0:T(8,128)(2,1)S(1)} %fusion.2.refs_3_), custom_call_target="tpu_custom_call" | custom-call | tf_op jit(solution)/shard_map/attend_forward/pallas_call | solution.py:53
  82.6 3.6 %collective-permute-start.14 = (bf16[512,192]{1,0:T(8,128)(2,1)S(1)}, bf16[512,192]{1,0:T(8,128)(2,1)S(1)}, u32[]{:S(2)}, u32[]{:S(2)}) collective-permute-start(bf16[512,192]{1,0:T(8,128)(2,1)S(1)} %get-tuple-element.423.refs_10_), channel_id=1, source_target_pairs={{0,16},{8,24},{16,0},{24,8},{1,17},{9,25},{17,1},{25,9},{2,18},{10... | collective-permute-start | bytes 589832 | tf_op jit(solution)/shard_map/ppermute | solution.py:683
  86.2 5.4 %attend_forward.5 = (bf16[512,192]{1,0:T(8,128)(2,1)S(1)}, f32[512,8]{1,0:T(8,128)S(1)}) custom-call(bf16[512,576]{1,0:T(8,128)(2,1)S(1)} %fusion.4.refs_0_, bf16[512,576]{1,0:T(8,128)(2,1)S(1)} %fusion.refs_1_, bf16[512,576]{1,0:T(8,128)(2,1)S(1)} %fusion.1.refs_2_, bf16[512,576]{1,0:T(8,128)(2,1)S(1)} %fusion.2.refs_3_), custom_call_target="tpu_custom_call" | custom-call | tf_op jit(solution)/shard_map/attend_forward/pallas_call | solution.py:53
  91.6 5.0 %attend_forward.6 = (bf16[512,192]{1,0:T(8,128)(2,1)S(1)}, f32[512,8]{1,0:T(8,128)S(1)}) custom-call(bf16[512,576]{1,0:T(8,128)(2,1)S(1)} %fusion.4.refs_0_, bf16[512,576]{1,0:T(8,128)(2,1)S(1)} %fusion.refs_1_, bf16[512,576]{1,0:T(8,128)(2,1)S(1)} %fusion.1.refs_2_, bf16[512,576]{1,0:T(8,128)(2,1)S(1)} %fusion.2.refs_3_), custom_call_target="tpu_custom_call" | custom-call | tf_op jit(solution)/shard_map/attend_forward/pallas_call | solution.py:53
  98.6 3.3 collective-permute-start.19
  102.0 5.0 %attend_forward.7 = (bf16[512,192]{1,0:T(8,128)(2,1)S(1)}, f32[512,8]{1,0:T(8,128)S(1)}) custom-call(bf16[512,576]{1,0:T(8,128)(2,1)S(1)} %fusion.4.refs_0_, bf16[512,576]{1,0:T(8,128)(2,1)S(1)} %fusion.refs_1_, bf16[512,576]{1,0:T(8,128)(2,1)S(1)} %fusion.1.refs_2_, bf16[512,576]{1,0:T(8,128)(2,1)S(1)} %fusion.2.refs_3_), custom_call_target="tpu_custom_call" | custom-call | tf_op jit(solution)/shard_map/attend_forward/pallas_call | solution.py:53
  108.7 5.4 %collective-permute-done.20.refs_4_.refs_3_ = bf16[512,192]{1,0:T(8,128)(2,1)S(1)} collective-permute-done((bf16[512,192]{1,0:T(8,128)(2,1)S(1)}, bf16[512,192]{1,0:T(8,128)(2,1)S(1)}, u32[]{:S(2)}, u32[]{:S(2)}) %collective-permute-start.20) | collective-permute-done | bytes 196640 | tf_op jit(solution)/shard_map/ppermute | solution.py:683
  114.7 1.5 collective-permute-start.24
  117.1 27.2 %feed_forward.1 = (f32[512,128]{1,0:T(8,128)}, f32[512,768]{1,0:T(8,128)}, bf16[512,768]{1,0:T(8,128)(2,1)}, bf16[512,3072]{1,0:T(8,128)(2,1)}, bf16[512,768]{1,...) custom-call(s32[1]{0:T(128)} %bitcast.place_ref, ...), custom_call_target="tpu_custom_call" | custom-call | tf_op jit(solution)/shard_map/feed_forward/pallas_call | solution.py:284
  145.6 1.6 collective-permute-start.25
  147.2 1.8 collective-permute-start.21
  149.5 1.9 collective-permute-start.23
  151.4 11.9 %weight_grads.1 = (bf16[4,896,768]{2,1,0:T(8,128)(2,1)}, bf16[4,896,768]{2,1,0:T(8,128)(2,1)}) custom-call(s32[1]{0:T(128)} %bitcast.1.turn_ref, s32[1]{0:T(128)} %bitcast.place_ref, bf16[512,192]{1,0:T(8,128)(2,1)} %copy-done.4, bf16[512,192]{1,0:T(8,128)(2,1)} %copy-done.28, bf16[512,192]{1,0:T(8,128)(2,1)} %copy-done.27, bf16[512,192]{1,0:T(8,128)(2,1)} %copy-done.29, ...), custom_call_target="tpu_custom_call" | custom-call | tf_op jit(solution)/shard_map/weight_grads/pallas_call | solution.py:526
  163.4 4.1 %collective-permute-done.22.refs_6_ = bf16[512,192]{1,0:T(8,128)(2,1)S(1)} collective-permute-done((bf16[512,192]{1,0:T(8,128)(2,1)S(1)}, bf16[512,192]{1,0:T(8,128)(2,1)S(1)}, u32[]{:S(2)}, u32[]{:S(2)}) %collective-permute-start.22) | collective-permute-done | bytes 196640 | tf_op jit(solution)/shard_map/ppermute | solution.py:683
  168.3 13.7 %attend_backward.3 = (bf16[512,192]{1,0:T(8,128)(2,1)}, bf16[512,192]{1,0:T(8,128)(2,1)}, bf16[512,192]{1,0:T(8,128)(2,1)}, bf16[512,192]{1,0:T(8,128)(2,1)}) custom-call(bf16[512,576]{1,0:T(8,128)(2,1)} %copy-done, bf16[512,576]{1,0:T(8,128)(2,1)} %copy-done.2, bf16[512,576]{1,0:T(8,128)(2,1)} %copy-done.1, bf16[512,576]{1,0:T(8,128)(2,1)} %copy-done.3, ...), custom_call_target="tpu_custom_call" | custom-call | tf_op jit(solution)/shard_map/attend_backward/pallas_call | solution.py:113
  182.0 6.0 %add_convert_fusion.2 = (bf16[2,448,768]{2,1,0:T(8,128)(2,1)}, bf16[2,448,768]{2,1,0:T(8,128)(2,1)S(1)}, bf16[2,448,768]{2,1,0:T(8,128)(2,1)}, bf16[2,448,768]{2,1,0:T(8,128)(2,1)S(1)}) fusion(bf16[4,896,768]{2,1,0:T(8,128)(2,1)} %collective-permute-done.26, bf16[4,896,768]{2,1,0:T(8,128)(2,1)} %get-tuple-element.377), kind=kLoop, calls=%fused_computation.2 | loop fusion | flops 11010048 | bytes 16515072 | tf_op jit(solution)/shard_map/convert_element_type | solution.py:704
  189.1 5.8 %collective-permute-start.34 = (bf16[512,192]{1,0:T(8,128)(2,1)}, bf16[512,192]{1,0:T(8,128)(2,1)}, u32[]{:S(2)}, u32[]{:S(2)}) collective-permute-start(bf16[512,192]{1,0:T(8,128)(2,1)} %get-tuple-element.450.refs_5_), channel_id=1, source_target_pairs={{0,24},{8,0},{16,8},{24,16},{1,25},{9,1},{17,9},{25,17},{2,26},{10... | collective-permute-start | bytes 589832 | tf_op jit(solution)/shard_map/ppermute | solution.py:683
  194.9 1.7 collective-permute-start.35
  196.6 13.9 %attend_backward.4 = (bf16[512,192]{1,0:T(8,128)(2,1)}, bf16[512,192]{1,0:T(8,128)(2,1)}, bf16[512,192]{1,0:T(8,128)(2,1)}, bf16[512,192]{1,0:T(8,128)(2,1)}) custom-call(bf16[512,576]{1,0:T(8,128)(2,1)} %copy-done, bf16[512,576]{1,0:T(8,128)(2,1)} %copy-done.2, bf16[512,576]{1,0:T(8,128)(2,1)} %copy-done.1, bf16[512,576]{1,0:T(8,128)(2,1)} %copy-done.3, ...), custom_call_target="tpu_custom_call" | custom-call | tf_op jit(solution)/shard_map/attend_backward/pallas_call | solution.py:113
  210.5 3.9 %collective-permute-start.31 = (bf16[512,192]{1,0:T(8,128)(2,1)}, bf16[512,192]{1,0:T(8,128)(2,1)}, u32[]{:S(2)}, u32[]{:S(2)}) collective-permute-start(bf16[512,192]{1,0:T(8,128)(2,1)} %get-tuple-element.454.refs_9_), channel_id=1, source_target_pairs={{0,24},{8,0},{16,8},{24,16},{1,25},{9,1},{17,9},{25,17},{2,26},{10... | collective-permute-start | bytes 589832 | tf_op jit(solution)/shard_map/ppermute | solution.py:683
  214.4 15.0 %collective-permute-done.35.refs_2_ = bf16[512,192]{1,0:T(8,128)(2,1)} collective-permute-done((bf16[512,192]{1,0:T(8,128)(2,1)}, bf16[512,192]{1,0:T(8,128)(2,1)}, u32[]{:S(2)}, u32[]{:S(2)}) %collective-permute-start.35) | collective-permute-done | bytes 196640 | tf_op jit(solution)/shard_map/ppermute | solution.py:683
  229.6 13.5 %attend_backward.5 = (bf16[512,192]{1,0:T(8,128)(2,1)}, bf16[512,192]{1,0:T(8,128)(2,1)}, bf16[512,192]{1,0:T(8,128)(2,1)}, bf16[512,192]{1,0:T(8,128)(2,1)}) custom-call(bf16[512,576]{1,0:T(8,128)(2,1)} %copy-done, bf16[512,576]{1,0:T(8,128)(2,1)} %copy-done.2, bf16[512,576]{1,0:T(8,128)(2,1)} %copy-done.1, bf16[512,576]{1,0:T(8,128)(2,1)} %copy-done.3, ...), custom_call_target="tpu_custom_call" | custom-call | tf_op jit(solution)/shard_map/attend_backward/pallas_call | solution.py:113
  243.1 2.0 add_convert_fusion
  245.3 1.6 collective-permute-start.37
  246.9 1.5 collective-permute-start.38
  248.4 3.8 %collective-permute-start.39 = (bf16[512,192]{1,0:T(8,128)(2,1)}, bf16[512,192]{1,0:T(8,128)(2,1)}, u32[]{:S(2)}, u32[]{:S(2)}) collective-permute-start(bf16[512,192]{1,0:T(8,128)(2,1)} %get-tuple-element.458.refs_13_), channel_id=1, source_target_pairs={{0,24},{8,0},{16,8},{24,16},{1,25},{9,1},{17,9},{25,17},{2,26},{10... | collective-permute-start | bytes 589832 | tf_op jit(solution)/shard_map/ppermute | solution.py:683
  253.6 7.0 %triple_grads.1 = (bf16[4,112,576]{2,1,0:T(8,128)(2,1)}, bf16[4,112,576]{2,1,0:T(8,128)(2,1)}) custom-call(s32[1]{0:T(128)} %bitcast.1.turn_ref, bf16[512,768]{1,0:T(8,128)(2,1)} %bitcast.79, bf16[512,768]{1,0:T(8,128)(2,1)} %copy-done.15, bf16[512,768]{1,0:T(8,128)(2,1)} %copy-done.14, bf16[512,768]{1,0:T(8,128)(2,1)} %copy-done.16, ...), custom_call_target="tpu_custom_call" | custom-call | tf_op jit(solution)/shard_map/triple_grads/pallas_call | solution.py:564
  260.6 11.3 %collective-permute-done.40.refs_10_ = bf16[512,192]{1,0:T(8,128)(2,1)} collective-permute-done((bf16[512,192]{1,0:T(8,128)(2,1)}, bf16[512,192]{1,0:T(8,128)(2,1)}, u32[]{:S(2)}, u32[]{:S(2)}) %collective-permute-start.40) | collective-permute-done | bytes 196640 | tf_op jit(solution)/shard_map/ppermute | solution.py:683
  274.6 1.4 collective-permute-start.45
  276.1 9.5 %collective-permute-done.42 = bf16[2,112,768]{2,1,0:T(8,128)(2,1)S(1)} collective-permute-done((bf16[2,112,768]{2,1,0:T(8,128)(2,1)S(1)}, bf16[2,112,768]{2,1,0:T(8,128)(2,1)S(1)}, u32[]{:S(2)}, u32[]{:S(2)}) %collective-permute-start.42) | collective-permute-done | bytes 344096 | tf_op jit(solution)/shard_map/ppermute | solution.py:736
  286.5 3.5 collective-permute-done.45
  290.0 2.2 collective-permute-start.46
  292.2 9.2 %collective-permute-done.43 = bf16[112,768]{1,0:T(8,128)(2,1)S(1)} collective-permute-done((bf16[112,768]{1,0:T(8,128)(2,1)S(1)}, bf16[112,768]{1,0:T(8,128)(2,1)S(1)}, u32[]{:S(2)}, u32[]{:S(2)}) %collective-permute-start.43) | collective-permute-done | bytes 172064 | tf_op jit(solution)/shard_map/ppermute | solution.py:736
  302.2 11.5 %collective-permute-done.46 = bf16[112,768]{1,0:T(8,128)(2,1)S(1)} collective-permute-done((bf16[112,768]{1,0:T(8,128)(2,1)S(1)}, bf16[112,768]{1,0:T(8,128)(2,1)S(1)}, u32[]{:S(2)}, u32[]{:S(2)}) %collective-permute-start.46) | collective-permute-done | bytes 172064 | tf_op jit(solution)/shard_map/ppermute | solution.py:736
  313.9 2.9 collective-permute-start.50
  317.4 5.2 %collective-permute-done.50.refs_1_ = bf16[112,576]{1,0:T(8,128)(2,1)S(1)} collective-permute-done((bf16[112,576]{1,0:T(8,128)(2,1)S(1)}, bf16[112,576]{1,0:T(8,128)(2,1)S(1)}, u32[]{:S(2)}, u32[]{:S(2)}) %collective-permute-start.50) | collective-permute-done | bytes 129056 | tf_op jit(solution)/shard_map/ppermute | solution.py:736
  322.7 2.1 collective-permute-start.53
  324.8 1.9 collective-permute-start.55
  326.8 6.9 %input_gradient.1 = f32[512,768]{1,0:T(8,128)} custom-call(s32[1]{0:T(128)} %bitcast.1.turn_ref, f32[512,768]{1,0:T(8,128)} %get-tuple-element.478.resid_ref, bf16[768,576]{1,0:T(8,128)(2,1)} %get-tuple-element.276.own_ref, bf16[512,192]{1,0:T(8,128)(2,1)} %get-tuple-element.479.refs_4_.refs_0_, bf16[512,192]{1,0:T(8,128)(2,1)} %collective-permute-done.34.refs_1_, ...), custom_call_target="tpu_custom_call" | custom-call | tf_op jit(solution)/shard_map/input_gradient/pallas_call | solution.py:422
  333.7 8.4 %collective-permute-done.54.refs_2_ = bf16[112,576]{1,0:T(8,128)(2,1)S(1)} collective-permute-done((bf16[112,576]{1,0:T(8,128)(2,1)S(1)}, bf16[112,576]{1,0:T(8,128)(2,1)S(1)}, u32[]{:S(2)}, u32[]{:S(2)}) %collective-permute-start.54) | collective-permute-done | bytes 129056 | tf_op jit(solution)/shard_map/ppermute | solution.py:736
  342.1 1.5 collective-permute-done.55.refs_3_
  344.3 2.5 unpack_triple.1
  347.6 3.1 unpack.1
  (195 shorter events, 29.2 us)
Async XLA Ops:
  0.6 24.6 %copy-start.31 = (bf16[384,768]{1,0:T(8,128)(2,1)S(1)}, bf16[384,768]{1,0:T(8,128)(2,1)}, u32[]{:S(2)}) copy-start(bf16[384,768]{1,0:T(8,128)(2,1)} %param.27) | copy-start | bytes 1769476
  0.7 22.9 %collective-permute-start.3 = (bf16[512,768]{1,0:T(8,128)(2,1)}, bf16[512,768]{1,0:T(8,128)(2,1)}, u32[]{:S(2)}, u32[]{:S(2)}) collective-permute-start(bf16[512,768]{1,0:T(8,128)(2,1)} %bitcast.76), channel_id=1, source_target_pairs={{8,0},{16,8},{24,16},{9,1},{17,9},{25,17},{10,2},{18,10},{26,18},{... | collective-permute-start | bytes 2359304 | tf_op jit(solution)/shard_map/ppermute | solution.py:688
  2.1 23.1 %collective-permute-start.6 = (bf16[512,768]{1,0:T(8,128)(2,1)}, bf16[512,768]{1,0:T(8,128)(2,1)}, u32[]{:S(2)}, u32[]{:S(2)}) collective-permute-start(bf16[512,768]{1,0:T(8,128)(2,1)} %bitcast.77), channel_id=1, source_target_pairs={{0,8},{8,16},{16,24},{1,9},{9,17},{17,25},{2,10},{10,18},{18,26},{... | collective-permute-start | bytes 2359304 | tf_op jit(solution)/shard_map/ppermute | solution.py:688
  11.1 22.6 %copy-start.37 = (bf16[112,576]{1,0:T(8,128)(2,1)S(1)}, bf16[112,576]{1,0:T(8,128)(2,1)}, u32[]{:S(2)}) copy-start(bf16[112,576]{1,0:T(8,128)(2,1)} %get-tuple-element.270) | copy-start | bytes 387076
  11.1 6.2 %collective-permute-start = (bf16[112,576]{1,0:T(8,128)(2,1)}, bf16[112,576]{1,0:T(8,128)(2,1)S(1)}, u32[]{:S(2)}, u32[]{:S(2)}) collective-permute-start(bf16[112,576]{1,0:T(8,128)(2,1)} %get-tuple-element.270), channel_id=1, source_target_pairs={{0,2},{1,3},{2,0},{3,1},{4,6},{5,7},{6,4},{7,5},{8,10},{9,11},{10,... | collective-permute-start | bytes 387080 | tf_op jit(solution)/shard_map/ppermute | solution.py:692
  13.1 8.4 %collective-permute-start.1 = (bf16[112,576]{1,0:T(8,128)(2,1)}, bf16[112,576]{1,0:T(8,128)(2,1)S(1)}, u32[]{:S(2)}, u32[]{:S(2)}) collective-permute-start(bf16[112,576]{1,0:T(8,128)(2,1)} %get-tuple-element.270), channel_id=1, source_target_pairs={{0,4},{1,5},{2,6},{3,7},{4,0},{5,1},{6,2},{7,3},{8,12},{9,13},{10,... | collective-permute-start | bytes 387080 | tf_op jit(solution)/shard_map/ppermute | solution.py:692
  14.6 6.9 %collective-permute-start.2 = (bf16[112,576]{1,0:T(8,128)(2,1)}, bf16[112,576]{1,0:T(8,128)(2,1)S(1)}, u32[]{:S(2)}, u32[]{:S(2)}) collective-permute-start(bf16[112,576]{1,0:T(8,128)(2,1)} %get-tuple-element.270), channel_id=1, source_target_pairs={{0,6},{1,7},{2,4},{3,5},{4,2},{5,3},{6,0},{7,1},{8,14},{9,15},{10,... | collective-permute-start | bytes 387080 | tf_op jit(solution)/shard_map/ppermute | solution.py:692
  23.6 18.5 %collective-permute-start.5 = (bf16[1,96,3968]{2,1,0:T(8,128)(2,1)}, bf16[1,96,3968]{2,1,0:T(8,128)(2,1)}, u32[]{:S(2)}, u32[]{:S(2)}) collective-permute-start(bf16[1,96,3968]{2,1,0:T(8,128)(2,1)} %maximum_bitcast_fusion), channel_id=1, source_target_pairs={{0,2},{1,3},{2,0},{3,1},{4,6},{5,7},{6,4},{7,5},{8,10},{9,11},{10,... | collective-permute-start | bytes 2285576 | tf_op jit(solution)/shard_map/ppermute | solution.py:692
  25.2 13.9 %collective-permute-start.7 = (bf16[1,384,768]{2,1,0:T(8,128)(2,1)S(1)}, bf16[1,384,768]{2,1,0:T(8,128)(2,1)S(1)}, u32[]{:S(2)}, u32[]{:S(2)}) collective-permute-start(bf16[1,384,768]{2,1,0:T(8,128)(2,1)S(1)} %bitcast.83), channel_id=1, source_target_pairs={{0,4},{1,5},{2,6},{3,7},{4,0},{5,1},{6,2},{7,3},{8,12},{9,13},{10,... | collective-permute-start | bytes 1769480 | tf_op jit(solution)/shard_map/ppermute | solution.py:692
  26.8 20.4 %collective-permute-start.4 = (bf16[512,768]{1,0:T(8,128)(2,1)}, bf16[512,768]{1,0:T(8,128)(2,1)}, u32[]{:S(2)}, u32[]{:S(2)}) collective-permute-start(bf16[512,768]{1,0:T(8,128)(2,1)} %collective-permute-done.3), channel_id=1, source_target_pairs={{8,0},{16,8},{24,16},{9,1},{17,9},{25,17},{10,2},{18,10},{26,18},{... | collective-permute-start | bytes 2359304 | tf_op jit(solution)/shard_map/ppermute | solution.py:688
  28.0 24.5 %collective-permute-start.10 = (bf16[512,768]{1,0:T(8,128)(2,1)}, bf16[512,768]{1,0:T(8,128)(2,1)}, u32[]{:S(2)}, u32[]{:S(2)}) collective-permute-start(bf16[512,768]{1,0:T(8,128)(2,1)} %collective-permute-done.6), channel_id=1, source_target_pairs={{0,8},{8,16},{16,24},{1,9},{9,17},{17,25},{2,10},{10,18},{18,26},{... | collective-permute-start | bytes 2359304 | tf_op jit(solution)/shard_map/ppermute | solution.py:688
  33.8 10.9 %collective-permute-start.8 = (bf16[4,112,576]{2,1,0:T(8,128)(2,1)S(1)}, bf16[4,112,576]{2,1,0:T(8,128)(2,1)S(1)}, u32[]{:S(2)}, u32[]{:S(2)}) collective-permute-start(bf16[4,112,576]{2,1,0:T(8,128)(2,1)S(1)} %pad_maximum_fusion.5.refs_0_), channel_id=1, source_target_pairs={{0,1},{1,0},{2,3},{3,2},{4,5},{5,4},{6,7},{7,6},{8,9},{9,8},{10,11... | collective-permute-start | bytes 1548296 | tf_op jit(solution)/shard_map/ppermute | solution.py:692
  39.3 30.5 %copy-start.12 = (bf16[2,384,768]{2,1,0:T(8,128)(2,1)}, bf16[2,384,768]{2,1,0:T(8,128)(2,1)S(1)}, u32[]{:S(2)}) copy-start(bf16[2,384,768]{2,1,0:T(8,128)(2,1)S(1)} %pad_maximum_fusion.1.refs_13_) | copy-start | bytes 3538948
  47.2 30.3 %collective-permute-start.12 = (bf16[2,96,3968]{2,1,0:T(8,128)(2,1)}, bf16[2,96,3968]{2,1,0:T(8,128)(2,1)}, u32[]{:S(2)}, u32[]{:S(2)}) collective-permute-start(bf16[2,96,3968]{2,1,0:T(8,128)(2,1)} %pad_maximum_fusion.refs_9_), channel_id=1, source_target_pairs={{0,1},{1,0},{2,3},{3,2},{4,5},{5,4},{6,7},{7,6},{8,9},{9,8},{10,11... | collective-permute-start | bytes 4571144 | tf_op jit(solution)/shard_map/ppermute | solution.py:692
  47.2 49.8 %collective-permute-start.15 = (bf16[2,96,3968]{2,1,0:T(8,128)(2,1)}, bf16[2,96,3968]{2,1,0:T(8,128)(2,1)}, u32[]{:S(2)}, u32[]{:S(2)}) collective-permute-start(bf16[2,96,3968]{2,1,0:T(8,128)(2,1)} %pad_maximum_fusion.refs_9_), channel_id=1, source_target_pairs={{0,4},{1,5},{2,6},{3,7},{4,0},{5,1},{6,2},{7,3},{8,12},{9,13},{10,... | collective-permute-start | bytes 4571144 | tf_op jit(solution)/shard_map/ppermute | solution.py:692
  47.9 21.9 %collective-permute-start.9 = (bf16[512,768]{1,0:T(8,128)(2,1)}, bf16[512,768]{1,0:T(8,128)(2,1)}, u32[]{:S(2)}, u32[]{:S(2)}) collective-permute-start(bf16[512,768]{1,0:T(8,128)(2,1)} %collective-permute-done.4), channel_id=1, source_target_pairs={{8,0},{16,8},{24,16},{9,1},{17,9},{25,17},{10,2},{18,10},{26,18},{... | collective-permute-start | bytes 2359304 | tf_op jit(solution)/shard_map/ppermute | solution.py:688
  49.2 28.4 %collective-permute-start.13 = (bf16[2,384,768]{2,1,0:T(8,128)(2,1)S(1)}, bf16[2,384,768]{2,1,0:T(8,128)(2,1)}, u32[]{:S(2)}, u32[]{:S(2)}) collective-permute-start(bf16[2,384,768]{2,1,0:T(8,128)(2,1)S(1)} %pad_maximum_fusion.1.refs_13_), channel_id=1, source_target_pairs={{0,1},{1,0},{2,3},{3,2},{4,5},{5,4},{6,7},{7,6},{8,9},{9,8},{10,11... | collective-permute-start | bytes 3538952 | tf_op jit(solution)/shard_map/ppermute | solution.py:692
  52.5 22.1 %collective-permute-start.11 = (bf16[512,768]{1,0:T(8,128)(2,1)}, bf16[512,768]{1,0:T(8,128)(2,1)S(1)}, u32[]{:S(2)}, u32[]{:S(2)}) collective-permute-start(bf16[512,768]{1,0:T(8,128)(2,1)} %collective-permute-done.10), channel_id=1, source_target_pairs={{0,8},{8,16},{16,24},{1,9},{9,17},{17,25},{2,10},{10,18},{18,26},{... | collective-permute-start | bytes 2359304 | tf_op jit(solution)/shard_map/ppermute | solution.py:688
  59.1 42.9 %copy-start = (bf16[512,576]{1,0:T(8,128)(2,1)}, bf16[512,576]{1,0:T(8,128)(2,1)S(1)}, u32[]{:S(2)}) copy-start(bf16[512,576]{1,0:T(8,128)(2,1)S(1)} %fusion.4.refs_0_) | copy-start | bytes 1769476
  61.6 40.3 %copy-start.1 = (bf16[512,576]{1,0:T(8,128)(2,1)}, bf16[512,576]{1,0:T(8,128)(2,1)S(1)}, u32[]{:S(2)}) copy-start(bf16[512,576]{1,0:T(8,128)(2,1)S(1)} %fusion.1.refs_2_) | copy-start | bytes 1769476
  69.7 27.3 %collective-permute-start.16 = (bf16[2,384,768]{2,1,0:T(8,128)(2,1)S(1)}, bf16[2,384,768]{2,1,0:T(8,128)(2,1)S(1)}, u32[]{:S(2)}, u32[]{:S(2)}) collective-permute-start(bf16[2,384,768]{2,1,0:T(8,128)(2,1)S(1)} %pad_maximum_fusion.1.refs_13_), channel_id=1, source_target_pairs={{0,2},{1,3},{2,0},{3,1},{4,6},{5,7},{6,4},{7,5},{8,10},{9,11},{10,... | collective-permute-start | bytes 3538952 | tf_op jit(solution)/shard_map/ppermute | solution.py:692
  76.7 25.2 %copy-start.2 = (bf16[512,576]{1,0:T(8,128)(2,1)}, bf16[512,576]{1,0:T(8,128)(2,1)S(1)}, u32[]{:S(2)}) copy-start(bf16[512,576]{1,0:T(8,128)(2,1)S(1)} %fusion.refs_1_) | copy-start | bytes 1769476
  77.5 24.4 %copy-start.3 = (bf16[512,576]{1,0:T(8,128)(2,1)}, bf16[512,576]{1,0:T(8,128)(2,1)S(1)}, u32[]{:S(2)}) copy-start(bf16[512,576]{1,0:T(8,128)(2,1)S(1)} %fusion.2.refs_3_) | copy-start | bytes 1769476
  82.6 15.5 %collective-permute-start.14 = (bf16[512,192]{1,0:T(8,128)(2,1)S(1)}, bf16[512,192]{1,0:T(8,128)(2,1)S(1)}, u32[]{:S(2)}, u32[]{:S(2)}) collective-permute-start(bf16[512,192]{1,0:T(8,128)(2,1)S(1)} %get-tuple-element.423.refs_10_), channel_id=1, source_target_pairs={{0,16},{8,24},{16,0},{24,8},{1,17},{9,25},{17,1},{25,9},{2,18},{10... | collective-permute-start | bytes 589832 | tf_op jit(solution)/shard_map/ppermute | solution.py:683
  98.1 15.9 %collective-permute-start.17 = (bf16[2,96,3968]{2,1,0:T(8,128)(2,1)}, bf16[2,96,3968]{2,1,0:T(8,128)(2,1)S(1)}, u32[]{:S(2)}, u32[]{:S(2)}) collective-permute-start(bf16[2,96,3968]{2,1,0:T(8,128)(2,1)} %collective-permute-done.15.refs_10_), channel_id=1, source_target_pairs={{0,1},{1,0},{2,3},{3,2},{4,5},{5,4},{6,7},{7,6},{8,9},{9,8},{10,11... | collective-permute-start | bytes 4571144 | tf_op jit(solution)/shard_map/ppermute | solution.py:692
  98.1 15.9 %collective-permute-start.18 = (bf16[2,384,768]{2,1,0:T(8,128)(2,1)S(1)}, bf16[2,384,768]{2,1,0:T(8,128)(2,1)S(1)}, u32[]{:S(2)}, u32[]{:S(2)}) collective-permute-start(bf16[2,384,768]{2,1,0:T(8,128)(2,1)S(1)} %collective-permute-done.16.refs_14_), channel_id=1, source_target_pairs={{0,1},{1,0},{2,3},{3,2},{4,5},{5,4},{6,7},{7,6},{8,9},{9,8},{10,11... | collective-permute-start | bytes 3538952 | tf_op jit(solution)/shard_map/ppermute | solution.py:692
  98.6 10.0 %collective-permute-start.19 = (bf16[512,192]{1,0:T(8,128)(2,1)S(1)}, bf16[512,192]{1,0:T(8,128)(2,1)S(1)}, u32[]{:S(2)}, u32[]{:S(2)}) collective-permute-start(bf16[512,192]{1,0:T(8,128)(2,1)S(1)} %get-tuple-element.422.refs_9_), channel_id=1, source_target_pairs={{0,24},{8,0},{16,8},{24,16},{1,25},{9,1},{17,9},{25,17},{2,26},{10... | collective-permute-start | bytes 589832 | tf_op jit(solution)/shard_map/ppermute | solution.py:683
  101.9 12.1 %collective-permute-start.20 = (bf16[512,192]{1,0:T(8,128)(2,1)S(1)}, bf16[512,192]{1,0:T(8,128)(2,1)S(1)}, u32[]{:S(2)}, u32[]{:S(2)}) collective-permute-start(bf16[512,192]{1,0:T(8,128)(2,1)S(1)} %get-tuple-element.424.refs_11_), channel_id=1, source_target_pairs={{0,8},{8,16},{16,24},{24,0},{1,9},{9,17},{17,25},{25,1},{2,10},{10... | collective-permute-start | bytes 589832 | tf_op jit(solution)/shard_map/ppermute | solution.py:683
  107.7 36.7 %copy-start.11 = (f32[512,8]{1,0:T(8,128)}, f32[512,8]{1,0:T(8,128)S(1)}, u32[]{:S(2)}) copy-start(f32[512,8]{1,0:T(8,128)S(1)} %get-tuple-element.425.refs_12_) | copy-start | bytes 49156
  114.7 29.6 %collective-permute-start.24 = (bf16[1,96,1728]{2,1,0:T(8,128)(2,1)}, bf16[1,96,1728]{2,1,0:T(8,128)(2,1)}, u32[]{:S(2)}, u32[]{:S(2)}) collective-permute-start(bf16[1,96,1728]{2,1,0:T(8,128)(2,1)} %bitcast.3), channel_id=1, source_target_pairs={{0,2},{1,3},{2,0},{3,1},{4,6},{5,7},{6,4},{7,5},{8,10},{9,11},{10,... | collective-permute-start | bytes 995336 | tf_op jit(solution)/shard_map/ppermute | solution.py:692
  145.6 21.9 %collective-permute-start.25 = (bf16[2,96,1728]{2,1,0:T(8,128)(2,1)S(1)}, bf16[2,96,1728]{2,1,0:T(8,128)(2,1)}, u32[]{:S(2)}, u32[]{:S(2)}) collective-permute-start(bf16[2,96,1728]{2,1,0:T(8,128)(2,1)S(1)} %pad_maximum_fusion.2.refs_12_), channel_id=1, source_target_pairs={{0,4},{1,5},{2,6},{3,7},{4,0},{5,1},{6,2},{7,3},{8,12},{9,13},{10,... | collective-permute-start | bytes 1990664 | tf_op jit(solution)/shard_map/ppermute | solution.py:692
  147.2 16.2 %collective-permute-start.21 = (bf16[512,192]{1,0:T(8,128)(2,1)S(1)}, bf16[512,192]{1,0:T(8,128)(2,1)S(1)}, u32[]{:S(2)}, u32[]{:S(2)}) collective-permute-start(bf16[512,192]{1,0:T(8,128)(2,1)S(1)} %copy-done.45), channel_id=1, source_target_pairs={{0,8},{8,16},{16,24},{24,0},{1,9},{9,17},{17,25},{25,1},{2,10},{10... | collective-permute-start | bytes 589832 | tf_op jit(solution)/shard_map/ppermute | solution.py:683
  149.0 18.5 %collective-permute-start.22 = (bf16[512,192]{1,0:T(8,128)(2,1)S(1)}, bf16[512,192]{1,0:T(8,128)(2,1)S(1)}, u32[]{:S(2)}, u32[]{:S(2)}) collective-permute-start(bf16[512,192]{1,0:T(8,128)(2,1)S(1)} %copy-done.44), channel_id=1, source_target_pairs={{0,16},{8,24},{16,0},{24,8},{1,17},{9,25},{17,1},{25,9},{2,18},{10... | collective-permute-start | bytes 589832 | tf_op jit(solution)/shard_map/ppermute | solution.py:683
  149.5 18.0 %collective-permute-start.23 = (bf16[512,192]{1,0:T(8,128)(2,1)S(1)}, bf16[512,192]{1,0:T(8,128)(2,1)S(1)}, u32[]{:S(2)}, u32[]{:S(2)}) collective-permute-start(bf16[512,192]{1,0:T(8,128)(2,1)S(1)} %copy-done.43), channel_id=1, source_target_pairs={{0,24},{8,0},{16,8},{24,16},{1,25},{9,1},{17,9},{25,17},{2,26},{10... | collective-permute-start | bytes 589832 | tf_op jit(solution)/shard_map/ppermute | solution.py:683
  167.5 14.5 %collective-permute-start.26 = (bf16[4,896,768]{2,1,0:T(8,128)(2,1)}, bf16[4,896,768]{2,1,0:T(8,128)(2,1)}, u32[]{:S(2)}, u32[]{:S(2)}) collective-permute-start(bf16[4,896,768]{2,1,0:T(8,128)(2,1)} %get-tuple-element.372), channel_id=1, source_target_pairs={{0,1},{1,0},{2,3},{3,2},{4,5},{5,4},{6,7},{7,6},{8,9},{9,8},{10,11... | collective-permute-start | bytes 16515080 | tf_op jit(solution)/shard_map/ppermute | solution.py:692
  167.6 20.4 %collective-permute-start.27 = (bf16[2,96,1728]{2,1,0:T(8,128)(2,1)S(1)}, bf16[2,96,1728]{2,1,0:T(8,128)(2,1)}, u32[]{:S(2)}, u32[]{:S(2)}) collective-permute-start(bf16[2,96,1728]{2,1,0:T(8,128)(2,1)S(1)} %pad_maximum_fusion.2.refs_12_), channel_id=1, source_target_pairs={{0,1},{1,0},{2,3},{3,2},{4,5},{5,4},{6,7},{7,6},{8,9},{9,8},{10,11... | collective-permute-start | bytes 1990664 | tf_op jit(solution)/shard_map/ppermute | solution.py:692
  168.1 19.9 %collective-permute-start.28 = (bf16[2,96,1728]{2,1,0:T(8,128)(2,1)}, bf16[2,96,1728]{2,1,0:T(8,128)(2,1)}, u32[]{:S(2)}, u32[]{:S(2)}) collective-permute-start(bf16[2,96,1728]{2,1,0:T(8,128)(2,1)} %collective-permute-done.25.refs_13_), channel_id=1, source_target_pairs={{0,1},{1,0},{2,3},{3,2},{4,5},{5,4},{6,7},{7,6},{8,9},{9,8},{10,11... | collective-permute-start | bytes 1990664 | tf_op jit(solution)/shard_map/ppermute | solution.py:692
  188.0 55.1 %collective-permute-start.29 = (bf16[2,448,768]{2,1,0:T(8,128)(2,1)}, bf16[2,448,768]{2,1,0:T(8,128)(2,1)S(1)}, u32[]{:S(2)}, u32[]{:S(2)}) collective-permute-start(bf16[2,448,768]{2,1,0:T(8,128)(2,1)} %get-tuple-element.382), channel_id=1, source_target_pairs={{0,2},{1,3},{2,0},{3,1},{4,6},{5,7},{6,4},{7,5},{8,10},{9,11},{10,... | collective-permute-start | bytes 4128776 | tf_op jit(solution)/shard_map/ppermute | solution.py:692
  188.6 54.5 %collective-permute-start.30 = (bf16[2,448,768]{2,1,0:T(8,128)(2,1)}, bf16[2,448,768]{2,1,0:T(8,128)(2,1)}, u32[]{:S(2)}, u32[]{:S(2)}) collective-permute-start(bf16[2,448,768]{2,1,0:T(8,128)(2,1)} %get-tuple-element.384), channel_id=1, source_target_pairs={{0,4},{1,5},{2,6},{3,7},{4,0},{5,1},{6,2},{7,3},{8,12},{9,13},{10,... | collective-permute-start | bytes 4128776 | tf_op jit(solution)/shard_map/ppermute | solution.py:692
  189.1 21.4 %collective-permute-start.34 = (bf16[512,192]{1,0:T(8,128)(2,1)}, bf16[512,192]{1,0:T(8,128)(2,1)}, u32[]{:S(2)}, u32[]{:S(2)}) collective-permute-start(bf16[512,192]{1,0:T(8,128)(2,1)} %get-tuple-element.450.refs_5_), channel_id=1, source_target_pairs={{0,24},{8,0},{16,8},{24,16},{1,25},{9,1},{17,9},{25,17},{2,26},{10... | collective-permute-start | bytes 589832 | tf_op jit(solution)/shard_map/ppermute | solution.py:683
  194.9 34.5 %collective-permute-start.35 = (bf16[512,192]{1,0:T(8,128)(2,1)}, bf16[512,192]{1,0:T(8,128)(2,1)}, u32[]{:S(2)}, u32[]{:S(2)}) collective-permute-start(bf16[512,192]{1,0:T(8,128)(2,1)} %get-tuple-element.451.refs_6_), channel_id=1, source_target_pairs={{0,16},{8,24},{16,0},{24,8},{1,17},{9,25},{17,1},{25,9},{2,18},{10... | collective-permute-start | bytes 589832 | tf_op jit(solution)/shard_map/ppermute | solution.py:683
  196.6 32.8 %collective-permute-start.36 = (bf16[512,192]{1,0:T(8,128)(2,1)}, bf16[512,192]{1,0:T(8,128)(2,1)}, u32[]{:S(2)}, u32[]{:S(2)}) collective-permute-start(bf16[512,192]{1,0:T(8,128)(2,1)} %get-tuple-element.452.refs_7_), channel_id=1, source_target_pairs={{0,8},{8,16},{16,24},{24,0},{1,9},{9,17},{17,25},{25,1},{2,10},{10... | collective-permute-start | bytes 589832 | tf_op jit(solution)/shard_map/ppermute | solution.py:683
  210.5 32.6 %collective-permute-start.31 = (bf16[512,192]{1,0:T(8,128)(2,1)}, bf16[512,192]{1,0:T(8,128)(2,1)}, u32[]{:S(2)}, u32[]{:S(2)}) collective-permute-start(bf16[512,192]{1,0:T(8,128)(2,1)} %get-tuple-element.454.refs_9_), channel_id=1, source_target_pairs={{0,24},{8,0},{16,8},{24,16},{1,25},{9,1},{17,9},{25,17},{2,26},{10... | collective-permute-start | bytes 589832 | tf_op jit(solution)/shard_map/ppermute | solution.py:683
  229.3 13.7 %collective-permute-start.32 = (bf16[512,192]{1,0:T(8,128)(2,1)}, bf16[512,192]{1,0:T(8,128)(2,1)}, u32[]{:S(2)}, u32[]{:S(2)}) collective-permute-start(bf16[512,192]{1,0:T(8,128)(2,1)} %get-tuple-element.455.refs_10_), channel_id=1, source_target_pairs={{0,16},{8,24},{16,0},{24,8},{1,17},{9,25},{17,1},{25,9},{2,18},{10... | collective-permute-start | bytes 589832 | tf_op jit(solution)/shard_map/ppermute | solution.py:683
  229.4 13.8 %collective-permute-start.33 = (bf16[512,192]{1,0:T(8,128)(2,1)}, bf16[512,192]{1,0:T(8,128)(2,1)}, u32[]{:S(2)}, u32[]{:S(2)}) collective-permute-start(bf16[512,192]{1,0:T(8,128)(2,1)} %get-tuple-element.456.refs_11_), channel_id=1, source_target_pairs={{0,8},{8,16},{16,24},{24,0},{1,9},{9,17},{17,25},{25,1},{2,10},{10... | collective-permute-start | bytes 589832 | tf_op jit(solution)/shard_map/ppermute | solution.py:683
  245.3 26.6 %collective-permute-start.37 = (bf16[448,768]{1,0:T(8,128)(2,1)S(1)}, bf16[448,768]{1,0:T(8,128)(2,1)}, u32[]{:S(2)}, u32[]{:S(2)}) collective-permute-start(bf16[448,768]{1,0:T(8,128)(2,1)S(1)} %get-tuple-element.463), channel_id=1, source_target_pairs={{0,4},{1,5},{2,6},{3,7},{4,0},{5,1},{6,2},{7,3},{8,12},{9,13},{10,... | collective-permute-start | bytes 2064392 | tf_op jit(solution)/shard_map/ppermute | solution.py:692
  246.9 25.0 %collective-permute-start.38 = (bf16[448,768]{1,0:T(8,128)(2,1)S(1)}, bf16[448,768]{1,0:T(8,128)(2,1)S(1)}, u32[]{:S(2)}, u32[]{:S(2)}) collective-permute-start(bf16[448,768]{1,0:T(8,128)(2,1)S(1)} %get-tuple-element.465), channel_id=1, source_target_pairs={{0,2},{1,3},{2,0},{3,1},{4,6},{5,7},{6,4},{7,5},{8,10},{9,11},{10,... | collective-permute-start | bytes 2064392 | tf_op jit(solution)/shard_map/ppermute | solution.py:692
  248.4 12.2 %collective-permute-start.39 = (bf16[512,192]{1,0:T(8,128)(2,1)}, bf16[512,192]{1,0:T(8,128)(2,1)}, u32[]{:S(2)}, u32[]{:S(2)}) collective-permute-start(bf16[512,192]{1,0:T(8,128)(2,1)} %get-tuple-element.458.refs_13_), channel_id=1, source_target_pairs={{0,24},{8,0},{16,8},{24,16},{1,25},{9,1},{17,9},{25,17},{2,26},{10... | collective-permute-start | bytes 589832 | tf_op jit(solution)/shard_map/ppermute | solution.py:683
  252.2 19.7 %collective-permute-start.40 = (bf16[512,192]{1,0:T(8,128)(2,1)}, bf16[512,192]{1,0:T(8,128)(2,1)}, u32[]{:S(2)}, u32[]{:S(2)}) collective-permute-start(bf16[512,192]{1,0:T(8,128)(2,1)} %get-tuple-element.459.refs_14_), channel_id=1, source_target_pairs={{0,16},{8,24},{16,0},{24,8},{1,17},{9,25},{17,1},{25,9},{2,18},{10... | collective-permute-start | bytes 589832 | tf_op jit(solution)/shard_map/ppermute | solution.py:683
  253.3 18.6 %collective-permute-start.41 = (bf16[512,192]{1,0:T(8,128)(2,1)}, bf16[512,192]{1,0:T(8,128)(2,1)}, u32[]{:S(2)}, u32[]{:S(2)}) collective-permute-start(bf16[512,192]{1,0:T(8,128)(2,1)} %get-tuple-element.460.refs_15_), channel_id=1, source_target_pairs={{0,8},{8,16},{16,24},{24,0},{1,9},{9,17},{17,25},{25,1},{2,10},{10... | collective-permute-start | bytes 589832 | tf_op jit(solution)/shard_map/ppermute | solution.py:683
  273.4 12.1 %collective-permute-start.42 = (bf16[2,112,768]{2,1,0:T(8,128)(2,1)S(1)}, bf16[2,112,768]{2,1,0:T(8,128)(2,1)S(1)}, u32[]{:S(2)}, u32[]{:S(2)}) collective-permute-start(bf16[2,112,768]{2,1,0:T(8,128)(2,1)S(1)} %pad_maximum_fusion.6), channel_id=1, source_target_pairs={{0,8},{8,0},{16,24},{24,16},{1,9},{9,1},{17,25},{25,17},{2,10},{10... | collective-permute-start | bytes 1032200 | tf_op jit(solution)/shard_map/ppermute | solution.py:736
  274.5 11.2 %collective-permute-start.47 = (bf16[4,112,576]{2,1,0:T(8,128)(2,1)S(1)}, bf16[4,112,576]{2,1,0:T(8,128)(2,1)S(1)}, u32[]{:S(2)}, u32[]{:S(2)}) collective-permute-start(bf16[4,112,576]{2,1,0:T(8,128)(2,1)S(1)} %copy-done.42), channel_id=1, source_target_pairs={{0,1},{1,0},{2,3},{3,2},{4,5},{5,4},{6,7},{7,6},{8,9},{9,8},{10,11... | collective-permute-start | bytes 1548296 | tf_op jit(solution)/shard_map/ppermute | solution.py:692
  274.6 15.3 %collective-permute-start.45 = (bf16[2,112,768]{2,1,0:T(8,128)(2,1)S(1)}, bf16[2,112,768]{2,1,0:T(8,128)(2,1)S(1)}, u32[]{:S(2)}, u32[]{:S(2)}) collective-permute-start(bf16[2,112,768]{2,1,0:T(8,128)(2,1)S(1)} %pad_maximum_fusion.8), channel_id=1, source_target_pairs={{0,8},{8,0},{16,24},{24,16},{1,9},{9,1},{17,25},{25,17},{2,10},{10... | collective-permute-start | bytes 1032200 | tf_op jit(solution)/shard_map/ppermute | solution.py:736
  285.6 15.8 %collective-permute-start.43 = (bf16[112,768]{1,0:T(8,128)(2,1)S(1)}, bf16[112,768]{1,0:T(8,128)(2,1)S(1)}, u32[]{:S(2)}, u32[]{:S(2)}) collective-permute-start(bf16[112,768]{1,0:T(8,128)(2,1)S(1)} %fusion.9), channel_id=1, source_target_pairs={{0,16},{8,24},{16,0},{24,8},{1,17},{9,25},{17,1},{25,9},{2,18},{10... | collective-permute-start | bytes 516104 | tf_op jit(solution)/shard_map/ppermute | solution.py:736
  285.9 15.7 %collective-permute-start.48 = (bf16[2,112,576]{2,1,0:T(8,128)(2,1)S(1)}, bf16[2,112,576]{2,1,0:T(8,128)(2,1)S(1)}, u32[]{:S(2)}, u32[]{:S(2)}) collective-permute-start(bf16[2,112,576]{2,1,0:T(8,128)(2,1)S(1)} %slice.161), channel_id=1, source_target_pairs={{0,2},{1,3},{2,0},{3,1},{4,6},{5,7},{6,4},{7,5},{8,10},{9,11},{10,... | collective-permute-start | bytes 774152 | tf_op jit(solution)/shard_map/ppermute | solution.py:692
  290.0 23.7 %collective-permute-start.46 = (bf16[112,768]{1,0:T(8,128)(2,1)S(1)}, bf16[112,768]{1,0:T(8,128)(2,1)S(1)}, u32[]{:S(2)}, u32[]{:S(2)}) collective-permute-start(bf16[112,768]{1,0:T(8,128)(2,1)S(1)} %fusion.11), channel_id=1, source_target_pairs={{0,16},{8,24},{16,0},{24,8},{1,17},{9,25},{17,1},{25,9},{2,18},{10... | collective-permute-start | bytes 516104 | tf_op jit(solution)/shard_map/ppermute | solution.py:736
  301.5 15.9 %collective-permute-start.44 = (bf16[112,768]{1,0:T(8,128)(2,1)S(1)}, bf16[112,768]{1,0:T(8,128)(2,1)S(1)}, u32[]{:S(2)}, u32[]{:S(2)}) collective-permute-start(bf16[112,768]{1,0:T(8,128)(2,1)S(1)} %fusion.6), channel_id=1, source_target_pairs={{0,16},{8,24},{16,0},{24,8},{1,17},{9,25},{17,1},{25,9},{2,18},{10... | collective-permute-start | bytes 516104 | tf_op jit(solution)/shard_map/ppermute | solution.py:736
  301.7 12.1 %collective-permute-start.49 = (bf16[112,576]{1,0:T(8,128)(2,1)S(1)}, bf16[112,576]{1,0:T(8,128)(2,1)S(1)}, u32[]{:S(2)}, u32[]{:S(2)}) collective-permute-start(bf16[112,576]{1,0:T(8,128)(2,1)S(1)} %slice_bitcast_fusion.12), channel_id=1, source_target_pairs={{0,4},{1,5},{2,6},{3,7},{4,0},{5,1},{6,2},{7,3},{8,12},{9,13},{10,... | collective-permute-start | bytes 387080 | tf_op jit(solution)/shard_map/ppermute | solution.py:692
  313.8 8.8 %collective-permute-start.52 = (bf16[112,768]{1,0:T(8,128)(2,1)S(1)}, bf16[112,768]{1,0:T(8,128)(2,1)S(1)}, u32[]{:S(2)}, u32[]{:S(2)}) collective-permute-start(bf16[112,768]{1,0:T(8,128)(2,1)S(1)} %fusion.5), channel_id=1, source_target_pairs={{0,16},{8,24},{16,0},{24,8},{1,17},{9,25},{17,1},{25,9},{2,18},{10... | collective-permute-start | bytes 516104 | tf_op jit(solution)/shard_map/ppermute | solution.py:736
  313.9 8.7 %collective-permute-start.50 = (bf16[112,576]{1,0:T(8,128)(2,1)S(1)}, bf16[112,576]{1,0:T(8,128)(2,1)S(1)}, u32[]{:S(2)}, u32[]{:S(2)}) collective-permute-start(bf16[112,576]{1,0:T(8,128)(2,1)S(1)} %fusion.7.refs_0_), channel_id=1, source_target_pairs={{0,16},{8,24},{16,0},{24,8},{1,17},{9,25},{17,1},{25,9},{2,18},{10... | collective-permute-start | bytes 387080 | tf_op jit(solution)/shard_map/ppermute | solution.py:736
  322.6 24.2 %collective-permute-start.51 = (bf16[2,112,768]{2,1,0:T(8,128)(2,1)S(1)}, bf16[2,112,768]{2,1,0:T(8,128)(2,1)S(1)}, u32[]{:S(2)}, u32[]{:S(2)}) collective-permute-start(bf16[2,112,768]{2,1,0:T(8,128)(2,1)S(1)} %pad_maximum_fusion.7.refs_0_), channel_id=1, source_target_pairs={{0,8},{8,0},{16,24},{24,16},{1,9},{9,1},{17,25},{25,17},{2,10},{10... | collective-permute-start | bytes 1032200 | tf_op jit(solution)/shard_map/ppermute | solution.py:736
  322.7 24.1 %collective-permute-start.53 = (bf16[2,112,768]{2,1,0:T(8,128)(2,1)S(1)}, bf16[2,112,768]{2,1,0:T(8,128)(2,1)S(1)}, u32[]{:S(2)}, u32[]{:S(2)}) collective-permute-start(bf16[2,112,768]{2,1,0:T(8,128)(2,1)S(1)} %pad_maximum_fusion.9.refs_2_), channel_id=1, source_target_pairs={{0,8},{8,0},{16,24},{24,16},{1,9},{9,1},{17,25},{25,17},{2,10},{10... | collective-permute-start | bytes 1032200 | tf_op jit(solution)/shard_map/ppermute | solution.py:736
  324.7 17.3 %collective-permute-start.54 = (bf16[112,576]{1,0:T(8,128)(2,1)S(1)}, bf16[112,576]{1,0:T(8,128)(2,1)S(1)}, u32[]{:S(2)}, u32[]{:S(2)}) collective-permute-start(bf16[112,576]{1,0:T(8,128)(2,1)S(1)} %fusion.7.refs_0_), channel_id=1, source_target_pairs={{0,8},{8,0},{16,24},{24,16},{1,9},{9,1},{17,25},{25,17},{2,10},{10... | collective-permute-start | bytes 387080 | tf_op jit(solution)/shard_map/ppermute | solution.py:736
  324.8 18.8 %collective-permute-start.55 = (bf16[112,576]{1,0:T(8,128)(2,1)S(1)}, bf16[112,576]{1,0:T(8,128)(2,1)S(1)}, u32[]{:S(2)}, u32[]{:S(2)}) collective-permute-start(bf16[112,576]{1,0:T(8,128)(2,1)S(1)} %collective-permute-done.50.refs_1_), channel_id=1, source_target_pairs={{0,8},{8,0},{16,24},{24,16},{1,9},{9,1},{17,25},{25,17},{2,10},{10... | collective-permute-start | bytes 387080 | tf_op jit(solution)/shard_map/ppermute | solution.py:736
  (38 other events, 320.0 us)
